TPU v7x, 256 devices: a whole 4x4x8 slice. The times are simulated.
256 devices in a mesh: side: 2 (over core), grp: 32 (over z, y), tp: 4 (over x).
Axes of the slice: x: 4, y: 4, z: 8, core: 2. Of those that a mesh axis runs over, the one named last changes fastest.
Arguments:
- queries: bfloat16 [4096, 4096], P(('side', 'grp'), 'tp'), may hold values from -80 to 80
- new_key: bfloat16 [4096, 512], P(('side', 'grp'), 'tp'), may hold values from -4 to 4
- new_value: bfloat16 [4096, 512], P(('side', 'grp'), 'tp'), may hold values from -6 to 6
- key_cache: bfloat16 [4096, 128, 512], P(('side', 'grp'), None, 'tp'), may hold values from -5 to 5
- value_cache: bfloat16 [4096, 128, 512], P(('side', 'grp'), None, 'tp'), may hold values from -6 to 6
- cache_len: int32 [4096], P(('side', 'grp')), may hold values from 1 to 128, as said below
- residual: bfloat16 [4096, 4096], P(('side', 'grp'), 'tp'), may hold values from -30 to 30
- norm_gain: float32 [4096], replicated, may hold values from 0.5 to 1.5
- expert_ids: int32 [4096, 8], P(('side', 'grp')), may hold values from 0 to 127, all different within a row; in each aligned block of 64 rows (0 to 63, 64 to 127, ...) at most 8 rows name the same one
- gate_probs: float32 [4096, 8], P(('side', 'grp')), may hold values from 0.1 to 1
- w_gate: bfloat16 [128, 768, 4096], P(('side', 'grp'), 'tp'), may hold values from -0.09375 to 0.09375
- w_up: bfloat16 [128, 768, 4096], P(('side', 'grp'), 'tp'), may hold values from -0.09375 to 0.09375
- w_down: bfloat16 [128, 768, 4096], P(('side', 'grp'), 'tp'), may hold values from -0.21875 to 0.21875
Outputs:
- layer_out: bfloat16 [4096, 4096], P(('side', 'grp'), 'tp')
Inputs may be any that keep to these rules, and one draw needn't show every extreme that they name: `cache_len`: some row's cache holds 128 tokens. `expert_ids`: A row names 8 different experts. Among the 64 rows of one device (aligned blocks of rows), no expert is named by more than 8 rows, and in some blocks one expert is named by exactly 8.
All inputs are finite; a program needn't handle non-finite values.
Results may differ from a plain program's by a relative error of at most 0.0085.
Values may be sent and summed in bfloat16 or wider, within the bound.
No kernel may reach another device: no remote copies, remote signals or barrier semaphores. Data moves between devices by JAX's collectives and lax.ppermute only.
A program may use at most 128 MiB of HBM per device.

v0:
```python
import math

import jax
import jax.numpy as jnp
from jax import lax
from jax.sharding import PartitionSpec as P

HD = 128
TOPK = 8
EXP_DEV = 2


epsilon = 1e-06


def expert_work(incoming, w_gate, w_up, w_down):
    gate_proj = jnp.einsum("sxcd,xfd->sxcf", incoming, w_gate, preferred_element_type=jnp.float32)
    up_proj = jnp.einsum("sxcd,xfd->sxcf", incoming, w_up, preferred_element_type=jnp.float32)
    activation = (jax.nn.silu(gate_proj) * up_proj).astype(jnp.bfloat16)
    partial_sum = jnp.einsum(
        "sxcf,xfd->sxcd", activation, w_down, preferred_element_type=jnp.float32
    )
    rounded = lax.optimization_barrier(partial_sum.astype(jnp.bfloat16)).astype(jnp.float32)
    reduced = lax.psum_scatter(rounded.astype(jnp.bfloat16), "tp", scatter_dimension=3, tiled=True)
    return reduced


def body(
    queries,
    new_key,
    new_value,
    key_cache,
    value_cache,
    cache_len,
    residual,
    norm_gain,
    expert_ids,
    gate_probs,
    w_gate,
    w_up,
    w_down,
):
    row_count = queries.shape[0]
    head_count = queries.shape[1] // HD
    kv_count = new_key.shape[1] // HD
    group_size = head_count // kv_count
    cache_span = key_cache.shape[1]
    query_heads = queries.reshape(row_count, kv_count, group_size, HD)
    cache_keys = key_cache.reshape(row_count, cache_span, kv_count, HD)
    cache_values = value_cache.reshape(row_count, cache_span, kv_count, HD)
    fresh_keys = new_key.reshape(row_count, kv_count, HD)
    fresh_values = new_value.reshape(row_count, kv_count, HD)
    score_scale = 1.0 / math.sqrt(HD)
    cache_scores = (
        jnp.einsum("rkgd,rjkd->rkgj", query_heads, cache_keys, preferred_element_type=jnp.float32)
        * score_scale
    )
    live_mask = jnp.arange(cache_span)[None, :] < cache_len[:, None]
    cache_scores = jnp.where(live_mask[:, None, None, :], cache_scores, -jnp.inf)
    fresh_scores = (
        jnp.einsum("rkgd,rkd->rkg", query_heads, fresh_keys, preferred_element_type=jnp.float32)
        * score_scale
    )
    top_score = jnp.maximum(jnp.max(cache_scores, axis=-1), fresh_scores)
    cache_exp = jnp.exp(cache_scores - top_score[..., None])
    fresh_exp = jnp.exp(fresh_scores - top_score)
    denominator = jnp.sum(cache_exp, axis=-1) + fresh_exp
    cache_weights = (cache_exp / denominator[..., None]).astype(jnp.bfloat16)
    fresh_weights = (fresh_exp / denominator).astype(jnp.bfloat16)
    attended = jnp.einsum(
        "rkgj,rjkd->rkgd", cache_weights, cache_values, preferred_element_type=jnp.float32
    )
    attended = (
        attended
        + fresh_weights.astype(jnp.float32)[..., None]
        * fresh_values.astype(jnp.float32)[:, :, None, :]
    )
    attended = attended.reshape(row_count, head_count * HD)
    own_summed = residual.astype(jnp.float32) + attended
    summed = lax.all_gather(own_summed.astype(jnp.bfloat16), "tp", axis=1, tiled=True).astype(
        own_summed.dtype
    )
    mean_square = jnp.mean(summed * summed, axis=-1, keepdims=True)
    normed = (summed * lax.rsqrt(mean_square + epsilon) * norm_gain).astype(jnp.bfloat16)
    quarter = own_summed.shape[1]
    group_total = lax.axis_size("side") * lax.axis_size("grp")
    experts = EXP_DEV * group_total
    slot_count = max(2, 2 * row_count * TOPK // experts)
    expert_hits = jnp.sum(
        (expert_ids[:, :, None] == jnp.arange(experts)[None, None, :]).astype(jnp.int32), axis=1
    )
    earlier = jnp.cumsum(expert_hits, axis=0) - expert_hits
    slot_rank = jnp.take_along_axis(earlier, expert_ids, axis=1)
    slot_index = expert_ids * slot_count + slot_rank
    placing = jnp.sum(
        (slot_index[:, :, None] == jnp.arange(experts * slot_count)[None, None, :]).astype(
            jnp.int32
        ),
        axis=1,
    ).astype(jnp.bfloat16)
    outgoing = jnp.einsum("rs,rd->sd", placing, normed, preferred_element_type=jnp.float32).astype(
        jnp.bfloat16
    )
    outgoing = outgoing.reshape(group_total, EXP_DEV, slot_count, normed.shape[1])
    produced = expert_work(
        lax.all_to_all(outgoing, ("side", "grp"), split_axis=0, concat_axis=0, tiled=True),
        w_gate,
        w_up,
        w_down,
    )
    returned = lax.all_to_all(produced, ("side", "grp"), split_axis=0, concat_axis=0, tiled=True)
    returned_flat = returned.reshape(experts * slot_count, quarter)
    picked = returned_flat[slot_index]
    mix = gate_probs / jnp.sum(gate_probs, axis=-1, keepdims=True)
    mixed = jnp.sum(mix[:, :, None] * picked.astype(jnp.float32), axis=1)
    return (own_summed + mixed).astype(jnp.bfloat16)


def solution(mesh):
    in_specs = (
        P(("side", "grp"), "tp"),
        P(("side", "grp"), "tp"),
        P(("side", "grp"), "tp"),
        P(("side", "grp"), None, "tp"),
        P(("side", "grp"), None, "tp"),
        P(("side", "grp")),
        P(("side", "grp"), "tp"),
        P(),
        P(("side", "grp"), None),
        P(("side", "grp"), None),
        P(("side", "grp"), "tp", None),
        P(("side", "grp"), "tp", None),
        P(("side", "grp"), "tp", None),
    )
    out_specs = P(("side", "grp"), "tp")
    return jax.shard_map(body, mesh=mesh, in_specs=in_specs, out_specs=out_specs, check_vma=False)
```

profile of v0, /device:TPU:1, one launch (start us, length us, event | category | flops | bytes accessed | tf_op | source)
XLA Modules:
  0.0 418.4 jit_solution(2377038928856002106)
XLA Ops:
  6.5 0.0 copy-start
  6.5 0.0 copy-start.6
  6.5 0.0 reduce-scatter.2.cloned.1.call-start
  6.5 0.9 copy.54
  7.5 0.0 copy-start.8
  7.5 0.8 bitcast_or_fusion
  8.3 0.9 copy.67
  9.2 0.7 iota_compare_fusion.2
  10.0 0.0 copy-start.3
  10.0 1.0 fusion.50
  10.9 2.9 fusion.55
  13.8 0.2 fusion.45
  14.1 0.0 copy-done.6
  14.1 0.0 copy-done.8
  14.1 0.7 convolution_add_fusion
  14.9 0.0 copy-done.3
  14.9 0.1 fusion.46
  14.9 12.3 %all_gather.3 = bf16[64,4096]{1,0:T(8,128)(2,1)S(1)} all-gather(bf16[64,1024]{1,0:T(8,128)(2,1)S(1)} %fusion.46), channel_id=1, replica_groups=mesh['side'=2,'grp'=32,'tp'=4] {'tp'}, dimensions={1}, use_global_device_ids=true | all-gather | bytes 655360 | tf_op jit(solution)/shard_map/all_gather | solution.py:80
  27.3 0.0 copy-start.2
  27.3 0.8 copy-done.2
  28.1 0.2 fusion.33
  28.3 0.2 convert_reduce_fusion.1
  28.4 0.1 reduce_window_sum.11
  28.5 0.1 copy.55
  28.6 0.1 reshape.125
  28.7 0.0 copy-start.4
  28.7 0.0 copy-start.5
  28.7 3.6 gather_fusion.1
  32.4 0.1 reshape.128
  32.5 0.1 copy.56
  32.5 0.0 copy-done.4
  32.5 0.1 copy.57
  32.6 0.7 convert_reduce_fusion
  33.3 0.0 copy-done.5
  33.3 3.5 convolution_convert_fusion
  36.8 199.0 %all_to_all.10 = bf16[64,2,8,4096]{3,2,1,0:T(8,128)(2,1)S(1)} all-to-all(bf16[64,2,8,4096]{3,2,1,0:T(8,128)(2,1)S(1)} %bitcast.62), channel_id=1, replica_groups=mesh['side'=2,'grp'=32,'tp'=4] {'side','grp'}, dimensions={0} | all-to-all | bytes 16777216 | tf_op jit(solution)/shard_map/all_to_all | solution.py:106
  235.8 0.0 copy-start.1
  235.8 3.2 copy-done.1
  239.0 5.2 %fusion.8 = f32[64,2,8,192]{3,2,0,1:T(8,128)} fusion(bf16[2,192,4096]{2,1,0:T(8,128)(2,1)} %param.23, bf16[64,2,8,4096]{3,2,1,0:T(8,128)(2,1)S(1)} %all_to_all.10), kind=kOutput, calls=%fused_computation.15 | convolution fusion | flops 1610612736 | bytes 12320768 | tf_op jit(solution)/shard_map/sxcd,xfd->sxcf/dot_general | solution.py:17
  244.2 0.0 copy-done
  244.2 13.7 %convert_bitcast_fusion = bf16[64,2,8,4096]{3,2,0,1:T(8,128)(2,1)} fusion(bf16[2,192,4096]{2,1,0:T(8,128)(2,1)S(1)} %copy-done, bf16[2,192,4096]{2,1,0:T(8,128)(2,1)} %param.24, bf16[64,2,8,4096]{3,2,1,0:T(8,128)(2,1)} %copy-done.1, f32[64,2,8,192]{3,2,0,1:T(8,128)} %fusion.8), kind=kOutput, calls=%fused_computation.2 | convolution fusion | flops 3226599424 | bytes 23855104 | tf_op jit(solution)/shard_map/sxcf,xfd->sxcd/dot_general | solution.py:20
  257.9 0.0 reduce-scatter.2.cloned.1.call-update
  257.9 80.2 %reduce-scatter.2.cloned.1.call-done = bf16[64,2,8,1024]{3,2,0,1:T(8,128)(2,1)} async-done(((bf16[64,2,8,4096]{3,2,0,1:T(8,128)(2,1)}), bf16[64,2,8,1024]{3,2,0,1:T(8,128)(2,1)}) %reduce-scatter.2.cloned.1.call-update) | async-done | bytes 2097168 | tf_op jit(solution)/shard_map/reduce_scatter | solution.py:24
  338.1 3.1 copy.60
  341.3 0.0 copy-start.7
  341.3 11.1 %all-to-all-start.1 = ((bf16[64,2,8,1024]{3,2,1,0:T(8,128)(2,1)}), bf16[64,2,8,1024]{3,2,1,0:T(8,128)(2,1)}, u32[]{:S(2)}, u32[]{:S(2)}) async-start(bf16[64,2,8,1024]{3,2,1,0:T(8,128)(2,1)} %copy.60), calls=%async_computation.2 | async-start | bytes 4194304 | tf_op jit(solution)/shard_map/all_to_all | solution.py:111
  352.3 0.1 copy.61
  352.4 0.1 reshape.119
  352.5 0.0 copy-done.7
  352.6 0.1 copy.53
  352.7 49.9 %all-to-all-done.1 = bf16[64,2,8,1024]{3,2,1,0:T(8,128)(2,1)} async-done(((bf16[64,2,8,1024]{3,2,1,0:T(8,128)(2,1)}), bf16[64,2,8,1024]{3,2,1,0:T(8,128)(2,1)}, u32[]{:S(2)}, u32[]{:S(2)}) %all-to-all-start.1) | async-done | bytes 2097184 | tf_op jit(solution)/shard_map/all_to_all | solution.py:111
  402.6 5.3 %gather_fusion = bf16[512,1024]{1,0:T(8,128)(2,1)} fusion(bf16[1024,1024]{1,0:T(8,128)(2,1)} %bitcast.14, s32[1024]{0:T(1024)S(1)} %pad_clamp_fusion), kind=kCustom, calls=%fused_computation | custom fusion | bytes 2099200 | tf_op jit(solution)/shard_map/gather | solution.py:113
  407.9 1.9 fusion.7
  409.9 1.6 add_convert_fusion
  (9 shorter events, 0.1 us)
Async XLA Ops:
  6.5 237.7 %copy-start = (bf16[2,192,4096]{2,1,0:T(8,128)(2,1)S(1)}, bf16[2,192,4096]{2,1,0:T(8,128)(2,1)}, u32[]{:S(2)}) copy-start(bf16[2,192,4096]{2,1,0:T(8,128)(2,1)} %param.25) | copy-start | bytes 9437188
  6.5 7.6 %copy-start.6 = (bf16[64,128]{1,0:T(8,128)(2,1)S(1)}, bf16[64,128]{1,0:T(8,128)(2,1)}, u32[]{:S(2)}) copy-start(bf16[64,128]{1,0:T(8,128)(2,1)} %param.15) | copy-start | bytes 49156
  6.5 331.6 %reduce-scatter.2.cloned.1.call-start = ((), (), s32[]{:S(2)}) async-start(), calls=%async_computation.3 | async-start | bytes 10485760 | tf_op jit(solution)/shard_map/reduce_scatter | solution.py:24
  7.5 6.7 %copy-start.8 = (bf16[64,128,128]{2,1,0:T(8,128)(2,1)S(1)}, bf16[64,128,128]{2,1,0:T(8,128)(2,1)}, u32[]{:S(2)}) copy-start(bf16[64,128,128]{2,1,0:T(8,128)(2,1)} %param.17) | copy-start | bytes 6291460
  10.0 4.9 %copy-start.3 = (bf16[64,1024]{1,0:T(8,128)(2,1)S(1)}, bf16[64,1024]{1,0:T(8,128)(2,1)}, u32[]{:S(2)}) copy-start(bf16[64,1024]{1,0:T(8,128)(2,1)} %param.19) | copy-start | bytes 393220
  27.3 0.8 copy-start.2
  28.7 3.8 copy-start.4
  28.7 4.6 %copy-start.5 = (f32[4096]{0:T(1024)S(1)}, f32[4096]{0:T(1024)}, u32[]{:S(2)}) copy-start(f32[4096]{0:T(1024)} %param.20) | copy-start | bytes 49156
  235.8 3.2 copy-start.1
  341.3 11.2 %copy-start.7 = (f32[64,8]{0,1:T(8,128)S(1)}, f32[64,8]{0,1:T(8,128)}, u32[]{:S(2)}) copy-start(f32[64,8]{0,1:T(8,128)} %param.22) | copy-start | bytes 6148
  341.3 61.3 %all-to-all-start.1 = ((bf16[64,2,8,1024]{3,2,1,0:T(8,128)(2,1)}), bf16[64,2,8,1024]{3,2,1,0:T(8,128)(2,1)}, u32[]{:S(2)}, u32[]{:S(2)}) async-start(bf16[64,2,8,1024]{3,2,1,0:T(8,128)(2,1)} %copy.60), calls=%async_computation.2 | async-start | bytes 4194304 | tf_op jit(solution)/shard_map/all_to_all | solution.py:111
Sparse Core Ops, SparseCore 0:
  258.1 80.0 reduce-scatter.1
where the time goes:
time: 419 us; the launch traced here: 418 us
  blocking collectives  211 us (50%)
  waiting for transfers between devices  130 us (31%)
  matrix products  26.9 us (6%)
  local copies, waits for them, and re-layouts  18.7 us (4%)
  between operations  13.6 us (3%)
  starting transfers between devices  11.1 us (3%)
  other arithmetic  6.66 us (2%)
    all_to_all x1, blocking collectives, body(): lax.all_to_all(outgoing, ('side', 'grp'), split_axis=0, concat_axis=0, ti...  199 us
    reduce_scatter x1, waiting for transfers between devices, expert_work(): lax.psum_scatter(rounded.astype(jnp.bfloat16), 'tp', scatter_dimension=3,...  80.2 us
    all_to_all x1, waiting for transfers between devices, body(): lax.all_to_all(produced, ('side', 'grp'), split_axis=0, concat_axis=0, ti...  49.9 us
    dot_general x1, matrix products, expert_work(): jnp.einsum('sxcf,xfd->sxcd', activation, w_down, preferred_element_type=j...  13.7 us
    all_gather x1, blocking collectives, body(): lax.all_gather(own_summed.astype(jnp.bfloat16), 'tp', axis=1, tiled=True)  12.3 us
    all_to_all x1, starting transfers between devices, body(): lax.all_to_all(produced, ('side', 'grp'), split_axis=0, concat_axis=0, ti...  11.1 us
  transfers between devices with their start and end apart: 2, of which 2 were waited for; matrix products, arithmetic and copies ran while one was open for 0% of the time, Pallas kernels for 0%

commit v1 on v0

v1 whole, which is shorter than its diff:
```python
import functools
import math

import jax
import jax.numpy as jnp
from jax import lax
from jax.experimental import pallas as pl
from jax.experimental.pallas import tpu as pltpu
from jax.sharding import PartitionSpec as P

HD = 128
TOPK = 8
EXP_DEV = 2
N_TP = 4
SLOTS = 8

epsilon = 1e-06
F32 = jnp.float32
BF16 = jnp.bfloat16


def attention(queries, new_key, new_value, key_cache, value_cache, cache_len):
    row_count = queries.shape[0]
    head_count = queries.shape[1] // HD
    cache_span = key_cache.shape[1]
    query_heads = queries.reshape(row_count, head_count, HD)
    score_scale = 1.0 / math.sqrt(HD)
    cache_scores = (
        jnp.einsum("rgd,rjd->rgj", query_heads, key_cache, preferred_element_type=F32)
        * score_scale
    )
    live_mask = jnp.arange(cache_span)[None, :] < cache_len[:, None]
    cache_scores = jnp.where(live_mask[:, None, :], cache_scores, -jnp.inf)
    fresh_scores = (
        jnp.einsum("rgd,rd->rg", query_heads, new_key, preferred_element_type=F32) * score_scale
    )
    top_score = jnp.maximum(jnp.max(cache_scores, axis=-1), fresh_scores)
    cache_exp = jnp.exp(cache_scores - top_score[..., None])
    fresh_exp = jnp.exp(fresh_scores - top_score)
    denominator = jnp.sum(cache_exp, axis=-1) + fresh_exp
    cache_weights = (cache_exp / denominator[..., None]).astype(BF16)
    fresh_weights = (fresh_exp / denominator).astype(BF16)
    attended = jnp.einsum("rgj,rjd->rgd", cache_weights, value_cache, preferred_element_type=F32)
    attended = attended + fresh_weights.astype(F32)[..., None] * new_value.astype(F32)[:, None, :]
    return attended.reshape(row_count, head_count * HD)


def route_kernel(ids_ref, probs_ref, place0_ref, place1_ref, hi0_ref, hi1_ref, lo0_ref, lo1_ref):
    rows, experts = ids_ref.shape[0], EXP_DEV * place0_ref.shape[1] // SLOTS
    ids, probs = ids_ref[...], probs_ref[...]
    mix = probs / jnp.sum(probs, axis=1, keepdims=True)
    lane = lax.broadcasted_iota(jnp.int32, (rows, experts), 1)
    hits = jnp.zeros((rows, experts), F32)
    mixed = jnp.zeros((rows, experts), F32)
    for k in range(TOPK):
        same = ids[:, k : k + 1] == lane
        hits = hits + jnp.where(same, 1.0, 0.0)
        mixed = mixed + jnp.where(same, mix[:, k : k + 1], 0.0)
    before = lax.broadcasted_iota(jnp.int32, (rows, rows), 1) < lax.broadcasted_iota(
        jnp.int32, (rows, rows), 0
    )
    hits = hits.astype(BF16)
    earlier = jnp.dot(before.astype(F32).astype(BF16), hits, preferred_element_type=F32)
    earlier = earlier.astype(BF16)
    mix_hi = mixed.astype(BF16)
    mix_lo = (mixed - mix_hi.astype(F32)).astype(BF16)
    width = place0_ref.shape[1]
    slot = lax.broadcasted_iota(jnp.int32, (rows, width), 1) % SLOTS
    owner = lax.broadcasted_iota(jnp.int32, (experts, width), 1) // SLOTS
    expert = lax.broadcasted_iota(jnp.int32, (experts, width), 0)
    for j, (place_ref, hi_ref, lo_ref) in enumerate(
        ((place0_ref, hi0_ref, lo0_ref), (place1_ref, hi1_ref, lo1_ref))
    ):
        spread = jnp.where(expert == owner * EXP_DEV + j, 1.0, 0.0).astype(BF16)
        wide = functools.partial(jnp.dot, preferred_element_type=F32)
        chosen = (wide(hits, spread) > 0.5) & (
            wide(earlier, spread).astype(jnp.int32) == slot
        )
        place_ref[...] = jnp.where(chosen, 1.0, 0.0).astype(BF16)
        hi_ref[...] = jnp.where(chosen, wide(mix_hi, spread), 0.0).astype(BF16)
        lo_ref[...] = jnp.where(chosen, wide(mix_lo, spread), 0.0).astype(BF16)


def route(expert_ids, gate_probs, devices):
    rows = expert_ids.shape[0]
    shape = jax.ShapeDtypeStruct((rows, devices * SLOTS), BF16)
    return pl.pallas_call(
        route_kernel, out_shape=(shape,) * 6, name="route"
    )(expert_ids, gate_probs)


def split_kernel(me_ref, w_ref, *out_refs):
    part = out_refs[0].shape[2]
    for turn, out_ref in enumerate(out_refs):
        start = pl.multiple_of(lax.rem(me_ref[0] + turn, N_TP) * part, part)
        out_ref[...] = w_ref[:, :, pl.ds(start, part)]


def split_columns(me, w):
    count, hidden, width = w.shape
    part = width // N_TP
    return pl.pallas_call(
        split_kernel,
        grid_spec=pltpu.PrefetchScalarGridSpec(
            num_scalar_prefetch=1,
            grid=(count,),
            in_specs=[pl.BlockSpec((1, hidden, width), lambda e, m: (e, 0, 0))],
            out_specs=[pl.BlockSpec((1, hidden, part), lambda e, m: (e, 0, 0))] * N_TP,
        ),
        out_shape=[jax.ShapeDtypeStruct((count, hidden, part), w.dtype)] * N_TP,
        name="split_columns",
        cost_estimate=pl.CostEstimate(flops=0, bytes_accessed=4 * w.size, transcendentals=0),
    )(me, w)


RIGHT = [(i, (i + 1) % N_TP) for i in range(N_TP)]
LEFT = [(i, (i - 1) % N_TP) for i in range(N_TP)]
ACROSS = [(i, (i + 2) % N_TP) for i in range(N_TP)]


def exchange(blocks):
    own, for_right, for_across, for_left = blocks
    from_left = lax.ppermute(for_right, "tp", RIGHT)
    from_right = lax.ppermute(for_left, "tp", LEFT)
    return own, from_left, from_right, lax.ppermute(for_across, "tp", ACROSS)


def ring(x):
    half = x.shape[0] // 2
    from_left = lax.ppermute(x, "tp", RIGHT)
    from_right = lax.ppermute(x, "tp", LEFT)
    far_low = lax.ppermute(from_left[:half], "tp", RIGHT)
    far_high = lax.ppermute(from_right[half:], "tp", LEFT)
    return x, from_left, from_right, far_low, far_high


ORIGIN = (0, N_TP - 1, 1, 2)


def up_kernel(me_ref, own, left, right, low, high, gate_ref, up_ref, inv_ref, out_ref):
    part = own.shape[1]
    dims = (((1,), (1,)), ((), ()))

    def run(far):
        gate = up = squares = None
        for block, turn in zip((own, left, right, far), ORIGIN, strict=True):
            start = pl.multiple_of(lax.rem(me_ref[0] + turn, N_TP) * part, part)
            x = block[...]
            cols = pl.ds(start, part)
            g = lax.dot_general(x, gate_ref[0, :, cols], dims, preferred_element_type=F32)
            u = lax.dot_general(x, up_ref[0, :, cols], dims, preferred_element_type=F32)
            plain = x.astype(F32) * inv_ref[:, cols]
            s = jnp.sum(plain * plain, axis=1, keepdims=True)
            gate, up, squares = (g, u, s) if gate is None else (gate + g, up + u, squares + s)
        scale = lax.rsqrt(squares / (N_TP * part) + epsilon)
        gate, up = gate * scale, up * scale
        out_ref[...] = (gate / (1.0 + jnp.exp(-gate)) * up).astype(out_ref.dtype)

    @pl.when(pl.program_id(0) == 0)
    def _():
        run(low)

    @pl.when(pl.program_id(0) == 1)
    def _():
        run(high)


def up_project(me, blocks, w_gate, w_up, inv_gain, expert):
    rows, part = blocks[0].shape
    hidden, width = w_gate.shape[1:]
    half = rows // 2
    row = pl.BlockSpec((half, part), lambda i, m: (i, 0))
    far = pl.BlockSpec((half, part), lambda i, m: (0, 0))
    weight = pl.BlockSpec((1, hidden, width), lambda i, m: (expert, 0, 0))
    return pl.pallas_call(
        up_kernel,
        grid_spec=pltpu.PrefetchScalarGridSpec(
            num_scalar_prefetch=1,
            grid=(2,),
            in_specs=[row, row, row, far, far, weight, weight,
                      pl.BlockSpec((1, width), lambda i, m: (0, 0))],
            out_specs=pl.BlockSpec((half, hidden), lambda i, m: (i, 0)),
        ),
        out_shape=jax.ShapeDtypeStruct((rows, hidden), BF16),
        compiler_params=pltpu.CompilerParams(vmem_limit_bytes=40 << 20),
        cost_estimate=pl.CostEstimate(
            flops=4 * rows * width * hidden,
            bytes_accessed=2 * rows * width + 4 * hidden * width,
            transcendentals=rows * hidden,
        ),
        name="up_project",
    )(me, *blocks, w_gate, w_up, inv_gain)


def down_kernel(own, left, right, low, high, w0, w1, w2, w3, out_ref):
    def run(far):
        total = None
        for block, w_ref in zip((own, left, right, far), (w0, w1, w2, w3), strict=True):
            term = jnp.dot(block[...], w_ref[0], preferred_element_type=F32)
            total = term if total is None else total + term
        out_ref[...] = total.astype(out_ref.dtype)

    @pl.when(pl.program_id(0) == 0)
    def _():
        run(low)

    @pl.when(pl.program_id(0) == 1)
    def _():
        run(high)


def down_project(blocks, weights, expert):
    rows, hidden = blocks[0].shape
    part = weights[0].shape[2]
    half = rows // 2
    row = pl.BlockSpec((half, hidden), lambda i: (i, 0))
    far = pl.BlockSpec((half, hidden), lambda i: (0, 0))
    return pl.pallas_call(
        down_kernel,
        grid=(2,),
        in_specs=[row, row, row, far, far]
        + [pl.BlockSpec((1, hidden, part), lambda i: (expert, 0, 0))] * N_TP,
        out_specs=pl.BlockSpec((half, part), lambda i: (i, 0)),
        out_shape=jax.ShapeDtypeStruct((rows, part), BF16),
        compiler_params=pltpu.CompilerParams(vmem_limit_bytes=40 << 20),
        cost_estimate=pl.CostEstimate(
            flops=8 * rows * hidden * part,
            bytes_accessed=8 * rows * hidden + 8 * hidden * part + 2 * rows * part,
            transcendentals=0,
        ),
        name="down_project",
    )(*blocks, *weights)


def place_kernel(place_ref, rows_ref, *refs):
    out_ref = refs[-1]
    dims = (((0,), (0,)), ((), ()))
    out_ref[...] = lax.dot_general(
        place_ref[...], rows_ref[...], dims, preferred_element_type=F32
    ).astype(out_ref.dtype)


def place_rows(place, rows, *after):
    slots, part = place.shape[1], rows.shape[1]
    return pl.pallas_call(
        place_kernel,
        in_specs=[pl.BlockSpec(memory_space=pltpu.VMEM)] * 2
        + [pl.BlockSpec(memory_space=pl.ANY)] * len(after),
        out_shape=jax.ShapeDtypeStruct((slots, part), BF16),
        cost_estimate=pl.CostEstimate(
            flops=2 * place.size * part, bytes_accessed=4 * slots * part, transcendentals=0
        ),
        name="place_rows",
    )(place, rows, *after)


def combine_kernel(summed, hi0, lo0, hi1, lo1, back0, back1, out_ref):
    dot = functools.partial(jnp.dot, preferred_element_type=F32)
    total = summed[...]
    for hi, lo, back in ((hi0, lo0, back0), (hi1, lo1, back1)):
        values = back[...]
        total = total + (dot(hi[...], values) + dot(lo[...], values))
    out_ref[...] = total.astype(out_ref.dtype)


def combine(summed, hi0, lo0, hi1, lo1, back0, back1):
    rows, part = summed.shape
    steps = 4
    piece = part // steps
    slots = back0.shape[0]
    weight = pl.BlockSpec((rows, slots), lambda i: (0, 0))
    column = pl.BlockSpec((rows, piece), lambda i: (0, i))
    back = pl.BlockSpec((slots, piece), lambda i: (0, i))
    return pl.pallas_call(
        combine_kernel,
        grid=(steps,),
        in_specs=[column, weight, weight, weight, weight, back, back],
        out_specs=column,
        out_shape=jax.ShapeDtypeStruct((rows, part), BF16),
        name="combine",
    )(summed, hi0, lo0, hi1, lo1, back0, back1)


def body(
    queries, new_key, new_value, key_cache, value_cache, cache_len, residual,
    norm_gain, expert_ids, gate_probs, w_gate, w_up, w_down,
):
    rows, part = residual.shape
    group = ("side", "grp")
    devices = lax.axis_size("side") * lax.axis_size("grp")
    tp = lax.axis_index("tp")
    me = tp.astype(jnp.int32).reshape(1)
    place0, place1, hi0, hi1, lo0, lo1 = route(expert_ids, gate_probs, devices)
    attended = attention(queries, new_key, new_value, key_cache, value_cache, cache_len)
    summed = residual.astype(F32) + attended
    gain = lax.dynamic_slice(norm_gain, (tp * part,), (part,))
    scaled = (summed * gain[None, :]).astype(BF16)
    inv_gain = (1.0 / norm_gain).reshape(1, -1)
    swap = functools.partial(
        lax.all_to_all, axis_name=group, split_axis=0, concat_axis=0, tiled=True
    )
    moved = exchange(split_columns(me, w_down))
    backs = []
    arrived = [
        swap(place_rows(place0, scaled)), swap(place_rows(place1, scaled, *moved[1:]))
    ]
    for expert in range(EXP_DEV):
        activation = up_project(me, ring(arrived[expert]), w_gate, w_up, inv_gain, expert)
        produced = down_project(ring(activation), moved, expert)
        backs.append(swap(produced))
    return combine(summed, hi0, lo0, hi1, lo1, *backs)


def solution(mesh):
    in_specs = (
        P(("side", "grp"), "tp"),
        P(("side", "grp"), "tp"),
        P(("side", "grp"), "tp"),
        P(("side", "grp"), None, "tp"),
        P(("side", "grp"), None, "tp"),
        P(("side", "grp")),
        P(("side", "grp"), "tp"),
        P(),
        P(("side", "grp"), None),
        P(("side", "grp"), None),
        P(("side", "grp"), "tp", None),
        P(("side", "grp"), "tp", None),
        P(("side", "grp"), "tp", None),
    )
    out_specs = P(("side", "grp"), "tp")
    return jax.shard_map(body, mesh=mesh, in_specs=in_specs, out_specs=out_specs, check_vma=False)
```

time: 419 us -> 258 us (0.62)
  blocking collectives: 211 us -> 43.1 us
  starting transfers between devices: 11.1 us -> 62.9 us
  waiting for transfers between devices: 130 us -> 95.3 us
  Pallas kernels: 0 us -> 28.1 us
  matrix products: 26.9 us -> 4.48 us
  between operations: 13.6 us -> 0.26 us
    all_to_all x1, blocking collectives: 199 us -> 43.1 us  [body(): backs.append(swap(produced))]
    ppermute x0 -> x19, waiting for transfers between devices: none -> 95.3 us  [the longest x4 30.4 us: ring(): from_right = lax.ppermute(x, 'tp', LEFT)]
    reduce_scatter x1 -> x0, waiting for transfers between devices: 80.2 us -> none  [expert_work(): lax.psum_scatter(rounded.astype(jnp.bfloat16), 'tp', scatter_dimension=3,...]
    all_to_all x1 -> x3, waiting for transfers between devices: 49.9 us -> 0.01 us  [the longest x1 0.01 us: body(): swap(place_rows(place0, scaled))]
    all_to_all x1 -> x3, starting transfers between devices: 11.1 us -> 41.4 us  [the longest x1 16.4 us: body(): backs.append(swap(produced))]
    pallas_call x0 -> x9, Pallas kernels: none -> 28.1 us  [the longest x2 8.79 us: up_project(): pl.pallas_call(up_kernel, grid_spec=pltpu.PrefetchScalarGridSpec(num_scal...]
    dot_general x6 -> x3, matrix products: 26.9 us -> 4.48 us  [the longest x1 2.3 us: attention(): jnp.einsum('rgj,rjd->rgd', cache_weights, value_cache, preferred_element_...]
    ppermute x0 -> x19, starting transfers between devices: none -> 21.5 us  [the longest x4 7.48 us: ring(): far_high = lax.ppermute(from_right[half:], 'tp', LEFT)]
  transfers between devices with their start and end apart: 2 -> 22, of which waited for: 2 -> 11; matrix products, arithmetic and copies ran while one was open for 0% -> 1% of each run, Pallas kernels for 0% -> 8%
where the time goes in v1:
time: 258 us; the launch traced here: 256 us
  waiting for transfers between devices  95.3 us (37%)
  starting transfers between devices  62.9 us (24%)
  blocking collectives  43.1 us (17%)
  Pallas kernels  28.1 us (11%)
  local copies, waits for them, and re-layouts  19.7 us (8%)
  matrix products  4.48 us (2%)
  other arithmetic  2.68 us (1%)
    all_to_all x1, blocking collectives, body(): backs.append(swap(produced))  43.1 us
    ppermute x4, waiting for transfers between devices, ring(): from_right = lax.ppermute(x, 'tp', LEFT)  30.4 us
    ppermute x4, waiting for transfers between devices, ring(): far_high = lax.ppermute(from_right[half:], 'tp', LEFT)  22.7 us
    ppermute x1, waiting for transfers between devices, exchange(): return (own, from_left, from_right, lax.ppermute(for_across, 'tp', ACROSS))  17.8 us
    all_to_all x1, starting transfers between devices, body(): backs.append(swap(produced))  16.4 us
    unnamed x33, local copies, waits for them, and re-layouts  16 us
    ppermute x1, waiting for transfers between devices, exchange(): from_left = lax.ppermute(for_right, 'tp', RIGHT)  16 us
    all_to_all x1, starting transfers between devices, body(): swap(place_rows(place0, scaled))  13.4 us
  transfers between devices with their start and end apart: 22, of which 11 were waited for; matrix products, arithmetic and copies ran while one was open for 1% of the time, Pallas kernels for 8%

profile of v1, /device:TPU:1, one launch (start us, length us, event | category | flops | bytes accessed | tf_op | source)
XLA Modules:
  0.0 256.5 jit_solution(13866153800183482784)
XLA Ops:
  0.0 0.9 iota_compare_fusion
  0.9 0.7 convert_element_type.22
  1.6 1.4 copy.14.ids_ref
  3.0 1.4 copy.15.probs_ref
  4.4 0.9 copy.18
  5.3 0.9 fusion.4
  6.2 1.3 fusion.8
  7.5 0.2 fusion.1
  7.8 0.0 dynamic-slice-start
  7.8 2.1 route.1
  9.9 2.3 convolution_add_fusion
  12.2 0.8 multiply_convert_fusion
  13.0 2.4 place_rows.2
  15.4 13.4 %all-to-all-start = ((bf16[64,8,1024]{2,1,0:T(8,128)(2,1)}), bf16[64,8,1024]{2,1,0:T(8,128)(2,1)}, u32[]{:S(2)}, u32[]{:S(2)}) async-start(bf16[64,8,1024]{2,1,0:T(8,128)(2,1)} %bitcast.28), calls=%async_computation | async-start | bytes 2097152 | tf_op jit(solution)/shard_map/all_to_all | solution.py:305
  28.9 3.2 %split_columns.1 = (bf16[2,192,1024]{2,1,0:T(8,128)(2,1)}, bf16[2,192,1024]{2,1,0:T(8,128)(2,1)}, bf16[2,192,1024]{2,1,0:T(8,128)(2,1)}, bf16[2,192,1024]{2,1,0:T(8,128)(2,1)}) custom-call(s32[1]{0:T(128)} %bitcast.3.me_ref, bf16[2,192,4096]{2,1,0:T(8,128)(2,1)} %w_ref.1), custom_call_target="tpu_custom_call" | custom-call | bytes 6291456 | tf_op jit(solution)/shard_map/split_columns/pallas_call | solution.py:102
  32.1 1.2 collective-permute-start.8
  33.3 1.5 collective-permute-start.9
  34.7 1.5 collective-permute-start.10
  36.3 16.0 %collective-permute-done.8.w1.refs_0_ = bf16[2,192,1024]{2,1,0:T(8,128)(2,1)S(1)} collective-permute-done((bf16[2,192,1024]{2,1,0:T(8,128)(2,1)}, bf16[2,192,1024]{2,1,0:T(8,128)(2,1)S(1)}, u32[]{:S(2)}, u32[]{:S(2)}) %collective-permute-start.8) | collective-permute-done | bytes 786464 | tf_op jit(solution)/shard_map/ppermute | solution.py:123
  52.3 17.8 %collective-permute-done.10.w3.refs_2_ = bf16[2,192,1024]{2,1,0:T(8,128)(2,1)} collective-permute-done((bf16[2,192,1024]{2,1,0:T(8,128)(2,1)}, bf16[2,192,1024]{2,1,0:T(8,128)(2,1)}, u32[]{:S(2)}, u32[]{:S(2)}) %collective-permute-start.10) | collective-permute-done | bytes 786464 | tf_op jit(solution)/shard_map/ppermute | solution.py:125
  70.1 2.4 place_rows.3
  72.5 11.6 %all-to-all-start.2 = ((bf16[64,8,1024]{2,1,0:T(8,128)(2,1)}), bf16[64,8,1024]{2,1,0:T(8,128)(2,1)}, u32[]{:S(2)}, u32[]{:S(2)}) async-start(bf16[64,8,1024]{2,1,0:T(8,128)(2,1)} %bitcast.27), calls=%async_computation.2 | async-start | bytes 2097152 | tf_op jit(solution)/shard_map/all_to_all | solution.py:305
  84.1 1.8 collective-permute-start.1
  85.9 22.9 %collective-permute-done.1.right = bf16[512,1024]{1,0:T(8,128)(2,1)S(1)} collective-permute-done((bf16[512,1024]{1,0:T(8,128)(2,1)}, bf16[512,1024]{1,0:T(8,128)(2,1)S(1)}, u32[]{:S(2)}, u32[]{:S(2)}) %collective-permute-start.1) | collective-permute-done | bytes 1048608 | tf_op jit(solution)/shard_map/ppermute | solution.py:131
  108.8 3.0 %collective-permute-start.3 = (bf16[256,1024]{1,0:T(8,128)(2,1)S(1)}, bf16[256,1024]{1,0:T(8,128)(2,1)S(1)}, u32[]{:S(2)}, u32[]{:S(2)}) collective-permute-start(bf16[256,1024]{1,0:T(8,128)(2,1)S(1)} %slice.33), channel_id=1, source_target_pairs={{0,3},{1,0},{2,1},{3,2},{4,7},{5,4},{6,5},{7,6},{8,11},{9,8},{10,9... | collective-permute-start | bytes 1572872 | tf_op jit(solution)/shard_map/ppermute | solution.py:133
  111.9 0.3 collective-permute-start.2
  112.2 9.7 %collective-permute-done.3.high = bf16[256,1024]{1,0:T(8,128)(2,1)S(1)} collective-permute-done((bf16[256,1024]{1,0:T(8,128)(2,1)S(1)}, bf16[256,1024]{1,0:T(8,128)(2,1)S(1)}, u32[]{:S(2)}, u32[]{:S(2)}) %collective-permute-start.3) | collective-permute-done | bytes 524320 | tf_op jit(solution)/shard_map/ppermute | solution.py:133
  121.9 3.4 %collective-permute-done.2.low = bf16[256,1024]{1,0:T(8,128)(2,1)S(1)} collective-permute-done((bf16[256,1024]{1,0:T(8,128)(2,1)S(1)}, bf16[256,1024]{1,0:T(8,128)(2,1)S(1)}, u32[]{:S(2)}, u32[]{:S(2)}) %collective-permute-start.2) | collective-permute-done | bytes 524320 | tf_op jit(solution)/shard_map/ppermute | solution.py:132
  125.3 1.9 copy-done.1
  127.2 1.9 copy-done.3
  129.1 4.3 %up_project.2.own = bf16[512,192]{1,0:T(8,128)(2,1)S(1)} custom-call(s32[1]{0:T(128)} %bitcast.3.me_ref, bf16[512,1024]{1,0:T(8,128)(2,1)} %bitcast.5.own, bf16[512,1024]{1,0:T(8,128)(2,1)S(1)} %collective-permute-done.left, bf16[512,1024]{1,0:T(8,128)(2,1)S(1)} %collective-permute-done.1.right, bf16[256,1024]{1,0:T(8,128)(2,1)S(1)} %collective-permute-done.2.low, ...), custom_call_target="tpu_custom_call" | custom-call | flops 1610612736 | bytes 7340032 | tf_op jit(solution)/shard_map/up_project/pallas_call | solution.py:175
  133.4 0.1 collective-permute-start.5
  133.5 1.5 collective-permute-start.4
  134.9 3.8 %collective-permute-done.5.right = bf16[512,192]{1,0:T(8,128)(2,1)S(1)} collective-permute-done((bf16[512,192]{1,0:T(8,128)(2,1)S(1)}, bf16[512,192]{1,0:T(8,128)(2,1)S(1)}, u32[]{:S(2)}, u32[]{:S(2)}) %collective-permute-start.5) | collective-permute-done | bytes 196640 | tf_op jit(solution)/shard_map/ppermute | solution.py:131
  138.7 0.7 slice.35
  139.3 1.7 collective-permute-start.7
  141.0 0.7 slice.34
  141.7 0.7 copy-done.11
  142.4 2.7 %collective-permute-start.12 = (bf16[512,1024]{1,0:T(8,128)(2,1)}, bf16[512,1024]{1,0:T(8,128)(2,1)}, u32[]{:S(2)}, u32[]{:S(2)}) collective-permute-start(bf16[512,1024]{1,0:T(8,128)(2,1)} %bitcast.10.own), channel_id=1, source_target_pairs={{0,3},{1,0},{2,1},{3,2},{4,7},{5,4},{6,5},{7,6},{8,11},{9,8},{10,9... | collective-permute-start | bytes 3145736 | tf_op jit(solution)/shard_map/ppermute | solution.py:131
  145.1 2.7 %collective-permute-done.6.low = bf16[256,192]{1,0:T(8,128)(2,1)} collective-permute-done((bf16[256,192]{1,0:T(8,128)(2,1)}, bf16[256,192]{1,0:T(8,128)(2,1)}, u32[]{:S(2)}, u32[]{:S(2)}) %collective-permute-start.6) | collective-permute-done | bytes 98336 | tf_op jit(solution)/shard_map/ppermute | solution.py:132
  147.8 1.1 copy-done.9
  148.9 0.9 copy-done.12
  149.8 2.6 %down_project.2 = bf16[512,1024]{1,0:T(8,128)(2,1)S(1)} custom-call(bf16[512,192]{1,0:T(8,128)(2,1)S(1)} %up_project.2.own, bf16[512,192]{1,0:T(8,128)(2,1)S(1)} %copy-done.12, bf16[512,192]{1,0:T(8,128)(2,1)S(1)} %collective-permute-done.5.right, bf16[256,192]{1,0:T(8,128)(2,1)} %collective-permute-done.6.low, ...), custom_call_target="tpu_custom_call" | custom-call | flops 805306368 | bytes 3407872 | tf_op jit(solution)/shard_map/down_project/pallas_call | solution.py:218
  152.5 1.0 copy-done.7
  153.4 16.4 %all-to-all-start.1 = ((bf16[64,8,1024]{2,1,0:T(8,128)(2,1)}), bf16[64,8,1024]{2,1,0:T(8,128)(2,1)}, u32[]{:S(2)}, u32[]{:S(2)}) async-start(bf16[64,8,1024]{2,1,0:T(8,128)(2,1)} %bitcast.23), calls=%async_computation.1 | async-start | bytes 2097152 | tf_op jit(solution)/shard_map/all_to_all | solution.py:310
  169.8 1.1 slice.37
  170.9 0.1 collective-permute-start.14
  171.0 1.1 slice.36
  172.2 1.7 collective-permute-start.13
  173.9 10.2 %collective-permute-done.14.high = bf16[256,1024]{1,0:T(8,128)(2,1)S(1)} collective-permute-done((bf16[256,1024]{1,0:T(8,128)(2,1)S(1)}, bf16[256,1024]{1,0:T(8,128)(2,1)S(1)}, u32[]{:S(2)}, u32[]{:S(2)}) %collective-permute-start.14) | collective-permute-done | bytes 524320 | tf_op jit(solution)/shard_map/ppermute | solution.py:133
  184.2 1.9 copy-done.2
  186.1 1.9 copy-done.4
  188.0 4.5 %up_project.3.own = bf16[512,192]{1,0:T(8,128)(2,1)S(1)} custom-call(s32[1]{0:T(128)} %bitcast.3.me_ref, bf16[512,1024]{1,0:T(8,128)(2,1)} %bitcast.10.own, bf16[512,1024]{1,0:T(8,128)(2,1)} %collective-permute-done.11.left, bf16[512,1024]{1,0:T(8,128)(2,1)} %collective-permute-done.12.right, bf16[256,1024]{1,0:T(8,128)(2,1)S(1)} %collective-permute-done.13.low, ...), custom_call_target="tpu_custom_call" | custom-call | flops 1610612736 | bytes 7340032 | tf_op jit(solution)/shard_map/up_project/pallas_call | solution.py:175
  192.5 0.1 collective-permute-start.16
  192.6 1.6 collective-permute-start.15
  194.2 3.7 %collective-permute-done.16.right = bf16[512,192]{1,0:T(8,128)(2,1)S(1)} collective-permute-done((bf16[512,192]{1,0:T(8,128)(2,1)S(1)}, bf16[512,192]{1,0:T(8,128)(2,1)S(1)}, u32[]{:S(2)}, u32[]{:S(2)}) %collective-permute-start.16) | collective-permute-done | bytes 196640 | tf_op jit(solution)/shard_map/ppermute | solution.py:131
  197.9 2.7 %collective-permute-start.18 = (bf16[256,192]{1,0:T(8,128)(2,1)S(1)}, bf16[256,192]{1,0:T(8,128)(2,1)S(1)}, u32[]{:S(2)}, u32[]{:S(2)}) collective-permute-start(bf16[256,192]{1,0:T(8,128)(2,1)S(1)} %slice.39), channel_id=1, source_target_pairs={{0,3},{1,0},{2,1},{3,2},{4,7},{5,4},{6,5},{7,6},{8,11},{9,8},{10,9... | collective-permute-start | bytes 294920 | tf_op jit(solution)/shard_map/ppermute | solution.py:133
  200.6 0.1 collective-permute-start.17
  200.7 2.8 %collective-permute-done.18.high = bf16[256,192]{1,0:T(8,128)(2,1)S(1)} collective-permute-done((bf16[256,192]{1,0:T(8,128)(2,1)S(1)}, bf16[256,192]{1,0:T(8,128)(2,1)S(1)}, u32[]{:S(2)}, u32[]{:S(2)}) %collective-permute-start.18) | collective-permute-done | bytes 98336 | tf_op jit(solution)/shard_map/ppermute | solution.py:133
  203.5 2.2 collective-permute-done.17.low
  205.7 2.5 down_project.3
  208.3 1.0 copy-done.8
  209.3 43.1 %all_to_all.44 = bf16[64,8,1024]{2,1,0:T(8,128)(2,1)} all-to-all(bf16[64,8,1024]{2,1,0:T(8,128)(2,1)} %bitcast.24), channel_id=1, replica_groups=mesh['side'=2,'grp'=32,'tp'=4] {'side','grp'}, dimensions={0} | all-to-all | bytes 2097152 | tf_op jit(solution)/shard_map/all_to_all | solution.py:310
  252.4 4.1 %combine.1 = bf16[64,1024]{1,0:T(8,128)(2,1)} custom-call(f32[64,1024]{1,0:T(8,128)} %get-tuple-element.26.summed, bf16[64,512]{1,0:T(8,128)(2,1)} %get-tuple-element.15.hi0, bf16[64,512]{1,0:T(8,128)(2,1)} %get-tuple-element.16.lo0, bf16[64,512]{1,0:T(8,128)(2,1)} %get-tuple-element.17.hi1, bf16[64,512]{1,0:T(8,128)(2,1)} %get-tuple-element.18.lo1, ...), custom_call_target="tpu_custom_call" | custom-call | tf_op jit(solution)/shard_map/combine/pallas_call | solution.py:274
  (43 shorter events, 0.2 us)
Async XLA Ops:
  0.0 6.2 %copy-start = (bf16[64,128,128]{2,1,0:T(8,128)(2,1)S(1)}, bf16[64,128,128]{2,1,0:T(8,128)(2,1)}, u32[]{:S(2)}) copy-start(bf16[64,128,128]{2,1,0:T(8,128)(2,1)} %param.16) | copy-start | bytes 6291460
  7.5 4.7 %copy-start.13 = (bf16[64,1024]{1,0:T(8,128)(2,1)S(1)}, bf16[64,1024]{1,0:T(8,128)(2,1)}, u32[]{:S(2)}) copy-start(bf16[64,1024]{1,0:T(8,128)(2,1)} %param.19) | copy-start | bytes 393220
  7.8 4.4 %dynamic-slice-start = ((f32[4096]{0:T(1024)}, s32[]{:T(128)}), f32[1024]{0:T(1024)S(1)}, s32[]{:S(2)}) async-start(f32[4096]{0:T(1024)} %param.20, s32[]{:T(128)} %select_n.8), calls=%async_computation.4 | async-start | bytes 8704 | tf_op jit(solution)/shard_map/dynamic_slice | solution.py:296
  15.4 57.1 %all-to-all-start = ((bf16[64,8,1024]{2,1,0:T(8,128)(2,1)}), bf16[64,8,1024]{2,1,0:T(8,128)(2,1)}, u32[]{:S(2)}, u32[]{:S(2)}) async-start(bf16[64,8,1024]{2,1,0:T(8,128)(2,1)} %bitcast.28), calls=%async_computation | async-start | bytes 2097152 | tf_op jit(solution)/shard_map/all_to_all | solution.py:305
  32.1 20.2 %collective-permute-start.8 = (bf16[2,192,1024]{2,1,0:T(8,128)(2,1)}, bf16[2,192,1024]{2,1,0:T(8,128)(2,1)S(1)}, u32[]{:S(2)}, u32[]{:S(2)}) collective-permute-start(bf16[2,192,1024]{2,1,0:T(8,128)(2,1)} %get-tuple-element.21), channel_id=1, source_target_pairs={{0,1},{1,2},{2,3},{3,0},{4,5},{5,6},{6,7},{7,4},{8,9},{9,10},{10,1... | collective-permute-start | bytes 2359304 | tf_op jit(solution)/shard_map/ppermute | solution.py:123
  33.3 19.0 %collective-permute-start.9 = (bf16[2,192,1024]{2,1,0:T(8,128)(2,1)}, bf16[2,192,1024]{2,1,0:T(8,128)(2,1)}, u32[]{:S(2)}, u32[]{:S(2)}) collective-permute-start(bf16[2,192,1024]{2,1,0:T(8,128)(2,1)} %get-tuple-element.22), channel_id=1, source_target_pairs={{0,3},{1,0},{2,1},{3,2},{4,7},{5,4},{6,5},{7,6},{8,11},{9,8},{10,9... | collective-permute-start | bytes 2359304 | tf_op jit(solution)/shard_map/ppermute | solution.py:124
  34.7 35.4 %collective-permute-start.10 = (bf16[2,192,1024]{2,1,0:T(8,128)(2,1)}, bf16[2,192,1024]{2,1,0:T(8,128)(2,1)}, u32[]{:S(2)}, u32[]{:S(2)}) collective-permute-start(bf16[2,192,1024]{2,1,0:T(8,128)(2,1)} %get-tuple-element.23), channel_id=1, source_target_pairs={{0,2},{1,3},{2,0},{3,1},{4,6},{5,7},{6,4},{7,5},{8,10},{9,11},{10,... | collective-permute-start | bytes 2359304 | tf_op jit(solution)/shard_map/ppermute | solution.py:125
  52.3 17.8 %copy-start.5 = (bf16[2,192,1024]{2,1,0:T(8,128)(2,1)}, bf16[2,192,1024]{2,1,0:T(8,128)(2,1)S(1)}, u32[]{:S(2)}) copy-start(bf16[2,192,1024]{2,1,0:T(8,128)(2,1)S(1)} %collective-permute-done.8.w1.refs_0_) | copy-start | bytes 2359300
  72.5 39.6 %copy-start.14 = (f32[4096]{0:T(1024)S(1)}, f32[4096]{0:T(1024)}, u32[]{:S(2)}) copy-start(f32[4096]{0:T(1024)} %param.20) | copy-start | bytes 49156
  72.5 69.9 %all-to-all-start.2 = ((bf16[64,8,1024]{2,1,0:T(8,128)(2,1)}), bf16[64,8,1024]{2,1,0:T(8,128)(2,1)}, u32[]{:S(2)}, u32[]{:S(2)}) async-start(bf16[64,8,1024]{2,1,0:T(8,128)(2,1)} %bitcast.27), calls=%async_computation.2 | async-start | bytes 2097152 | tf_op jit(solution)/shard_map/all_to_all | solution.py:305
  84.1 24.7 %collective-permute-start.1 = (bf16[512,1024]{1,0:T(8,128)(2,1)}, bf16[512,1024]{1,0:T(8,128)(2,1)S(1)}, u32[]{:S(2)}, u32[]{:S(2)}) collective-permute-start(bf16[512,1024]{1,0:T(8,128)(2,1)} %bitcast.5.own), channel_id=1, source_target_pairs={{0,3},{1,0},{2,1},{3,2},{4,7},{5,4},{6,5},{7,6},{8,11},{9,8},{10,9... | collective-permute-start | bytes 3145736 | tf_op jit(solution)/shard_map/ppermute | solution.py:131
  85.9 25.9 %collective-permute-start = (bf16[512,1024]{1,0:T(8,128)(2,1)}, bf16[512,1024]{1,0:T(8,128)(2,1)S(1)}, u32[]{:S(2)}, u32[]{:S(2)}) collective-permute-start(bf16[512,1024]{1,0:T(8,128)(2,1)} %bitcast.5.own), channel_id=1, source_target_pairs={{0,1},{1,2},{2,3},{3,0},{4,5},{5,6},{6,7},{7,4},{8,9},{9,10},{10,1... | collective-permute-start | bytes 3145736 | tf_op jit(solution)/shard_map/ppermute | solution.py:130
  108.8 13.0 %collective-permute-start.3 = (bf16[256,1024]{1,0:T(8,128)(2,1)S(1)}, bf16[256,1024]{1,0:T(8,128)(2,1)S(1)}, u32[]{:S(2)}, u32[]{:S(2)}) collective-permute-start(bf16[256,1024]{1,0:T(8,128)(2,1)S(1)} %slice.33), channel_id=1, source_target_pairs={{0,3},{1,0},{2,1},{3,2},{4,7},{5,4},{6,5},{7,6},{8,11},{9,8},{10,9... | collective-permute-start | bytes 1572872 | tf_op jit(solution)/shard_map/ppermute | solution.py:133
  111.9 13.4 %collective-permute-start.2 = (bf16[256,1024]{1,0:T(8,128)(2,1)S(1)}, bf16[256,1024]{1,0:T(8,128)(2,1)S(1)}, u32[]{:S(2)}, u32[]{:S(2)}) collective-permute-start(bf16[256,1024]{1,0:T(8,128)(2,1)S(1)} %slice.32), channel_id=1, source_target_pairs={{0,1},{1,2},{2,3},{3,0},{4,5},{5,6},{6,7},{7,4},{8,9},{9,10},{10,1... | collective-permute-start | bytes 1572872 | tf_op jit(solution)/shard_map/ppermute | solution.py:132
  125.3 1.9 copy-start.1
  127.2 1.9 copy-start.3
  129.1 18.7 %copy-start.6 = (bf16[2,192,1024]{2,1,0:T(8,128)(2,1)S(1)}, bf16[2,192,1024]{2,1,0:T(8,128)(2,1)}, u32[]{:S(2)}) copy-start(bf16[2,192,1024]{2,1,0:T(8,128)(2,1)} %copy-done.5) | copy-start | bytes 2359300
  133.4 5.3 %collective-permute-start.5 = (bf16[512,192]{1,0:T(8,128)(2,1)S(1)}, bf16[512,192]{1,0:T(8,128)(2,1)S(1)}, u32[]{:S(2)}, u32[]{:S(2)}) collective-permute-start(bf16[512,192]{1,0:T(8,128)(2,1)S(1)} %up_project.2.own), channel_id=1, source_target_pairs={{0,3},{1,0},{2,1},{3,2},{4,7},{5,4},{6,5},{7,6},{8,11},{9,8},{10,9... | collective-permute-start | bytes 589832 | tf_op jit(solution)/shard_map/ppermute | solution.py:131
  133.5 7.6 %collective-permute-start.4 = (bf16[512,192]{1,0:T(8,128)(2,1)S(1)}, bf16[512,192]{1,0:T(8,128)(2,1)S(1)}, u32[]{:S(2)}, u32[]{:S(2)}) collective-permute-start(bf16[512,192]{1,0:T(8,128)(2,1)S(1)} %up_project.2.own), channel_id=1, source_target_pairs={{0,1},{1,2},{2,3},{3,0},{4,5},{5,6},{6,7},{7,4},{8,9},{9,10},{10,1... | collective-permute-start | bytes 589832 | tf_op jit(solution)/shard_map/ppermute | solution.py:130
  139.3 5.8 %collective-permute-start.7 = (bf16[256,192]{1,0:T(8,128)(2,1)}, bf16[256,192]{1,0:T(8,128)(2,1)S(1)}, u32[]{:S(2)}, u32[]{:S(2)}) collective-permute-start(bf16[256,192]{1,0:T(8,128)(2,1)} %slice.35), channel_id=1, source_target_pairs={{0,3},{1,0},{2,1},{3,2},{4,7},{5,4},{6,5},{7,6},{8,11},{9,8},{10,9... | collective-permute-start | bytes 294920 | tf_op jit(solution)/shard_map/ppermute | solution.py:133
  141.7 0.7 copy-start.11
  142.4 5.3 %collective-permute-start.6 = (bf16[256,192]{1,0:T(8,128)(2,1)}, bf16[256,192]{1,0:T(8,128)(2,1)}, u32[]{:S(2)}, u32[]{:S(2)}) collective-permute-start(bf16[256,192]{1,0:T(8,128)(2,1)} %slice.34), channel_id=1, source_target_pairs={{0,1},{1,2},{2,3},{3,0},{4,5},{5,6},{6,7},{7,4},{8,9},{9,10},{10,1... | collective-permute-start | bytes 294920 | tf_op jit(solution)/shard_map/ppermute | solution.py:132
  142.4 27.4 %collective-permute-start.12 = (bf16[512,1024]{1,0:T(8,128)(2,1)}, bf16[512,1024]{1,0:T(8,128)(2,1)}, u32[]{:S(2)}, u32[]{:S(2)}) collective-permute-start(bf16[512,1024]{1,0:T(8,128)(2,1)} %bitcast.10.own), channel_id=1, source_target_pairs={{0,3},{1,0},{2,1},{3,2},{4,7},{5,4},{6,5},{7,6},{8,11},{9,8},{10,9... | collective-permute-start | bytes 3145736 | tf_op jit(solution)/shard_map/ppermute | solution.py:131
  145.1 25.9 %collective-permute-start.11 = (bf16[512,1024]{1,0:T(8,128)(2,1)}, bf16[512,1024]{1,0:T(8,128)(2,1)}, u32[]{:S(2)}, u32[]{:S(2)}) collective-permute-start(bf16[512,1024]{1,0:T(8,128)(2,1)} %bitcast.10.own), channel_id=1, source_target_pairs={{0,1},{1,2},{2,3},{3,0},{4,5},{5,6},{6,7},{7,4},{8,9},{9,10},{10,1... | collective-permute-start | bytes 3145736 | tf_op jit(solution)/shard_map/ppermute | solution.py:130
  147.8 1.1 copy-start.9
  148.9 0.9 copy-start.12
  152.5 1.0 copy-start.7
  153.4 55.9 %all-to-all-start.1 = ((bf16[64,8,1024]{2,1,0:T(8,128)(2,1)}), bf16[64,8,1024]{2,1,0:T(8,128)(2,1)}, u32[]{:S(2)}, u32[]{:S(2)}) async-start(bf16[64,8,1024]{2,1,0:T(8,128)(2,1)} %bitcast.23), calls=%async_computation.1 | async-start | bytes 2097152 | tf_op jit(solution)/shard_map/all_to_all | solution.py:310
  170.9 13.2 %collective-permute-start.14 = (bf16[256,1024]{1,0:T(8,128)(2,1)S(1)}, bf16[256,1024]{1,0:T(8,128)(2,1)S(1)}, u32[]{:S(2)}, u32[]{:S(2)}) collective-permute-start(bf16[256,1024]{1,0:T(8,128)(2,1)S(1)} %slice.37), channel_id=1, source_target_pairs={{0,3},{1,0},{2,1},{3,2},{4,7},{5,4},{6,5},{7,6},{8,11},{9,8},{10,9... | collective-permute-start | bytes 1572872 | tf_op jit(solution)/shard_map/ppermute | solution.py:133
  171.0 34.7 %copy-start.10 = (bf16[2,192,1024]{2,1,0:T(8,128)(2,1)S(1)}, bf16[2,192,1024]{2,1,0:T(8,128)(2,1)}, u32[]{:S(2)}) copy-start(bf16[2,192,1024]{2,1,0:T(8,128)(2,1)} %get-tuple-element.20.w0) | copy-start | bytes 2359300
  172.2 12.0 %collective-permute-start.13 = (bf16[256,1024]{1,0:T(8,128)(2,1)S(1)}, bf16[256,1024]{1,0:T(8,128)(2,1)S(1)}, u32[]{:S(2)}, u32[]{:S(2)}) collective-permute-start(bf16[256,1024]{1,0:T(8,128)(2,1)S(1)} %slice.36), channel_id=1, source_target_pairs={{0,1},{1,2},{2,3},{3,0},{4,5},{5,6},{6,7},{7,4},{8,9},{9,10},{10,1... | collective-permute-start | bytes 1572872 | tf_op jit(solution)/shard_map/ppermute | solution.py:132
  184.2 1.9 copy-start.2
  186.1 1.9 copy-start.4
  192.5 5.4 %collective-permute-start.16 = (bf16[512,192]{1,0:T(8,128)(2,1)S(1)}, bf16[512,192]{1,0:T(8,128)(2,1)S(1)}, u32[]{:S(2)}, u32[]{:S(2)}) collective-permute-start(bf16[512,192]{1,0:T(8,128)(2,1)S(1)} %up_project.3.own), channel_id=1, source_target_pairs={{0,3},{1,0},{2,1},{3,2},{4,7},{5,4},{6,5},{7,6},{8,11},{9,8},{10,9... | collective-permute-start | bytes 589832 | tf_op jit(solution)/shard_map/ppermute | solution.py:131
  192.6 8.0 %collective-permute-start.15 = (bf16[512,192]{1,0:T(8,128)(2,1)S(1)}, bf16[512,192]{1,0:T(8,128)(2,1)S(1)}, u32[]{:S(2)}, u32[]{:S(2)}) collective-permute-start(bf16[512,192]{1,0:T(8,128)(2,1)S(1)} %up_project.3.own), channel_id=1, source_target_pairs={{0,1},{1,2},{2,3},{3,0},{4,5},{5,6},{6,7},{7,4},{8,9},{9,10},{10,1... | collective-permute-start | bytes 589832 | tf_op jit(solution)/shard_map/ppermute | solution.py:130
  197.9 5.6 %collective-permute-start.18 = (bf16[256,192]{1,0:T(8,128)(2,1)S(1)}, bf16[256,192]{1,0:T(8,128)(2,1)S(1)}, u32[]{:S(2)}, u32[]{:S(2)}) collective-permute-start(bf16[256,192]{1,0:T(8,128)(2,1)S(1)} %slice.39), channel_id=1, source_target_pairs={{0,3},{1,0},{2,1},{3,2},{4,7},{5,4},{6,5},{7,6},{8,11},{9,8},{10,9... | collective-permute-start | bytes 294920 | tf_op jit(solution)/shard_map/ppermute | solution.py:133
  200.6 5.1 %collective-permute-start.17 = (bf16[256,192]{1,0:T(8,128)(2,1)S(1)}, bf16[256,192]{1,0:T(8,128)(2,1)S(1)}, u32[]{:S(2)}, u32[]{:S(2)}) collective-permute-start(bf16[256,192]{1,0:T(8,128)(2,1)S(1)} %slice.38), channel_id=1, source_target_pairs={{0,1},{1,2},{2,3},{3,0},{4,5},{5,6},{6,7},{7,4},{8,9},{9,10},{10,1... | collective-permute-start | bytes 294920 | tf_op jit(solution)/shard_map/ppermute | solution.py:132
  208.3 1.0 copy-start.8

commit v2 on v0

v2 whole, which is shorter than its diff:
```python
import functools
import math

import jax
import jax.numpy as jnp
from jax import lax
from jax.experimental import pallas as pl
from jax.experimental.pallas import tpu as pltpu
from jax.sharding import PartitionSpec as P

HD = 128
TOPK = 8
EXP_DEV = 2
N_TP = 4
SLOTS = 8

epsilon = 1e-06
FAR_WEIGHT = (1, 14)
F32 = jnp.float32
BF16 = jnp.bfloat16


RIGHT = [(i, (i + 1) % N_TP) for i in range(N_TP)]
LEFT = [(i, (i - 1) % N_TP) for i in range(N_TP)]
ACROSS = [(i, (i + 2) % N_TP) for i in range(N_TP)]
VMEM = pl.BlockSpec(memory_space=pltpu.VMEM)
ANY = pl.BlockSpec(memory_space=pl.ANY)
BIG = pltpu.CompilerParams(vmem_limit_bytes=20 << 20)
dot = functools.partial(jnp.dot, preferred_element_type=F32)


def route_kernel(ids_ref, probs_ref, *tables):
    slots, rows = tables[0].shape
    experts = EXP_DEV * slots // SLOTS
    ids, probs = ids_ref[...], probs_ref[...]
    mix = probs / jnp.sum(probs, axis=0, keepdims=True)
    line = lax.broadcasted_iota(jnp.int32, (experts, rows), 0)
    hits = jnp.zeros((experts, rows), F32)
    mixed = jnp.zeros((experts, rows), F32)
    for k in range(TOPK):
        same = ids[k : k + 1, :] == line
        hits = hits + jnp.where(same, 1.0, 0.0)
        mixed = mixed + jnp.where(same, mix[k : k + 1, :], 0.0)
    before = lax.broadcasted_iota(jnp.int32, (rows, rows), 0) < lax.broadcasted_iota(
        jnp.int32, (rows, rows), 1
    )
    hits = hits.astype(BF16)
    earlier = dot(hits, jnp.where(before, 1.0, 0.0).astype(BF16)).astype(BF16)
    mix_hi = mixed.astype(BF16)
    mix_lo = (mixed - mix_hi.astype(F32)).astype(BF16)
    slot = (lax.broadcasted_iota(jnp.int32, (slots, rows), 0) % SLOTS).astype(F32)
    owner = lax.broadcasted_iota(jnp.int32, (slots, experts), 0) // SLOTS
    expert = lax.broadcasted_iota(jnp.int32, (slots, experts), 1)

    def table(spread, tall):
        return (dot(spread, hits) > 0.5) & (dot(spread, earlier) == tall)

    for j in range(EXP_DEV):
        spread = jnp.where(expert == owner * EXP_DEV + j, 1.0, 0.0).astype(BF16)
        chosen = table(spread, slot)
        tables[j][...] = jnp.where(chosen, dot(spread, mix_hi), 0.0).astype(BF16)
        tables[2 + j][...] = jnp.where(chosen, dot(spread, mix_lo), 0.0).astype(BF16)
    for j in range(EXP_DEV):
        spread = jnp.where(expert == owner + j * (slots // SLOTS), 1.0, 0.0).astype(BF16)
        tables[4][pl.ds(j * slots, slots), :] = jnp.where(table(spread, slot), 1.0, 0.0).astype(BF16)


def route(ids, probs, devices):
    rows = ids.shape[1]
    table = jax.ShapeDtypeStruct((devices * SLOTS, rows), BF16)

    tall = jax.ShapeDtypeStruct((EXP_DEV * devices * SLOTS, rows), BF16)
    return pl.pallas_call(
        route_kernel,
        in_specs=[VMEM, VMEM],
        out_specs=[VMEM] * 5,
        out_shape=[table] * 4 + [tall],
        cost_estimate=pl.CostEstimate(
            flops=16 * devices * SLOTS * rows, bytes_accessed=0, transcendentals=0
        ),
        name="route",
    )(ids, probs)


def split_columns(me, w):
    count, hidden, width = w.shape
    part = width // N_TP
    block = pl.BlockSpec((1, hidden // 2, part), lambda h, m: (0, h, 0))
    shape = jax.ShapeDtypeStruct((1, hidden, part), w.dtype)

    def kernel(me_ref, w_ref, *out_refs):
        for e in range(count):
            for turn in range(1, N_TP):
                out_refs[e * (N_TP - 1) + turn - 1][0] = w_ref[e, :, columns(me_ref, turn, part)]

    return pl.pallas_call(
        kernel,
        grid_spec=pltpu.PrefetchScalarGridSpec(
            num_scalar_prefetch=1,
            grid=(2,),
            in_specs=[pl.BlockSpec((count, hidden // 2, width), lambda h, m: (0, h, 0))],
            out_specs=[block] * (count * (N_TP - 1)),
        ),
        out_shape=[shape] * (count * (N_TP - 1)),
        compiler_params=BIG,
        cost_estimate=pl.CostEstimate(flops=0, bytes_accessed=4 * w.size, transcendentals=0),
        name="split_columns",
    )(me, w)


def attention_kernel(
    lens_ref, q_ref, nk_ref, nv_ref, k_ref, v_ref, res_ref, gain_ref, summed_ref, scaled_ref
):
    rows, span, depth = k_ref.shape
    heads = q_ref.shape[1] // depth
    base = pl.program_id(0) * rows
    lines = rows * heads
    q = q_ref[...].astype(F32).reshape(rows, heads, depth)
    qb = q.astype(BF16)
    dims = (((1,), (1,)), ((), ()))
    scores = jnp.concatenate(
        [
            lax.dot_general(qb[r], k_ref[r], dims, preferred_element_type=F32)
            for r in range(rows)
        ],
        axis=0,
    )
    scale = 1.0 / math.sqrt(depth)
    line = lax.broadcasted_iota(jnp.int32, (lines, span), 0) // heads
    limit = jnp.zeros((lines, span), jnp.int32)
    for r in range(rows):
        limit = jnp.where(line == r, lens_ref[base + r], limit)
    live = lax.broadcasted_iota(jnp.int32, (lines, span), 1) < limit
    scores = jnp.where(live, scores * scale, -jnp.inf)
    fresh_key = jnp.broadcast_to(nk_ref[...].astype(F32)[:, None, :], (rows, heads, depth))
    fresh = jnp.sum(q * fresh_key, axis=2, keepdims=True).reshape(lines, 1) * scale
    top = jnp.maximum(jnp.max(scores, axis=1, keepdims=True), fresh)
    exps = jnp.exp(scores - top)
    fresh_exp = jnp.exp(fresh - top)
    total = jnp.sum(exps, axis=1, keepdims=True) + fresh_exp
    weights = (exps / total).astype(BF16)
    fresh_weight = (fresh_exp / total).astype(BF16).astype(F32)
    fresh_value = jnp.broadcast_to(nv_ref[...].astype(F32)[:, None, :], (rows, heads, depth))
    out = jnp.concatenate(
        [dot(weights[r * heads : (r + 1) * heads], v_ref[r]) for r in range(rows)], axis=0
    )
    out = out + fresh_weight * fresh_value.reshape(lines, depth)
    summed = res_ref[...].astype(F32) + out.reshape(rows, heads, depth).reshape(
        rows, heads * depth
    )
    summed_ref[...] = summed
    scaled_ref[...] = (summed * gain_ref[...]).astype(BF16)


def attention(lens, me, queries, new_key, new_value, keys, values, residual, gain):
    rows, part = queries.shape
    span, depth = keys.shape[1:]
    step = 16
    wide = pl.BlockSpec((step, part), lambda i, n, m: (i, 0))
    slim = pl.BlockSpec((step, depth), lambda i, n, m: (i, 0))
    cache = pl.BlockSpec((step, span, depth), lambda i, n, m: (i, 0, 0))

    def kernel(lens_ref, me_ref, *refs):
        attention_kernel(lens_ref, *refs)

    return pl.pallas_call(
        kernel,
        grid_spec=pltpu.PrefetchScalarGridSpec(
            num_scalar_prefetch=2,
            grid=(rows // step,),
            in_specs=[wide, slim, slim, cache, cache, wide,
                      pl.BlockSpec((1, part), lambda i, n, m: (0, m[0]))],
            out_specs=[wide, wide],
        ),
        out_shape=[
            jax.ShapeDtypeStruct((rows, part), F32), jax.ShapeDtypeStruct((rows, part), BF16)
        ],
        compiler_params=pltpu.CompilerParams(vmem_limit_bytes=58 << 20),
        cost_estimate=pl.CostEstimate(
            flops=4 * rows * part * span,
            bytes_accessed=4 * rows * span * depth,
            transcendentals=rows * part,
        ),
        name="attention",
    )(lens, me, queries, new_key, new_value, keys, values, residual, gain)


def place_kernel(table_ref, rows_ref, out_ref):
    out_ref[...] = dot(table_ref[...], rows_ref[...]).astype(BF16)


def place_rows(table, rows):
    slots, part = table.shape[0], rows.shape[1]
    return pl.pallas_call(
        place_kernel,
        grid=(2,),
        in_specs=[
            pl.BlockSpec((slots // 2, table.shape[1]), lambda i: (i, 0)),
            pl.BlockSpec(rows.shape, lambda i: (0, 0)),
        ],
        out_specs=pl.BlockSpec((slots // 2, part), lambda i: (i, 0)),
        out_shape=jax.ShapeDtypeStruct((slots, part), BF16),
        cost_estimate=pl.CostEstimate(
            flops=2 * table.size * part, bytes_accessed=4 * slots * part, transcendentals=0
        ),
        name="place_rows",
    )(table, rows)


def pick_kernel(all_ref, *refs):
    for i, out_ref in enumerate(refs[-2:]):
        count = all_ref.shape[0] // 2
        out_ref[...] = all_ref[pl.ds(i * count, count)].reshape(out_ref.shape)


def pick(everything, expert, *after):
    devices, _, slots, part = everything.shape
    half = devices * slots // 2
    return pl.pallas_call(
        pick_kernel,
        grid=(1,),
        in_specs=[pl.BlockSpec((devices, 1, slots, part), lambda i: (0, expert, 0, 0))]
        + [ANY] * len(after),
        out_specs=[pl.BlockSpec((half, part), lambda i: (0, 0))] * 2,
        out_shape=[jax.ShapeDtypeStruct((half, part), everything.dtype)] * 2,
        cost_estimate=pl.CostEstimate(
            flops=0, bytes_accessed=8 * half * part, transcendentals=0
        ),
        name="pick",
    )(everything, *after)


def in_hbm(*arrays):
    return [pltpu.with_memory_space_constraint(array, pltpu.HBM) for array in arrays]


def exchange(for_right, for_across, for_left):
    return (
        lax.ppermute(for_right, "tp", RIGHT),
        lax.ppermute(for_left, "tp", LEFT),
        lax.ppermute(for_across, "tp", ACROSS),
    )


def columns(me_ref, turn, part):
    return pl.ds(pl.multiple_of(lax.rem(me_ref[0] + turn, N_TP) * part, part), part)


def project(x, cols, gate_ref, up_ref, inv_ref):
    dims = (((1,), (1,)), ((), ()))
    plain = x.astype(F32) * inv_ref[:, cols]
    return (
        lax.dot_general(x, gate_ref[0, :, cols], dims, preferred_element_type=F32),
        lax.dot_general(x, up_ref[0, :, cols], dims, preferred_element_type=F32),
        jnp.sum(plain * plain, axis=1, keepdims=True),
    )


def near_kernel(
    me_ref, own0, own1, left0, left1, right0, right1, gate_ref, up_ref, inv_ref,
    gate_out, up_out, sq_out,
):
    half, part = own0.shape
    for i, blocks in enumerate(((own0, left0, right0), (own1, left1, right1))):
        rows = pl.ds(i * half, half)
        total = None
        for block, turn in zip(blocks, (0, N_TP - 1, 1), strict=True):
            term = project(block[...], columns(me_ref, turn, part), gate_ref, up_ref, inv_ref)
            total = term if total is None else tuple(
                a + b for a, b in zip(total, term, strict=True)
            )
        gate_out[rows, :], up_out[rows, :] = total[0], total[1]
        sq_out[rows, :] = jnp.broadcast_to(total[2], (half, sq_out.shape[1]))


def far_kernel(me_ref, low, high, gate_in, up_in, sq_in, gate_ref, up_ref, inv_ref, out_ref):
    half, part = low.shape
    hidden = gate_in.shape[1]
    tails = []
    for i, block in enumerate((low, high)):
        rows = slice(i * half, (i + 1) * half)
        cols = pl.ds(0, part)
        gate, up, squares = project(block[...], cols, gate_ref, up_ref, inv_ref)
        scale = lax.rsqrt((sq_in[rows, :1] + squares) / (N_TP * part) + epsilon)
        gate, up = (gate_in[rows] + gate) * scale, (up_in[rows] + up) * scale
        value = gate / (1.0 + jnp.exp(-gate)) * up
        out_ref[rows, :] = value[:, :128].astype(BF16)
        tails.append(value[:, 128:hidden])
    out_ref[2 * half :, :] = jnp.concatenate(tails, axis=1).astype(BF16)


def near_project(me, blocks, w_gate, w_up, inv_gain, expert):
    rows, part = 2 * blocks[0].shape[0], blocks[0].shape[1]
    hidden, width = w_gate.shape[1:]

    def whole(shape):
        return pl.BlockSpec(shape, lambda i, m: (0,) * len(shape))

    weight = pl.BlockSpec((1, hidden, width), lambda i, m: (expert, 0, 0))
    return pl.pallas_call(
        near_kernel,
        grid_spec=pltpu.PrefetchScalarGridSpec(
            num_scalar_prefetch=1,
            grid=(1,),
            in_specs=[whole(blocks[0].shape)] * 6 + [weight, weight, whole((1, width))],
            out_specs=[whole((rows, hidden)), whole((rows, hidden)), whole((rows, 128))],
        ),
        out_shape=[jax.ShapeDtypeStruct((rows, hidden), F32)] * 2
        + [jax.ShapeDtypeStruct((rows, 128), F32)],
        compiler_params=pltpu.CompilerParams(vmem_limit_bytes=32 << 20),
        cost_estimate=pl.CostEstimate(
            flops=3 * rows * width * hidden,
            bytes_accessed=2 * rows * width + 4 * hidden * width,
            transcendentals=0,
        ),
        name="near_project",
    )(me, *blocks, w_gate, w_up, inv_gain)


def far_project(me, low, high, near, w_gate, w_up, inv_gain, expert, weight_us):
    half, part = low.shape
    hidden, width = w_gate.shape[1:]
    rows = 2 * half

    def whole(shape):
        return pl.BlockSpec(shape, lambda i, m: (0,) * len(shape))

    def across(m):
        return lax.rem(m[0] + 2, N_TP)

    weight = pl.BlockSpec((1, hidden, part), lambda i, m: (expert, 0, across(m)))
    packed = (rows + rows * (hidden - 128) // 128, 128)

    return pl.pallas_call(
        far_kernel,
        grid_spec=pltpu.PrefetchScalarGridSpec(
            num_scalar_prefetch=1,
            grid=(1,),
            in_specs=[whole(low.shape), whole(high.shape)]
            + [whole(a.shape) for a in near]
            + [weight, weight, pl.BlockSpec((1, part), lambda i, m: (0, across(m)))],
            out_specs=whole(packed),
        ),
        out_shape=jax.ShapeDtypeStruct(packed, BF16),
        compiler_params=BIG,
        cost_estimate=pl.CostEstimate(
            flops=int(weight_us * 1e9), bytes_accessed=8 * rows * part, transcendentals=0
        ),
        name="far_project",
    )(me, low, high, *near, w_gate, w_up, inv_gain)


def down_kernel(me_ref, h0, h1, h2, h3, w0, w1, w2, w3, out_ref, *plain):
    rows, hidden = plain[0].shape

    @pl.when(pl.program_id(0) == 0)
    def _():
        for packed, full in zip((h0, h1, h2, h3), plain, strict=True):
            tails = packed[rows:, :]
            full[:, :128] = packed[:rows, :]
            full[: rows // 2, 128:] = tails[:, : hidden - 128]
            full[rows // 2 :, 128:] = tails[:, hidden - 128 :]

    total = None
    for full, w_ref in zip(plain, (w0, w1, w2, w3), strict=True):
        term = dot(full[...], w_ref[0])
        total = term if total is None else total + term
    out_ref[...] = total.astype(out_ref.dtype)


def down_project(me, packed, w_down, moved, rows, expert, *after):
    _, hidden, part = moved[0].shape
    whole = pl.BlockSpec(packed[0].shape, lambda i, m: (0, 0))
    steps = 2
    piece = part // steps
    own = pl.BlockSpec((1, hidden, piece), lambda i, m: (expert, 0, m[0] * steps + i))
    other = pl.BlockSpec((1, hidden, piece), lambda i, m: (0, 0, i))

    def kernel(*refs):
        head = 1 + 2 * N_TP
        down_kernel(*refs[:head], *refs[head + len(after) :])

    return pl.pallas_call(
        kernel,
        grid_spec=pltpu.PrefetchScalarGridSpec(
            num_scalar_prefetch=1,
            grid=(steps,),
            in_specs=[whole] * N_TP + [own] + [other] * (N_TP - 1) + [ANY] * len(after),
            out_specs=pl.BlockSpec((rows, piece), lambda i, m: (0, i)),
            scratch_shapes=[pltpu.VMEM((rows, hidden), BF16)] * N_TP,
        ),
        out_shape=pltpu.HBM((rows, part), BF16),
        compiler_params=BIG,
        cost_estimate=pl.CostEstimate(
            flops=8 * rows * hidden * part,
            bytes_accessed=8 * rows * hidden + 8 * hidden * part + 2 * rows * part,
            transcendentals=0,
        ),
        name="down_project",
    )(me, *packed, w_down, *moved, *after)


def mix_kernel(total_ref, hi_ref, lo_ref, back_ref, out_ref):
    back = back_ref[...]
    total = total_ref[...].astype(F32)
    for weight in (hi_ref, lo_ref):
        total = total + dot(weight[...], back)
    out_ref[...] = total.astype(out_ref.dtype)


def mix_in(total, hi, lo, back, dtype):
    rows, part = total.shape
    steps = 2
    column = pl.BlockSpec((rows, part // steps), lambda i: (0, i))
    weight = pl.BlockSpec(hi.shape, lambda i: (0, 0))
    return pl.pallas_call(
        mix_kernel,
        grid=(steps,),
        in_specs=[column, weight, weight,
                  pl.BlockSpec((back.shape[0], part // steps), lambda i: (0, i))],
        out_specs=column,
        out_shape=jax.ShapeDtypeStruct((rows, part), dtype),
        cost_estimate=pl.CostEstimate(
            flops=4 * hi.size * part, bytes_accessed=2 * back.size, transcendentals=0
        ),
        name="mix_in",
    )(total, hi, lo, back)


def body(
    queries, new_key, new_value, key_cache, value_cache, cache_len, residual,
    norm_gain, expert_ids, gate_probs, w_gate, w_up, w_down,
):
    rows, part = residual.shape
    group = ("side", "grp")
    devices = lax.axis_size("side") * lax.axis_size("grp")
    slots = devices * SLOTS
    me = lax.axis_index("tp").astype(jnp.int32).reshape(1)
    hi0, hi1, lo0, lo1, table = route(expert_ids.T, gate_probs.T, devices)
    blocks = split_columns(me, w_down)
    gain = norm_gain.reshape(1, -1)
    inv_gain = 1.0 / gain
    summed, scaled = attention(
        cache_len, me, queries, new_key, new_value, key_cache, value_cache, residual, gain
    )
    swap = functools.partial(
        lax.all_to_all, axis_name=group, split_axis=0, concat_axis=0, tiled=True
    )
    moved = [exchange(*blocks[: N_TP - 1]), exchange(*blocks[N_TP - 1 :])]
    moved[0] = in_hbm(*moved[0])
    w_gate, w_up = in_hbm(w_gate, w_up)
    arrived = swap(place_rows(table, scaled).reshape(devices, EXP_DEV, SLOTS, part))
    total = summed
    for expert, hi, lo in ((0, hi0, lo0), (1, hi1, lo1)):
        own = pick(arrived, expert, *moved[0], *moved[1])
        left = [lax.ppermute(half, "tp", RIGHT) for half in own]
        right = [lax.ppermute(half, "tp", LEFT) for half in own]
        low = lax.ppermute(left[0], "tp", RIGHT)
        high = lax.ppermute(right[1], "tp", LEFT)
        sums = near_project(me, (*own, *left, *right), w_gate, w_up, inv_gain, expert)
        packed = far_project(
            me, low, high, sums, w_gate, w_up, inv_gain, expert, FAR_WEIGHT[expert]
        )
        packed = packed, *exchange(packed, packed, packed)
        produced = down_project(me, packed, w_down, moved[expert], slots, expert)
        back = swap(produced.reshape(devices, SLOTS, part)).reshape(slots, part)
        total = mix_in(total, hi.T, lo.T, back, F32 if expert == 0 else BF16)
    return total


def solution(mesh):
    in_specs = (
        P(("side", "grp"), "tp"),
        P(("side", "grp"), "tp"),
        P(("side", "grp"), "tp"),
        P(("side", "grp"), None, "tp"),
        P(("side", "grp"), None, "tp"),
        P(("side", "grp")),
        P(("side", "grp"), "tp"),
        P(),
        P(("side", "grp"), None),
        P(("side", "grp"), None),
        P(("side", "grp"), "tp", None),
        P(("side", "grp"), "tp", None),
        P(("side", "grp"), "tp", None),
    )
    out_specs = P(("side", "grp"), "tp")
    return jax.shard_map(body, mesh=mesh, in_specs=in_specs, out_specs=out_specs, check_vma=False)
```

time: 419 us -> 216 us (0.52)
  blocking collectives: 211 us -> 0 us
  starting transfers between devices: 11.1 us -> 59.2 us
  Pallas kernels: 0 us -> 42.7 us
  matrix products: 26.9 us -> 0 us
  waiting for transfers between devices: 130 us -> 107 us
  between operations: 13.6 us -> 0.17 us
  local copies, waits for them, and re-layouts: 18.7 us -> 6.02 us
  other arithmetic: 6.66 us -> 0.01 us
    all_to_all x1 -> x0, blocking collectives: 199 us -> none  [body(): lax.all_to_all(outgoing, ('side', 'grp'), split_axis=0, concat_axis=0, ti...]
    reduce_scatter x1 -> x0, waiting for transfers between devices: 80.2 us -> none  [expert_work(): lax.psum_scatter(rounded.astype(jnp.bfloat16), 'tp', scatter_dimension=3,...]
    ppermute x0 -> x24, waiting for transfers between devices: none -> 70.5 us  [the longest x4 24.6 us: exchange(): lax.ppermute(for_across, 'tp', ACROSS)]
    pallas_call x0 -> x14, Pallas kernels: none -> 42.7 us  [the longest x2 9.79 us: near_project(): pl.pallas_call(near_kernel, grid_spec=pltpu.PrefetchScalarGridSpec(num_sc...]
    ppermute x0 -> x24, starting transfers between devices: none -> 30.7 us  [the longest x4 8.08 us: exchange(): lax.ppermute(for_across, 'tp', ACROSS)]
    dot_general x6 -> x0, matrix products: 26.9 us -> none  [the longest x1 13.7 us: expert_work(): jnp.einsum('sxcf,xfd->sxcd', activation, w_down, preferred_element_type=j...]
    all_to_all x1 -> x3, starting transfers between devices: 11.1 us -> 28.5 us  [the longest x2 14.8 us: body(): back = swap(produced.reshape(devices, SLOTS, part)).reshape(slots, part)]
    all_to_all x1 -> x3, waiting for transfers between devices: 49.9 us -> 36.6 us  [the longest x2 24.8 us: body(): back = swap(produced.reshape(devices, SLOTS, part)).reshape(slots, part)]
  transfers between devices with their start and end apart: 2 -> 27, of which waited for: 2 -> 18; matrix products, arithmetic and copies ran while one was open for 0% -> 1% of each run, Pallas kernels for 0% -> 13%
where the time goes in v2:
time: 216 us; the launch traced here: 215 us
  waiting for transfers between devices  107 us (50%)
  starting transfers between devices  59.2 us (27%)
  Pallas kernels  42.7 us (20%)
  local copies, waits for them, and re-layouts  6.02 us (3%)
    all_to_all x2, waiting for transfers between devices, body(): back = swap(produced.reshape(devices, SLOTS, part)).reshape(slots, part)  24.8 us
    ppermute x4, waiting for transfers between devices, exchange(): lax.ppermute(for_across, 'tp', ACROSS)  24.6 us
    ppermute x4, waiting for transfers between devices, body(): left = [lax.ppermute(half, 'tp', RIGHT) for half in own]  16.1 us
    all_to_all x2, starting transfers between devices, body(): back = swap(produced.reshape(devices, SLOTS, part)).reshape(slots, part)  14.8 us
    all_to_all x1, starting transfers between devices, body(): swap(place_rows(table, scaled).reshape(devices, EXP_DEV, SLOTS, part))  13.7 us
    ppermute x4, waiting for transfers between devices, exchange(): lax.ppermute(for_right, 'tp', RIGHT)  12.1 us
    all_to_all x1, waiting for transfers between devices, body(): swap(place_rows(table, scaled).reshape(devices, EXP_DEV, SLOTS, part))  11.8 us
    pallas_call x2, Pallas kernels, near_project(): pl.pallas_call(near_kernel, grid_spec=pltpu.PrefetchScalarGridSpec(num_sc...  9.79 us
  transfers between devices with their start and end apart: 27, of which 18 were waited for; matrix products, arithmetic and copies ran while one was open for 1% of the time, Pallas kernels for 13%

profile of v2, /device:TPU:1, one launch (start us, length us, event | category | flops | bytes accessed | tf_op | source)
XLA Modules:
  0.0 215.1 jit_solution(50028413771574200)
XLA Ops:
  0.0 2.2 %route.1 = (bf16[512,64]{1,0:T(8,128)(2,1)}, bf16[512,64]{1,0:T(8,128)(2,1)}, bf16[512,64]{1,0:T(8,128)(2,1)}, bf16[512,64]{1,0:T(8,128)(2,1)}, bf16[1024,64]{1,0:T(8,128)(2,1)}) custom-call(s32[8,64]{1,0:T(8,128)} %bitcast.27, f32[8,64]{1,0:T(8,128)} %bitcast.28), custom_call_target="tpu_custom_call" | custom-call | flops 524288 | tf_op jit(solution)/shard_map/route/pallas_call | solution.py:73
  2.2 6.0 %attention.1 = (f32[64,1024]{1,0:T(8,128)}, bf16[64,1024]{1,0:T(8,128)(2,1)}) custom-call(s32[64]{0:T(128)} %lens_ref.1, s32[1]{0:T(128)} %bitcast.me_ref.refs_0_, bf16[64,1024]{1,0:T(8,128)(2,1)} %refs_0_.1, bf16[64,128]{1,0:T(8,128)(2,1)} %refs_1_.1, bf16[64,128]{1,0:T(8,128)(2,1)} %refs_2_.1, bf16[64,128,128]{2,1,0:T(8,128)(2,1)} %refs_3_.1, ...), custom_call_target="tpu_custom_call" | custom-call | flops 33554432 | bytes 4194304 | tf_op jit(solution)/shard_map/attention/pallas_call | solution.py:166
  8.3 2.8 %place_rows.1 = bf16[1024,1024]{1,0:T(8,128)(2,1)} custom-call(bf16[1024,64]{1,0:T(8,128)(2,1)} %get-tuple-element.31.table_ref, bf16[64,1024]{1,0:T(8,128)(2,1)} %get-tuple-element.32.rows_ref), custom_call_target="tpu_custom_call" | custom-call | flops 134217728 | bytes 4194304 | tf_op jit(solution)/shard_map/place_rows/pallas_call | solution.py:194
  11.1 13.7 %all-to-all-start = ((bf16[64,2,8,1024]{3,2,1,0:T(8,128)(2,1)}), bf16[64,2,8,1024]{3,2,1,0:T(8,128)(2,1)}, u32[]{:S(2)}, u32[]{:S(2)}) async-start(bf16[64,2,8,1024]{3,2,1,0:T(8,128)(2,1)} %bitcast.18), calls=%async_computation | async-start | bytes 4194304 | tf_op jit(solution)/shard_map/all_to_all | solution.py:452
  24.8 0.4 split_columns.1
  25.2 1.3 collective-permute-start
  26.5 1.5 collective-permute-start.1
  28.0 1.5 collective-permute-start.2
  29.5 0.4 collective-permute-start.3
  29.9 2.3 %collective-permute-start.4 = (bf16[1,192,1024]{2,1,0:T(8,128)(2,1)S(1)}, bf16[1,192,1024]{2,1,0:T(8,128)(2,1)}, u32[]{:S(2)}, u32[]{:S(2)}) collective-permute-start(bf16[1,192,1024]{2,1,0:T(8,128)(2,1)S(1)} %get-tuple-element.37), channel_id=1, source_target_pairs={{0,3},{1,0},{2,1},{3,2},{4,7},{5,4},{6,5},{7,6},{8,11},{9,8},{10,9... | collective-permute-start | bytes 1179656 | tf_op jit(solution)/shard_map/ppermute | solution.py:240
  32.2 4.7 %collective-permute-done.refs_0_.refs_6_ = bf16[1,192,1024]{2,1,0:T(8,128)(2,1)S(1)} collective-permute-done((bf16[1,192,1024]{2,1,0:T(8,128)(2,1)S(1)}, bf16[1,192,1024]{2,1,0:T(8,128)(2,1)S(1)}, u32[]{:S(2)}, u32[]{:S(2)}) %collective-permute-start) | collective-permute-done | bytes 393248 | tf_op jit(solution)/shard_map/ppermute | solution.py:239
  36.9 1.5 collective-permute-start.5
  38.4 8.0 %collective-permute-done.2.refs_2_.refs_8_ = bf16[1,192,1024]{2,1,0:T(8,128)(2,1)S(1)} collective-permute-done((bf16[1,192,1024]{2,1,0:T(8,128)(2,1)S(1)}, bf16[1,192,1024]{2,1,0:T(8,128)(2,1)S(1)}, u32[]{:S(2)}, u32[]{:S(2)}) %collective-permute-start.2) | collective-permute-done | bytes 393248 | tf_op jit(solution)/shard_map/ppermute | solution.py:241
  46.4 7.3 %collective-permute-done.3.refs_3_.refs_6_ = bf16[1,192,1024]{2,1,0:T(8,128)(2,1)S(1)} collective-permute-done((bf16[1,192,1024]{2,1,0:T(8,128)(2,1)S(1)}, bf16[1,192,1024]{2,1,0:T(8,128)(2,1)S(1)}, u32[]{:S(2)}, u32[]{:S(2)}) %collective-permute-start.3) | collective-permute-done | bytes 393248 | tf_op jit(solution)/shard_map/ppermute | solution.py:239
  53.8 9.5 %collective-permute-done.5.refs_5_.refs_8_ = bf16[1,192,1024]{2,1,0:T(8,128)(2,1)} collective-permute-done((bf16[1,192,1024]{2,1,0:T(8,128)(2,1)S(1)}, bf16[1,192,1024]{2,1,0:T(8,128)(2,1)}, u32[]{:S(2)}, u32[]{:S(2)}) %collective-permute-start.5) | collective-permute-done | bytes 393248 | tf_op jit(solution)/shard_map/ppermute | solution.py:241
  63.3 11.8 %all-to-all-done.all_ref = bf16[64,2,8,1024]{3,2,1,0:T(8,128)(2,1)} async-done(((bf16[64,2,8,1024]{3,2,1,0:T(8,128)(2,1)}), bf16[64,2,8,1024]{3,2,1,0:T(8,128)(2,1)}, u32[]{:S(2)}, u32[]{:S(2)}) %all-to-all-start) | async-done | bytes 2097184 | tf_op jit(solution)/shard_map/all_to_all | solution.py:452
  75.0 2.3 %pick.2 = (bf16[256,1024]{1,0:T(8,128)(2,1)}, bf16[256,1024]{1,0:T(8,128)(2,1)}) custom-call(bf16[64,2,8,1024]{3,2,1,0:T(8,128)(2,1)} %all-to-all-done.all_ref, bf16[1,192,1024]{2,1,0:T(8,128)(2,1)} %copy-done.6, bf16[1,192,1024]{2,1,0:T(8,128)(2,1)} %copy-done.7, bf16[1,192,1024]{2,1,0:T(8,128)(2,1)} %copy-done.8, bf16[1,192,1024]{2,1,0:T(8,128)(2,1)} %copy-done.1, ...), custom_call_target="tpu_custom_call" | custom-call | bytes 2097152 | tf_op jit(solution)/shard_map/pick/pallas_call | solution.py:219
  77.3 1.2 collective-permute-start.6
  78.5 1.5 collective-permute-start.8
  80.0 1.3 collective-permute-start.11
  81.3 0.1 collective-permute-start.10
  81.4 11.2 %collective-permute-done.6.left0 = bf16[256,1024]{1,0:T(8,128)(2,1)} collective-permute-done((bf16[256,1024]{1,0:T(8,128)(2,1)}, bf16[256,1024]{1,0:T(8,128)(2,1)}, u32[]{:S(2)}, u32[]{:S(2)}) %collective-permute-start.6) | collective-permute-done | bytes 524320 | tf_op jit(solution)/shard_map/ppermute | solution.py:456
  92.7 2.7 %collective-permute-start.9 = (bf16[256,1024]{1,0:T(8,128)(2,1)}, bf16[256,1024]{1,0:T(8,128)(2,1)}, u32[]{:S(2)}, u32[]{:S(2)}) collective-permute-start(bf16[256,1024]{1,0:T(8,128)(2,1)} %collective-permute-done.8.right1), channel_id=1, source_target_pairs={{0,3},{1,0},{2,1},{3,2},{4,7},{5,4},{6,5},{7,6},{8,11},{9,8},{10,9... | collective-permute-start | bytes 1572872 | tf_op jit(solution)/shard_map/ppermute | solution.py:459
  95.3 2.2 %pick.3 = (bf16[256,1024]{1,0:T(8,128)(2,1)}, bf16[256,1024]{1,0:T(8,128)(2,1)}) custom-call(bf16[64,2,8,1024]{3,2,1,0:T(8,128)(2,1)} %all-to-all-done.all_ref, bf16[1,192,1024]{2,1,0:T(8,128)(2,1)} %copy-done.6, bf16[1,192,1024]{2,1,0:T(8,128)(2,1)} %copy-done.7, bf16[1,192,1024]{2,1,0:T(8,128)(2,1)} %copy-done.8, bf16[1,192,1024]{2,1,0:T(8,128)(2,1)} %copy-done.1, ...), custom_call_target="tpu_custom_call" | custom-call | bytes 2097152 | tf_op jit(solution)/shard_map/pick/pallas_call | solution.py:219
  97.6 6.1 %collective-permute-done.11.right0 = bf16[256,1024]{1,0:T(8,128)(2,1)} collective-permute-done((bf16[256,1024]{1,0:T(8,128)(2,1)}, bf16[256,1024]{1,0:T(8,128)(2,1)}, u32[]{:S(2)}, u32[]{:S(2)}) %collective-permute-start.11) | collective-permute-done | bytes 524320 | tf_op jit(solution)/shard_map/ppermute | solution.py:457
  103.7 2.7 %collective-permute-start.17 = (bf16[256,1024]{1,0:T(8,128)(2,1)}, bf16[256,1024]{1,0:T(8,128)(2,1)}, u32[]{:S(2)}, u32[]{:S(2)}) collective-permute-start(bf16[256,1024]{1,0:T(8,128)(2,1)} %get-tuple-element.47.own1), channel_id=1, source_target_pairs={{0,3},{1,0},{2,1},{3,2},{4,7},{5,4},{6,5},{7,6},{8,11},{9,8},{10,9... | collective-permute-start | bytes 1572872 | tf_op jit(solution)/shard_map/ppermute | solution.py:457
  106.4 1.0 copy-done.3
  107.4 1.0 copy-done.4
  108.5 4.7 %near_project.2 = (f32[512,192]{1,0:T(8,128)S(1)}, f32[512,192]{1,0:T(8,128)S(1)}, f32[512,128]{1,0:T(8,128)S(1)}) custom-call(s32[1]{0:T(128)} %bitcast.me_ref.refs_0_, bf16[256,1024]{1,0:T(8,128)(2,1)S(1)} %copy-done.3, bf16[256,1024]{1,0:T(8,128)(2,1)S(1)} %copy-done.4, bf16[256,1024]{1,0:T(8,128)(2,1)} %collective-permute-done.6.left0, ...), custom_call_target="tpu_custom_call" | custom-call | flops 1207959552 | bytes 7340032 | tf_op jit(solution)/shard_map/near_project/pallas_call | solution.py:300
  113.2 1.9 collective-permute-done.7.low
  115.1 2.5 %far_project.2.refs_1_ = bf16[768,128]{1,0:T(8,128)(2,1)S(1)} custom-call(s32[1]{0:T(128)} %bitcast.me_ref.refs_0_, bf16[256,1024]{1,0:T(8,128)(2,1)} %collective-permute-done.7.low, bf16[256,1024]{1,0:T(8,128)(2,1)} %collective-permute-done.9.high, f32[512,192]{1,0:T(8,128)S(1)} %get-tuple-element.41.gate_in, f32[512,192]{1,0:T(8,128)S(1)} %get-tuple-element.42.up_in, ...), custom_call_target="tpu_custom_call" | custom-call | flops 1000000000 | bytes 4194304 | tf_op jit(solution)/shard_map/far_project/pallas_call | solution.py:334
  117.6 2.4 %collective-permute-start.14 = (bf16[768,128]{1,0:T(8,128)(2,1)S(1)}, bf16[768,128]{1,0:T(8,128)(2,1)S(1)}, u32[]{:S(2)}, u32[]{:S(2)}) collective-permute-start(bf16[768,128]{1,0:T(8,128)(2,1)S(1)} %far_project.2.refs_1_), channel_id=1, source_target_pairs={{0,2},{1,3},{2,0},{3,1},{4,6},{5,7},{6,4},{7,5},{8,10},{9,11},{10,... | collective-permute-start | bytes 589832 | tf_op jit(solution)/shard_map/ppermute | solution.py:241
  120.0 1.1 collective-permute-start.13
  121.1 0.4 collective-permute-start.12
  121.5 4.9 %collective-permute-done.15.left0 = bf16[256,1024]{1,0:T(8,128)(2,1)} collective-permute-done((bf16[256,1024]{1,0:T(8,128)(2,1)}, bf16[256,1024]{1,0:T(8,128)(2,1)}, u32[]{:S(2)}, u32[]{:S(2)}) %collective-permute-start.15) | collective-permute-done | bytes 524320 | tf_op jit(solution)/shard_map/ppermute | solution.py:456
  126.4 1.3 collective-permute-start.20
  127.7 0.1 collective-permute-start.19
  127.8 3.7 %collective-permute-done.14.refs_4_ = bf16[768,128]{1,0:T(8,128)(2,1)S(1)} collective-permute-done((bf16[768,128]{1,0:T(8,128)(2,1)S(1)}, bf16[768,128]{1,0:T(8,128)(2,1)S(1)}, u32[]{:S(2)}, u32[]{:S(2)}) %collective-permute-start.14) | collective-permute-done | bytes 196640 | tf_op jit(solution)/shard_map/ppermute | solution.py:241
  131.6 0.7 collective-permute-start.16
  132.2 2.3 %collective-permute-done.13.refs_3_ = bf16[768,128]{1,0:T(8,128)(2,1)S(1)} collective-permute-done((bf16[768,128]{1,0:T(8,128)(2,1)S(1)}, bf16[768,128]{1,0:T(8,128)(2,1)S(1)}, u32[]{:S(2)}, u32[]{:S(2)}) %collective-permute-start.13) | collective-permute-done | bytes 196640 | tf_op jit(solution)/shard_map/ppermute | solution.py:240
  134.5 2.6 %collective-permute-start.18 = (bf16[256,1024]{1,0:T(8,128)(2,1)}, bf16[256,1024]{1,0:T(8,128)(2,1)}, u32[]{:S(2)}, u32[]{:S(2)}) collective-permute-start(bf16[256,1024]{1,0:T(8,128)(2,1)} %collective-permute-done.17.right1), channel_id=1, source_target_pairs={{0,3},{1,0},{2,1},{3,2},{4,7},{5,4},{6,5},{7,6},{8,11},{9,8},{10,9... | collective-permute-start | bytes 1572872 | tf_op jit(solution)/shard_map/ppermute | solution.py:459
  137.2 3.6 %down_project.2 = bf16[512,1024]{1,0:T(8,128)(2,1)} custom-call(s32[1]{0:T(128)} %bitcast.me_ref.refs_0_, bf16[768,128]{1,0:T(8,128)(2,1)S(1)} %far_project.2.refs_1_, bf16[768,128]{1,0:T(8,128)(2,1)S(1)} %collective-permute-done.12.refs_2_, bf16[768,128]{1,0:T(8,128)(2,1)S(1)} %collective-permute-done.13.refs_3_, ...), custom_call_target="tpu_custom_call" | custom-call | flops 805306368 | bytes 3407872 | tf_op jit(solution)/shard_map/down_project/pallas_call | solution.py:383
  140.8 8.4 %all-to-all-start.1 = ((bf16[64,8,1024]{2,1,0:T(8,128)(2,1)}), bf16[64,8,1024]{2,1,0:T(8,128)(2,1)}, u32[]{:S(2)}, u32[]{:S(2)}) async-start(bf16[64,8,1024]{2,1,0:T(8,128)(2,1)} %bitcast.19), calls=%async_computation.1 | async-start | bytes 2097152 | tf_op jit(solution)/shard_map/all_to_all | solution.py:466
  149.2 5.1 %near_project.3 = (f32[512,192]{1,0:T(8,128)S(1)}, f32[512,192]{1,0:T(8,128)S(1)}, f32[512,128]{1,0:T(8,128)S(1)}) custom-call(s32[1]{0:T(128)} %bitcast.me_ref.refs_0_, bf16[256,1024]{1,0:T(8,128)(2,1)} %get-tuple-element.46.own0, bf16[256,1024]{1,0:T(8,128)(2,1)} %get-tuple-element.47.own1, bf16[256,1024]{1,0:T(8,128)(2,1)} %collective-permute-done.15.left0, ...), custom_call_target="tpu_custom_call" | custom-call | flops 1207959552 | bytes 7340032 | tf_op jit(solution)/shard_map/near_project/pallas_call | solution.py:300
  154.2 2.2 %collective-permute-done.16.low = bf16[256,1024]{1,0:T(8,128)(2,1)} collective-permute-done((bf16[256,1024]{1,0:T(8,128)(2,1)}, bf16[256,1024]{1,0:T(8,128)(2,1)}, u32[]{:S(2)}, u32[]{:S(2)}) %collective-permute-start.16) | collective-permute-done | bytes 524320 | tf_op jit(solution)/shard_map/ppermute | solution.py:458
  156.4 0.7 collective-permute-done.18.high
  157.1 2.5 %far_project.3.refs_1_ = bf16[768,128]{1,0:T(8,128)(2,1)S(1)} custom-call(s32[1]{0:T(128)} %bitcast.me_ref.refs_0_, bf16[256,1024]{1,0:T(8,128)(2,1)} %collective-permute-done.16.low, bf16[256,1024]{1,0:T(8,128)(2,1)} %collective-permute-done.18.high, f32[512,192]{1,0:T(8,128)S(1)} %get-tuple-element.48.gate_in, f32[512,192]{1,0:T(8,128)S(1)} %get-tuple-element.49.up_in, ...), custom_call_target="tpu_custom_call" | custom-call | flops 14000000000 | bytes 4194304 | tf_op jit(solution)/shard_map/far_project/pallas_call | solution.py:334
  159.6 2.6 %collective-permute-start.23 = (bf16[768,128]{1,0:T(8,128)(2,1)S(1)}, bf16[768,128]{1,0:T(8,128)(2,1)S(1)}, u32[]{:S(2)}, u32[]{:S(2)}) collective-permute-start(bf16[768,128]{1,0:T(8,128)(2,1)S(1)} %far_project.3.refs_1_), channel_id=1, source_target_pairs={{0,2},{1,3},{2,0},{3,1},{4,6},{5,7},{6,4},{7,5},{8,10},{9,11},{10,... | collective-permute-start | bytes 589832 | tf_op jit(solution)/shard_map/ppermute | solution.py:241
  162.3 1.0 collective-permute-start.22
  163.3 0.4 collective-permute-start.21
  163.7 3.4 %collective-permute-done.23.refs_4_ = bf16[768,128]{1,0:T(8,128)(2,1)S(1)} collective-permute-done((bf16[768,128]{1,0:T(8,128)(2,1)S(1)}, bf16[768,128]{1,0:T(8,128)(2,1)S(1)}, u32[]{:S(2)}, u32[]{:S(2)}) %collective-permute-start.23) | collective-permute-done | bytes 196640 | tf_op jit(solution)/shard_map/ppermute | solution.py:241
  167.1 4.5 %collective-permute-done.22.refs_3_ = bf16[768,128]{1,0:T(8,128)(2,1)S(1)} collective-permute-done((bf16[768,128]{1,0:T(8,128)(2,1)S(1)}, bf16[768,128]{1,0:T(8,128)(2,1)S(1)}, u32[]{:S(2)}, u32[]{:S(2)}) %collective-permute-start.22) | collective-permute-done | bytes 196640 | tf_op jit(solution)/shard_map/ppermute | solution.py:240
  171.6 0.1 collective-permute-done.21.refs_2_
  171.7 3.5 %down_project.3 = bf16[512,1024]{1,0:T(8,128)(2,1)} custom-call(s32[1]{0:T(128)} %bitcast.me_ref.refs_0_, bf16[768,128]{1,0:T(8,128)(2,1)S(1)} %far_project.3.refs_1_, bf16[768,128]{1,0:T(8,128)(2,1)S(1)} %collective-permute-done.21.refs_2_, bf16[768,128]{1,0:T(8,128)(2,1)S(1)} %collective-permute-done.22.refs_3_, ...), custom_call_target="tpu_custom_call" | custom-call | flops 805306368 | bytes 3407872 | tf_op jit(solution)/shard_map/down_project/pallas_call | solution.py:383
  175.2 2.0 all-to-all-done.1
  177.2 6.4 %all-to-all-start.2 = ((bf16[64,8,1024]{2,1,0:T(8,128)(2,1)}), bf16[64,8,1024]{2,1,0:T(8,128)(2,1)S(1)}, u32[]{:S(2)}, u32[]{:S(2)}) async-start(bf16[64,8,1024]{2,1,0:T(8,128)(2,1)} %bitcast.20), calls=%async_computation.2 | async-start | bytes 2097152 | tf_op jit(solution)/shard_map/all_to_all | solution.py:466
  183.6 0.7 copy.14
  184.3 0.7 copy.15
  185.1 0.7 copy.16
  185.8 0.7 copy.17
  186.5 2.4 %mix_in.2.total_ref = f32[64,1024]{1,0:T(8,128)} custom-call(f32[64,1024]{1,0:T(8,128)} %get-tuple-element.28.total_ref, bf16[64,512]{1,0:T(8,128)(2,1)} %bitcast.24, bf16[64,512]{1,0:T(8,128)(2,1)} %bitcast.25, bf16[512,1024]{1,0:T(8,128)(2,1)} %bitcast.9.back_ref), custom_call_target="tpu_custom_call" | custom-call | flops 134217728 | bytes 1048576 | tf_op jit(solution)/shard_map/mix_in/pallas_call | solution.py:416
  188.9 22.8 %all-to-all-done.2 = bf16[64,8,1024]{2,1,0:T(8,128)(2,1)S(1)} async-done(((bf16[64,8,1024]{2,1,0:T(8,128)(2,1)}), bf16[64,8,1024]{2,1,0:T(8,128)(2,1)S(1)}, u32[]{:S(2)}, u32[]{:S(2)}) %all-to-all-start.2) | async-done | bytes 1048608 | tf_op jit(solution)/shard_map/all_to_all | solution.py:466
  211.7 1.0 copy-done.5
  212.7 2.4 %mix_in.3 = bf16[64,1024]{1,0:T(8,128)(2,1)} custom-call(f32[64,1024]{1,0:T(8,128)} %mix_in.2.total_ref, bf16[64,512]{1,0:T(8,128)(2,1)} %bitcast.22, bf16[64,512]{1,0:T(8,128)(2,1)} %bitcast.23, bf16[512,1024]{1,0:T(8,128)(2,1)} %bitcast.21), custom_call_target="tpu_custom_call" | custom-call | flops 134217728 | bytes 1048576 | tf_op jit(solution)/shard_map/mix_in/pallas_call | solution.py:416
  (37 shorter events, 0.1 us)
Async XLA Ops:
  11.1 13.7 %copy-start = (bf16[2,192,4096]{2,1,0:T(8,128)(2,1)S(1)}, bf16[2,192,4096]{2,1,0:T(8,128)(2,1)}, u32[]{:S(2)}) copy-start(bf16[2,192,4096]{2,1,0:T(8,128)(2,1)} %refs_5_.5) | copy-start | bytes 9437188
  11.1 64.0 %all-to-all-start = ((bf16[64,2,8,1024]{3,2,1,0:T(8,128)(2,1)}), bf16[64,2,8,1024]{3,2,1,0:T(8,128)(2,1)}, u32[]{:S(2)}, u32[]{:S(2)}) async-start(bf16[64,2,8,1024]{3,2,1,0:T(8,128)(2,1)} %bitcast.18), calls=%async_computation | async-start | bytes 4194304 | tf_op jit(solution)/shard_map/all_to_all | solution.py:452
  25.2 11.7 %collective-permute-start = (bf16[1,192,1024]{2,1,0:T(8,128)(2,1)S(1)}, bf16[1,192,1024]{2,1,0:T(8,128)(2,1)S(1)}, u32[]{:S(2)}, u32[]{:S(2)}) collective-permute-start(bf16[1,192,1024]{2,1,0:T(8,128)(2,1)S(1)} %get-tuple-element.33), channel_id=1, source_target_pairs={{0,1},{1,2},{2,3},{3,0},{4,5},{5,6},{6,7},{7,4},{8,9},{9,10},{10,1... | collective-permute-start | bytes 1179656 | tf_op jit(solution)/shard_map/ppermute | solution.py:239
  26.5 11.9 %collective-permute-start.1 = (bf16[1,192,1024]{2,1,0:T(8,128)(2,1)S(1)}, bf16[1,192,1024]{2,1,0:T(8,128)(2,1)S(1)}, u32[]{:S(2)}, u32[]{:S(2)}) collective-permute-start(bf16[1,192,1024]{2,1,0:T(8,128)(2,1)S(1)} %get-tuple-element.34), channel_id=1, source_target_pairs={{0,3},{1,0},{2,1},{3,2},{4,7},{5,4},{6,5},{7,6},{8,11},{9,8},{10,9... | collective-permute-start | bytes 1179656 | tf_op jit(solution)/shard_map/ppermute | solution.py:240
  28.0 18.4 %collective-permute-start.2 = (bf16[1,192,1024]{2,1,0:T(8,128)(2,1)S(1)}, bf16[1,192,1024]{2,1,0:T(8,128)(2,1)S(1)}, u32[]{:S(2)}, u32[]{:S(2)}) collective-permute-start(bf16[1,192,1024]{2,1,0:T(8,128)(2,1)S(1)} %get-tuple-element.35), channel_id=1, source_target_pairs={{0,2},{1,3},{2,0},{3,1},{4,6},{5,7},{6,4},{7,5},{8,10},{9,11},{10,... | collective-permute-start | bytes 1179656 | tf_op jit(solution)/shard_map/ppermute | solution.py:241
  29.5 24.2 %collective-permute-start.3 = (bf16[1,192,1024]{2,1,0:T(8,128)(2,1)S(1)}, bf16[1,192,1024]{2,1,0:T(8,128)(2,1)S(1)}, u32[]{:S(2)}, u32[]{:S(2)}) collective-permute-start(bf16[1,192,1024]{2,1,0:T(8,128)(2,1)S(1)} %get-tuple-element.36), channel_id=1, source_target_pairs={{0,1},{1,2},{2,3},{3,0},{4,5},{5,6},{6,7},{7,4},{8,9},{9,10},{10,1... | collective-permute-start | bytes 1179656 | tf_op jit(solution)/shard_map/ppermute | solution.py:239
  29.9 23.8 %collective-permute-start.4 = (bf16[1,192,1024]{2,1,0:T(8,128)(2,1)S(1)}, bf16[1,192,1024]{2,1,0:T(8,128)(2,1)}, u32[]{:S(2)}, u32[]{:S(2)}) collective-permute-start(bf16[1,192,1024]{2,1,0:T(8,128)(2,1)S(1)} %get-tuple-element.37), channel_id=1, source_target_pairs={{0,3},{1,0},{2,1},{3,2},{4,7},{5,4},{6,5},{7,6},{8,11},{9,8},{10,9... | collective-permute-start | bytes 1179656 | tf_op jit(solution)/shard_map/ppermute | solution.py:240
  36.9 16.9 %copy-start.6 = (bf16[1,192,1024]{2,1,0:T(8,128)(2,1)}, bf16[1,192,1024]{2,1,0:T(8,128)(2,1)S(1)}, u32[]{:S(2)}) copy-start(bf16[1,192,1024]{2,1,0:T(8,128)(2,1)S(1)} %collective-permute-done.refs_0_.refs_6_) | copy-start | bytes 1179652
  36.9 26.4 %collective-permute-start.5 = (bf16[1,192,1024]{2,1,0:T(8,128)(2,1)S(1)}, bf16[1,192,1024]{2,1,0:T(8,128)(2,1)}, u32[]{:S(2)}, u32[]{:S(2)}) collective-permute-start(bf16[1,192,1024]{2,1,0:T(8,128)(2,1)S(1)} %get-tuple-element.38), channel_id=1, source_target_pairs={{0,2},{1,3},{2,0},{3,1},{4,6},{5,7},{6,4},{7,5},{8,10},{9,11},{10,... | collective-permute-start | bytes 1179656 | tf_op jit(solution)/shard_map/ppermute | solution.py:241
  38.4 15.3 %copy-start.7 = (bf16[1,192,1024]{2,1,0:T(8,128)(2,1)}, bf16[1,192,1024]{2,1,0:T(8,128)(2,1)S(1)}, u32[]{:S(2)}) copy-start(bf16[1,192,1024]{2,1,0:T(8,128)(2,1)S(1)} %collective-permute-done.1.refs_1_.refs_7_) | copy-start | bytes 1179652
  46.4 7.3 %copy-start.8 = (bf16[1,192,1024]{2,1,0:T(8,128)(2,1)}, bf16[1,192,1024]{2,1,0:T(8,128)(2,1)S(1)}, u32[]{:S(2)}) copy-start(bf16[1,192,1024]{2,1,0:T(8,128)(2,1)S(1)} %collective-permute-done.2.refs_2_.refs_8_) | copy-start | bytes 1179652
  53.8 21.3 %copy-start.1 = (bf16[1,192,1024]{2,1,0:T(8,128)(2,1)}, bf16[1,192,1024]{2,1,0:T(8,128)(2,1)S(1)}, u32[]{:S(2)}) copy-start(bf16[1,192,1024]{2,1,0:T(8,128)(2,1)S(1)} %collective-permute-done.3.refs_3_.refs_6_) | copy-start | bytes 1179652
  77.3 15.4 %collective-permute-start.6 = (bf16[256,1024]{1,0:T(8,128)(2,1)}, bf16[256,1024]{1,0:T(8,128)(2,1)}, u32[]{:S(2)}, u32[]{:S(2)}) collective-permute-start(bf16[256,1024]{1,0:T(8,128)(2,1)} %get-tuple-element.39.own0), channel_id=1, source_target_pairs={{0,1},{1,2},{2,3},{3,0},{4,5},{5,6},{6,7},{7,4},{8,9},{9,10},{10,1... | collective-permute-start | bytes 1572872 | tf_op jit(solution)/shard_map/ppermute | solution.py:456
  78.5 27.9 %copy-start.13 = (f32[4096]{0:T(1024)S(1)}, f32[4096]{0:T(1024)}, u32[]{:S(2)}) copy-start(f32[4096]{0:T(1024)} %param.20) | copy-start | bytes 49156
  78.5 14.2 %collective-permute-start.8 = (bf16[256,1024]{1,0:T(8,128)(2,1)}, bf16[256,1024]{1,0:T(8,128)(2,1)}, u32[]{:S(2)}, u32[]{:S(2)}) collective-permute-start(bf16[256,1024]{1,0:T(8,128)(2,1)} %get-tuple-element.40.own1), channel_id=1, source_target_pairs={{0,3},{1,0},{2,1},{3,2},{4,7},{5,4},{6,5},{7,6},{8,11},{9,8},{10,9... | collective-permute-start | bytes 1572872 | tf_op jit(solution)/shard_map/ppermute | solution.py:457
  80.0 23.7 %collective-permute-start.11 = (bf16[256,1024]{1,0:T(8,128)(2,1)}, bf16[256,1024]{1,0:T(8,128)(2,1)}, u32[]{:S(2)}, u32[]{:S(2)}) collective-permute-start(bf16[256,1024]{1,0:T(8,128)(2,1)} %get-tuple-element.39.own0), channel_id=1, source_target_pairs={{0,3},{1,0},{2,1},{3,2},{4,7},{5,4},{6,5},{7,6},{8,11},{9,8},{10,9... | collective-permute-start | bytes 1572872 | tf_op jit(solution)/shard_map/ppermute | solution.py:457
  81.3 25.1 %collective-permute-start.10 = (bf16[256,1024]{1,0:T(8,128)(2,1)}, bf16[256,1024]{1,0:T(8,128)(2,1)}, u32[]{:S(2)}, u32[]{:S(2)}) collective-permute-start(bf16[256,1024]{1,0:T(8,128)(2,1)} %get-tuple-element.40.own1), channel_id=1, source_target_pairs={{0,1},{1,2},{2,3},{3,0},{4,5},{5,6},{6,7},{7,4},{8,9},{9,10},{10,1... | collective-permute-start | bytes 1572872 | tf_op jit(solution)/shard_map/ppermute | solution.py:456
  92.7 22.5 %collective-permute-start.7 = (bf16[256,1024]{1,0:T(8,128)(2,1)}, bf16[256,1024]{1,0:T(8,128)(2,1)}, u32[]{:S(2)}, u32[]{:S(2)}) collective-permute-start(bf16[256,1024]{1,0:T(8,128)(2,1)} %collective-permute-done.6.left0), channel_id=1, source_target_pairs={{0,1},{1,2},{2,3},{3,0},{4,5},{5,6},{6,7},{7,4},{8,9},{9,10},{10,1... | collective-permute-start | bytes 1572872 | tf_op jit(solution)/shard_map/ppermute | solution.py:458
  92.7 22.5 %collective-permute-start.9 = (bf16[256,1024]{1,0:T(8,128)(2,1)}, bf16[256,1024]{1,0:T(8,128)(2,1)}, u32[]{:S(2)}, u32[]{:S(2)}) collective-permute-start(bf16[256,1024]{1,0:T(8,128)(2,1)} %collective-permute-done.8.right1), channel_id=1, source_target_pairs={{0,3},{1,0},{2,1},{3,2},{4,7},{5,4},{6,5},{7,6},{8,11},{9,8},{10,9... | collective-permute-start | bytes 1572872 | tf_op jit(solution)/shard_map/ppermute | solution.py:459
  97.6 28.8 %collective-permute-start.15 = (bf16[256,1024]{1,0:T(8,128)(2,1)}, bf16[256,1024]{1,0:T(8,128)(2,1)}, u32[]{:S(2)}, u32[]{:S(2)}) collective-permute-start(bf16[256,1024]{1,0:T(8,128)(2,1)} %get-tuple-element.46.own0), channel_id=1, source_target_pairs={{0,1},{1,2},{2,3},{3,0},{4,5},{5,6},{6,7},{7,4},{8,9},{9,10},{10,1... | collective-permute-start | bytes 1572872 | tf_op jit(solution)/shard_map/ppermute | solution.py:456
  103.7 24.0 %collective-permute-start.17 = (bf16[256,1024]{1,0:T(8,128)(2,1)}, bf16[256,1024]{1,0:T(8,128)(2,1)}, u32[]{:S(2)}, u32[]{:S(2)}) collective-permute-start(bf16[256,1024]{1,0:T(8,128)(2,1)} %get-tuple-element.47.own1), channel_id=1, source_target_pairs={{0,3},{1,0},{2,1},{3,2},{4,7},{5,4},{6,5},{7,6},{8,11},{9,8},{10,9... | collective-permute-start | bytes 1572872 | tf_op jit(solution)/shard_map/ppermute | solution.py:457
  106.4 1.0 copy-start.3
  107.4 1.0 copy-start.4
  117.6 13.9 %collective-permute-start.14 = (bf16[768,128]{1,0:T(8,128)(2,1)S(1)}, bf16[768,128]{1,0:T(8,128)(2,1)S(1)}, u32[]{:S(2)}, u32[]{:S(2)}) collective-permute-start(bf16[768,128]{1,0:T(8,128)(2,1)S(1)} %far_project.2.refs_1_), channel_id=1, source_target_pairs={{0,2},{1,3},{2,0},{3,1},{4,6},{5,7},{6,4},{7,5},{8,10},{9,11},{10,... | collective-permute-start | bytes 589832 | tf_op jit(solution)/shard_map/ppermute | solution.py:241
  120.0 14.5 %collective-permute-start.13 = (bf16[768,128]{1,0:T(8,128)(2,1)S(1)}, bf16[768,128]{1,0:T(8,128)(2,1)S(1)}, u32[]{:S(2)}, u32[]{:S(2)}) collective-permute-start(bf16[768,128]{1,0:T(8,128)(2,1)S(1)} %far_project.2.refs_1_), channel_id=1, source_target_pairs={{0,3},{1,0},{2,1},{3,2},{4,7},{5,4},{6,5},{7,6},{8,11},{9,8},{10,9... | collective-permute-start | bytes 589832 | tf_op jit(solution)/shard_map/ppermute | solution.py:240
  121.1 16.1 %collective-permute-start.12 = (bf16[768,128]{1,0:T(8,128)(2,1)S(1)}, bf16[768,128]{1,0:T(8,128)(2,1)S(1)}, u32[]{:S(2)}, u32[]{:S(2)}) collective-permute-start(bf16[768,128]{1,0:T(8,128)(2,1)S(1)} %far_project.2.refs_1_), channel_id=1, source_target_pairs={{0,1},{1,2},{2,3},{3,0},{4,5},{5,6},{6,7},{7,4},{8,9},{9,10},{10,1... | collective-permute-start | bytes 589832 | tf_op jit(solution)/shard_map/ppermute | solution.py:239
  126.4 22.8 %collective-permute-start.20 = (bf16[256,1024]{1,0:T(8,128)(2,1)}, bf16[256,1024]{1,0:T(8,128)(2,1)}, u32[]{:S(2)}, u32[]{:S(2)}) collective-permute-start(bf16[256,1024]{1,0:T(8,128)(2,1)} %get-tuple-element.46.own0), channel_id=1, source_target_pairs={{0,3},{1,0},{2,1},{3,2},{4,7},{5,4},{6,5},{7,6},{8,11},{9,8},{10,9... | collective-permute-start | bytes 1572872 | tf_op jit(solution)/shard_map/ppermute | solution.py:457
  127.7 21.5 %collective-permute-start.19 = (bf16[256,1024]{1,0:T(8,128)(2,1)}, bf16[256,1024]{1,0:T(8,128)(2,1)}, u32[]{:S(2)}, u32[]{:S(2)}) collective-permute-start(bf16[256,1024]{1,0:T(8,128)(2,1)} %get-tuple-element.47.own1), channel_id=1, source_target_pairs={{0,1},{1,2},{2,3},{3,0},{4,5},{5,6},{6,7},{7,4},{8,9},{9,10},{10,1... | collective-permute-start | bytes 1572872 | tf_op jit(solution)/shard_map/ppermute | solution.py:456
  131.6 24.8 %collective-permute-start.16 = (bf16[256,1024]{1,0:T(8,128)(2,1)}, bf16[256,1024]{1,0:T(8,128)(2,1)}, u32[]{:S(2)}, u32[]{:S(2)}) collective-permute-start(bf16[256,1024]{1,0:T(8,128)(2,1)} %collective-permute-done.15.left0), channel_id=1, source_target_pairs={{0,1},{1,2},{2,3},{3,0},{4,5},{5,6},{6,7},{7,4},{8,9},{9,10},{10,1... | collective-permute-start | bytes 1572872 | tf_op jit(solution)/shard_map/ppermute | solution.py:458
  134.5 22.6 %collective-permute-start.18 = (bf16[256,1024]{1,0:T(8,128)(2,1)}, bf16[256,1024]{1,0:T(8,128)(2,1)}, u32[]{:S(2)}, u32[]{:S(2)}) collective-permute-start(bf16[256,1024]{1,0:T(8,128)(2,1)} %collective-permute-done.17.right1), channel_id=1, source_target_pairs={{0,3},{1,0},{2,1},{3,2},{4,7},{5,4},{6,5},{7,6},{8,11},{9,8},{10,9... | collective-permute-start | bytes 1572872 | tf_op jit(solution)/shard_map/ppermute | solution.py:459
  140.8 36.4 %all-to-all-start.1 = ((bf16[64,8,1024]{2,1,0:T(8,128)(2,1)}), bf16[64,8,1024]{2,1,0:T(8,128)(2,1)}, u32[]{:S(2)}, u32[]{:S(2)}) async-start(bf16[64,8,1024]{2,1,0:T(8,128)(2,1)} %bitcast.19), calls=%async_computation.1 | async-start | bytes 2097152 | tf_op jit(solution)/shard_map/all_to_all | solution.py:466
  157.1 14.6 %copy-start.2 = (bf16[1,192,1024]{2,1,0:T(8,128)(2,1)S(1)}, bf16[1,192,1024]{2,1,0:T(8,128)(2,1)}, u32[]{:S(2)}) copy-start(bf16[1,192,1024]{2,1,0:T(8,128)(2,1)} %copy-done.1) | copy-start | bytes 1179652
  159.6 7.4 %collective-permute-start.23 = (bf16[768,128]{1,0:T(8,128)(2,1)S(1)}, bf16[768,128]{1,0:T(8,128)(2,1)S(1)}, u32[]{:S(2)}, u32[]{:S(2)}) collective-permute-start(bf16[768,128]{1,0:T(8,128)(2,1)S(1)} %far_project.3.refs_1_), channel_id=1, source_target_pairs={{0,2},{1,3},{2,0},{3,1},{4,6},{5,7},{6,4},{7,5},{8,10},{9,11},{10,... | collective-permute-start | bytes 589832 | tf_op jit(solution)/shard_map/ppermute | solution.py:241
  162.3 9.3 %collective-permute-start.22 = (bf16[768,128]{1,0:T(8,128)(2,1)S(1)}, bf16[768,128]{1,0:T(8,128)(2,1)S(1)}, u32[]{:S(2)}, u32[]{:S(2)}) collective-permute-start(bf16[768,128]{1,0:T(8,128)(2,1)S(1)} %far_project.3.refs_1_), channel_id=1, source_target_pairs={{0,3},{1,0},{2,1},{3,2},{4,7},{5,4},{6,5},{7,6},{8,11},{9,8},{10,9... | collective-permute-start | bytes 589832 | tf_op jit(solution)/shard_map/ppermute | solution.py:240
  163.3 8.4 %collective-permute-start.21 = (bf16[768,128]{1,0:T(8,128)(2,1)S(1)}, bf16[768,128]{1,0:T(8,128)(2,1)S(1)}, u32[]{:S(2)}, u32[]{:S(2)}) collective-permute-start(bf16[768,128]{1,0:T(8,128)(2,1)S(1)} %far_project.3.refs_1_), channel_id=1, source_target_pairs={{0,1},{1,2},{2,3},{3,0},{4,5},{5,6},{6,7},{7,4},{8,9},{9,10},{10,1... | collective-permute-start | bytes 589832 | tf_op jit(solution)/shard_map/ppermute | solution.py:239
  175.2 8.4 %copy-start.12 = (bf16[512,64]{1,0:T(8,128)(2,1)S(1)}, bf16[512,64]{1,0:T(8,128)(2,1)}, u32[]{:S(2)}) copy-start(bf16[512,64]{1,0:T(8,128)(2,1)} %get-tuple-element.29) | copy-start | bytes 196612
  175.2 9.2 %copy-start.11 = (bf16[512,64]{1,0:T(8,128)(2,1)S(1)}, bf16[512,64]{1,0:T(8,128)(2,1)}, u32[]{:S(2)}) copy-start(bf16[512,64]{1,0:T(8,128)(2,1)} %get-tuple-element.30) | copy-start | bytes 196612
  175.2 9.9 %copy-start.10 = (bf16[512,64]{1,0:T(8,128)(2,1)S(1)}, bf16[512,64]{1,0:T(8,128)(2,1)}, u32[]{:S(2)}) copy-start(bf16[512,64]{1,0:T(8,128)(2,1)} %get-tuple-element.44) | copy-start | bytes 196612
  175.2 10.6 %copy-start.9 = (bf16[512,64]{1,0:T(8,128)(2,1)S(1)}, bf16[512,64]{1,0:T(8,128)(2,1)}, u32[]{:S(2)}) copy-start(bf16[512,64]{1,0:T(8,128)(2,1)} %get-tuple-element.45) | copy-start | bytes 196612
  177.2 34.5 %all-to-all-start.2 = ((bf16[64,8,1024]{2,1,0:T(8,128)(2,1)}), bf16[64,8,1024]{2,1,0:T(8,128)(2,1)S(1)}, u32[]{:S(2)}, u32[]{:S(2)}) async-start(bf16[64,8,1024]{2,1,0:T(8,128)(2,1)} %bitcast.20), calls=%async_computation.2 | async-start | bytes 2097152 | tf_op jit(solution)/shard_map/all_to_all | solution.py:466
  211.7 1.0 copy-start.5

commit v3 on v2

--- a/solution.py
+++ b/solution.py
@@ -15,6 +15,7 @@
 SLOTS = 8
 
 epsilon = 1e-06
+PICK_WEIGHT = (20, 0)
 FAR_WEIGHT = (1, 14)
 F32 = jnp.float32
 BF16 = jnp.bfloat16
@@ -60,21 +61,18 @@
         chosen = table(spread, slot)
         tables[j][...] = jnp.where(chosen, dot(spread, mix_hi), 0.0).astype(BF16)
         tables[2 + j][...] = jnp.where(chosen, dot(spread, mix_lo), 0.0).astype(BF16)
-    for j in range(EXP_DEV):
-        spread = jnp.where(expert == owner + j * (slots // SLOTS), 1.0, 0.0).astype(BF16)
-        tables[4][pl.ds(j * slots, slots), :] = jnp.where(table(spread, slot), 1.0, 0.0).astype(BF16)
+        tables[4 + j][...] = jnp.where(chosen, 1.0, 0.0).astype(BF16)
 
 
 def route(ids, probs, devices):
     rows = ids.shape[1]
     table = jax.ShapeDtypeStruct((devices * SLOTS, rows), BF16)
 
-    tall = jax.ShapeDtypeStruct((EXP_DEV * devices * SLOTS, rows), BF16)
     return pl.pallas_call(
         route_kernel,
         in_specs=[VMEM, VMEM],
-        out_specs=[VMEM] * 5,
-        out_shape=[table] * 4 + [tall],
+        out_specs=[VMEM] * 6,
+        out_shape=[table] * 6,
         cost_estimate=pl.CostEstimate(
             flops=16 * devices * SLOTS * rows, bytes_accessed=0, transcendentals=0
         ),
@@ -155,7 +153,7 @@
 def attention(lens, me, queries, new_key, new_value, keys, values, residual, gain):
     rows, part = queries.shape
     span, depth = keys.shape[1:]
-    step = 16
+    step = 32
     wide = pl.BlockSpec((step, part), lambda i, n, m: (i, 0))
     slim = pl.BlockSpec((step, depth), lambda i, n, m: (i, 0))
     cache = pl.BlockSpec((step, span, depth), lambda i, n, m: (i, 0, 0))
@@ -185,11 +183,11 @@
     )(lens, me, queries, new_key, new_value, keys, values, residual, gain)
 
 
-def place_kernel(table_ref, rows_ref, out_ref):
-    out_ref[...] = dot(table_ref[...], rows_ref[...]).astype(BF16)
-
-
-def place_rows(table, rows):
+def place_kernel(table_ref, rows_ref, *refs):
+    refs[-1][...] = dot(table_ref[...], rows_ref[...]).astype(BF16)
+
+
+def place_rows(table, rows, *after):
     slots, part = table.shape[0], rows.shape[1]
     return pl.pallas_call(
         place_kernel,
@@ -197,14 +195,15 @@
         in_specs=[
             pl.BlockSpec((slots // 2, table.shape[1]), lambda i: (i, 0)),
             pl.BlockSpec(rows.shape, lambda i: (0, 0)),
-        ],
+        ]
+        + [ANY] * len(after),
         out_specs=pl.BlockSpec((slots // 2, part), lambda i: (i, 0)),
         out_shape=jax.ShapeDtypeStruct((slots, part), BF16),
         cost_estimate=pl.CostEstimate(
             flops=2 * table.size * part, bytes_accessed=4 * slots * part, transcendentals=0
         ),
         name="place_rows",
-    )(table, rows)
+    )(table, rows, *after)
 
 
 def pick_kernel(all_ref, *refs):
@@ -213,7 +212,7 @@
         out_ref[...] = all_ref[pl.ds(i * count, count)].reshape(out_ref.shape)
 
 
-def pick(everything, expert, *after):
+def pick(everything, expert, work, *after):
     devices, _, slots, part = everything.shape
     half = devices * slots // 2
     return pl.pallas_call(
@@ -223,8 +222,9 @@
         + [ANY] * len(after),
         out_specs=[pl.BlockSpec((half, part), lambda i: (0, 0))] * 2,
         out_shape=[jax.ShapeDtypeStruct((half, part), everything.dtype)] * 2,
-        cost_estimate=pl.CostEstimate(
-            flops=0, bytes_accessed=8 * half * part, transcendentals=0
+        compiler_params=BIG,
+        cost_estimate=pl.CostEstimate(
+            flops=int(work * 1e9), bytes_accessed=8 * half * part, transcendentals=0
         ),
         name="pick",
     )(everything, *after)
@@ -420,6 +420,7 @@
                   pl.BlockSpec((back.shape[0], part // steps), lambda i: (0, i))],
         out_specs=column,
         out_shape=jax.ShapeDtypeStruct((rows, part), dtype),
+        compiler_params=BIG,
         cost_estimate=pl.CostEstimate(
             flops=4 * hi.size * part, bytes_accessed=2 * back.size, transcendentals=0
         ),
@@ -436,7 +437,7 @@
     devices = lax.axis_size("side") * lax.axis_size("grp")
     slots = devices * SLOTS
     me = lax.axis_index("tp").astype(jnp.int32).reshape(1)
-    hi0, hi1, lo0, lo1, table = route(expert_ids.T, gate_probs.T, devices)
+    hi0, hi1, lo0, lo1, table0, table1 = route(expert_ids.T, gate_probs.T, devices)
     blocks = split_columns(me, w_down)
     gain = norm_gain.reshape(1, -1)
     inv_gain = 1.0 / gain
@@ -449,10 +450,12 @@
     moved = [exchange(*blocks[: N_TP - 1]), exchange(*blocks[N_TP - 1 :])]
     moved[0] = in_hbm(*moved[0])
     w_gate, w_up = in_hbm(w_gate, w_up)
-    arrived = swap(place_rows(table, scaled).reshape(devices, EXP_DEV, SLOTS, part))
     total = summed
-    for expert, hi, lo in ((0, hi0, lo0), (1, hi1, lo1)):
-        own = pick(arrived, expert, *moved[0], *moved[1])
+    own = ()
+    for expert, table, hi, lo in ((0, table0, hi0, lo0), (1, table1, hi1, lo1)):
+        placed = place_rows(table, scaled)
+        arrived = swap(placed.reshape(devices, SLOTS, part)).reshape(devices, 1, SLOTS, part)
+        own = pick(arrived, 0, PICK_WEIGHT[expert], *moved[0], *moved[1])
         left = [lax.ppermute(half, "tp", RIGHT) for half in own]
         right = [lax.ppermute(half, "tp", LEFT) for half in own]
         low = lax.ppermute(left[0], "tp", RIGHT)

time: 216 us -> 206 us (0.954)
  waiting for transfers between devices: 107 us -> 76.3 us
  starting transfers between devices: 59.2 us -> 79.1 us
    ppermute x4, waiting for transfers between devices: 24.6 us -> 1.08 us  [exchange(): lax.ppermute(for_across, 'tp', ACROSS)]
    all_to_all x1 -> x2, starting transfers between devices: 13.7 us -> 23.8 us  [body(): swap(placed.reshape(devices, SLOTS, part)).reshape(devices, 1, SLOTS, part)]
    all_to_all x2, starting transfers between devices: 14.8 us -> 24.3 us  [body(): back = swap(produced.reshape(devices, SLOTS, part)).reshape(slots, part)]
    all_to_all x1 -> x2, waiting for transfers between devices: 11.8 us -> 18.6 us  [body(): swap(placed.reshape(devices, SLOTS, part)).reshape(devices, 1, SLOTS, part)]
    ppermute x4, waiting for transfers between devices: 6.8 us -> 0.01 us  [exchange(): lax.ppermute(for_left, 'tp', LEFT)]
    ppermute x4, waiting for transfers between devices: 6.12 us -> 0.01 us  [body(): right = [lax.ppermute(half, 'tp', LEFT) for half in own]]
    ppermute x4, starting transfers between devices: 8.08 us -> 3.99 us  [exchange(): lax.ppermute(for_across, 'tp', ACROSS)]
    ppermute x4, waiting for transfers between devices: 12.1 us -> 15.4 us  [exchange(): lax.ppermute(for_right, 'tp', RIGHT)]
  transfers between devices with their start and end apart: 27 -> 28, of which waited for: 18 -> 11; matrix products, arithmetic and copies ran while one was open for 1% -> 2% of each run, Pallas kernels for 13% -> 16%
where the time goes in v3:
time: 206 us
  starting transfers between devices  79.1 us (38%)
  waiting for transfers between devices  76.3 us (37%)
  Pallas kernels  43.6 us (21%)
  local copies, waits for them, and re-layouts  5.65 us (3%)
    all_to_all x2, waiting for transfers between devices, body(): back = swap(produced.reshape(devices, SLOTS, part)).reshape(slots, part)  27 us
    all_to_all x2, starting transfers between devices, body(): back = swap(produced.reshape(devices, SLOTS, part)).reshape(slots, part)  24.3 us
    all_to_all x2, starting transfers between devices, body(): swap(placed.reshape(devices, SLOTS, part)).reshape(devices, 1, SLOTS, part)  23.8 us
    all_to_all x2, waiting for transfers between devices, body(): swap(placed.reshape(devices, SLOTS, part)).reshape(devices, 1, SLOTS, part)  18.6 us
    ppermute x4, waiting for transfers between devices, exchange(): lax.ppermute(for_right, 'tp', RIGHT)  15.4 us
    ppermute x4, waiting for transfers between devices, body(): left = [lax.ppermute(half, 'tp', RIGHT) for half in own]  13.4 us
    pallas_call x2, Pallas kernels, near_project(): pl.pallas_call(near_kernel, grid_spec=pltpu.PrefetchScalarGridSpec(num_sc...  10.1 us
    ppermute x4, starting transfers between devices, body(): right = [lax.ppermute(half, 'tp', LEFT) for half in own]  9.95 us
  transfers between devices with their start and end apart: 28, of which 11 were waited for; matrix products, arithmetic and copies ran while one was open for 2% of the time, Pallas kernels for 16%

profile of v3, /device:TPU:1, one launch (start us, length us, event | category | flops | bytes accessed | tf_op | source)
XLA Modules:
  0.0 205.5 jit_solution(4821088398700485177)
XLA Ops:
  0.0 2.2 %route.1 = (bf16[512,64]{1,0:T(8,128)(2,1)}, bf16[512,64]{1,0:T(8,128)(2,1)}, bf16[512,64]{1,0:T(8,128)(2,1)}, bf16[512,64]{1,0:T(8,128)(2,1)}, bf16[512,64]{1,0:T(8,128)(2,1)}, /*index=5*/bf16[512,64]{1,0:T(8,128)(2,1)}) custom-call(s32[8,64]{1,0:T(8,128)} %bitcast.31, f32[8,64]{1,0:T(8,128)} %bitcast.32), custom_call_target="tpu_custom_call" | custom-call | flops 524288 | tf_op jit(solution)/shard_map/route/pallas_call | solution.py:71
  2.2 5.3 %attention.1 = (f32[64,1024]{1,0:T(8,128)}, bf16[64,1024]{1,0:T(8,128)(2,1)}) custom-call(s32[64]{0:T(128)} %lens_ref.1, s32[1]{0:T(128)} %bitcast.me_ref.refs_0_, bf16[64,1024]{1,0:T(8,128)(2,1)} %refs_0_.1, bf16[64,128]{1,0:T(8,128)(2,1)} %refs_1_.1, bf16[64,128]{1,0:T(8,128)(2,1)} %refs_2_.1, bf16[64,128,128]{2,1,0:T(8,128)(2,1)} %refs_3_.1, ...), custom_call_target="tpu_custom_call" | custom-call | flops 33554432 | bytes 4194304 | tf_op jit(solution)/shard_map/attention/pallas_call | solution.py:164
  7.5 2.3 %place_rows.2 = bf16[512,1024]{1,0:T(8,128)(2,1)} custom-call(bf16[512,64]{1,0:T(8,128)(2,1)} %get-tuple-element.32.table_ref, bf16[64,1024]{1,0:T(8,128)(2,1)} %get-tuple-element.33.rows_ref), custom_call_target="tpu_custom_call" | custom-call | flops 67108864 | bytes 2097152 | tf_op jit(solution)/shard_map/place_rows/pallas_call | solution.py:192
  9.8 13.4 %all-to-all-start = ((bf16[64,8,1024]{2,1,0:T(8,128)(2,1)}), bf16[64,8,1024]{2,1,0:T(8,128)(2,1)}, u32[]{:S(2)}, u32[]{:S(2)}) async-start(bf16[64,8,1024]{2,1,0:T(8,128)(2,1)} %bitcast.29), calls=%async_computation | async-start | bytes 2097152 | tf_op jit(solution)/shard_map/all_to_all | solution.py:457
  23.3 1.6 split_columns.1
  24.9 1.2 collective-permute-start
  26.1 1.5 collective-permute-start.1
  27.6 1.5 collective-permute-start.2
  29.1 0.3 collective-permute-start.3
  29.4 2.4 %collective-permute-start.4 = (bf16[1,192,1024]{2,1,0:T(8,128)(2,1)}, bf16[1,192,1024]{2,1,0:T(8,128)(2,1)}, u32[]{:S(2)}, u32[]{:S(2)}) collective-permute-start(bf16[1,192,1024]{2,1,0:T(8,128)(2,1)} %get-tuple-element.38), channel_id=1, source_target_pairs={{0,3},{1,0},{2,1},{3,2},{4,7},{5,4},{6,5},{7,6},{8,11},{9,8},{10,9... | collective-permute-start | bytes 1179656 | tf_op jit(solution)/shard_map/ppermute | solution.py:240
  31.8 4.7 %collective-permute-done.refs_0_.refs_6_ = bf16[1,192,1024]{2,1,0:T(8,128)(2,1)S(1)} collective-permute-done((bf16[1,192,1024]{2,1,0:T(8,128)(2,1)S(1)}, bf16[1,192,1024]{2,1,0:T(8,128)(2,1)S(1)}, u32[]{:S(2)}, u32[]{:S(2)}) %collective-permute-start) | collective-permute-done | bytes 393248 | tf_op jit(solution)/shard_map/ppermute | solution.py:239
  36.5 0.7 copy-done.2
  37.2 1.6 collective-permute-start.5
  38.8 2.3 %place_rows.3 = bf16[512,1024]{1,0:T(8,128)(2,1)} custom-call(bf16[512,64]{1,0:T(8,128)(2,1)} %get-tuple-element.47.table_ref, bf16[64,1024]{1,0:T(8,128)(2,1)} %get-tuple-element.33.rows_ref), custom_call_target="tpu_custom_call" | custom-call | flops 67108864 | bytes 2097152 | tf_op jit(solution)/shard_map/place_rows/pallas_call | solution.py:192
  41.1 10.3 %all-to-all-done = bf16[64,8,1024]{2,1,0:T(8,128)(2,1)} async-done(((bf16[64,8,1024]{2,1,0:T(8,128)(2,1)}), bf16[64,8,1024]{2,1,0:T(8,128)(2,1)}, u32[]{:S(2)}, u32[]{:S(2)}) %all-to-all-start) | async-done | bytes 1048608 | tf_op jit(solution)/shard_map/all_to_all | solution.py:457
  51.4 10.3 %all-to-all-start.2 = ((bf16[64,8,1024]{2,1,0:T(8,128)(2,1)}), bf16[64,8,1024]{2,1,0:T(8,128)(2,1)}, u32[]{:S(2)}, u32[]{:S(2)}) async-start(bf16[64,8,1024]{2,1,0:T(8,128)(2,1)} %bitcast.28), calls=%async_computation.2 | async-start | bytes 2097152 | tf_op jit(solution)/shard_map/all_to_all | solution.py:457
  61.7 0.0 collective-permute-done.3.refs_3_.refs_6_
  61.7 0.0 collective-permute-done.4.refs_4_.refs_7_
  61.7 1.1 collective-permute-done.5.refs_5_.refs_8_
  62.8 2.3 %pick.2 = (bf16[256,1024]{1,0:T(8,128)(2,1)}, bf16[256,1024]{1,0:T(8,128)(2,1)}) custom-call(bf16[64,1,8,1024]{3,2,1,0:T(8,128)(2,1)} %bitcast.7.all_ref, bf16[1,192,1024]{2,1,0:T(8,128)(2,1)} %copy-done.2, bf16[1,192,1024]{2,1,0:T(8,128)(2,1)} %collective-permute-done.1.refs_1_.refs_7_, bf16[1,192,1024]{2,1,0:T(8,128)(2,1)} %collective-permute-done.2.refs_2_.refs_8_, ...), custom_call_target="tpu_custom_call" | custom-call | flops 20000000000 | bytes 2097152 | tf_op jit(solution)/shard_map/pick/pallas_call | solution.py:218
  65.1 0.8 collective-permute-start.6
  65.8 1.9 collective-permute-start.8
  67.8 2.7 %collective-permute-start.11 = (bf16[256,1024]{1,0:T(8,128)(2,1)}, bf16[256,1024]{1,0:T(8,128)(2,1)}, u32[]{:S(2)}, u32[]{:S(2)}) collective-permute-start(bf16[256,1024]{1,0:T(8,128)(2,1)} %get-tuple-element.40.own0), channel_id=1, source_target_pairs={{0,3},{1,0},{2,1},{3,2},{4,7},{5,4},{6,5},{7,6},{8,11},{9,8},{10,9... | collective-permute-start | bytes 1572872 | tf_op jit(solution)/shard_map/ppermute | solution.py:460
  70.4 8.3 %collective-permute-done.6.left0 = bf16[256,1024]{1,0:T(8,128)(2,1)} collective-permute-done((bf16[256,1024]{1,0:T(8,128)(2,1)}, bf16[256,1024]{1,0:T(8,128)(2,1)}, u32[]{:S(2)}, u32[]{:S(2)}) %collective-permute-start.6) | collective-permute-done | bytes 524320 | tf_op jit(solution)/shard_map/ppermute | solution.py:459
  78.8 0.0 collective-permute-start.7
  78.8 0.0 collective-permute-done.8.right1
  78.8 2.7 %collective-permute-start.9 = (bf16[256,1024]{1,0:T(8,128)(2,1)}, bf16[256,1024]{1,0:T(8,128)(2,1)}, u32[]{:S(2)}, u32[]{:S(2)}) collective-permute-start(bf16[256,1024]{1,0:T(8,128)(2,1)} %collective-permute-done.8.right1), channel_id=1, source_target_pairs={{0,3},{1,0},{2,1},{3,2},{4,7},{5,4},{6,5},{7,6},{8,11},{9,8},{10,9... | collective-permute-start | bytes 1572872 | tf_op jit(solution)/shard_map/ppermute | solution.py:462
  81.4 8.3 %all-to-all-done.2 = bf16[64,8,1024]{2,1,0:T(8,128)(2,1)} async-done(((bf16[64,8,1024]{2,1,0:T(8,128)(2,1)}), bf16[64,8,1024]{2,1,0:T(8,128)(2,1)}, u32[]{:S(2)}, u32[]{:S(2)}) %all-to-all-start.2) | async-done | bytes 1048608 | tf_op jit(solution)/shard_map/all_to_all | solution.py:457
  89.8 2.3 %pick.3 = (bf16[256,1024]{1,0:T(8,128)(2,1)}, bf16[256,1024]{1,0:T(8,128)(2,1)}) custom-call(bf16[64,1,8,1024]{3,2,1,0:T(8,128)(2,1)} %bitcast.14.all_ref, bf16[1,192,1024]{2,1,0:T(8,128)(2,1)} %copy-done.2, bf16[1,192,1024]{2,1,0:T(8,128)(2,1)} %collective-permute-done.1.refs_1_.refs_7_, bf16[1,192,1024]{2,1,0:T(8,128)(2,1)} %collective-permute-done.2.refs_2_.refs_8_, ...), custom_call_target="tpu_custom_call" | custom-call | bytes 2097152 | tf_op jit(solution)/shard_map/pick/pallas_call | solution.py:218
  92.0 0.0 collective-permute-done.10.left1
  92.0 2.7 %collective-permute-start.17 = (bf16[256,1024]{1,0:T(8,128)(2,1)}, bf16[256,1024]{1,0:T(8,128)(2,1)}, u32[]{:S(2)}, u32[]{:S(2)}) collective-permute-start(bf16[256,1024]{1,0:T(8,128)(2,1)} %get-tuple-element.49.own1), channel_id=1, source_target_pairs={{0,3},{1,0},{2,1},{3,2},{4,7},{5,4},{6,5},{7,6},{8,11},{9,8},{10,9... | collective-permute-start | bytes 1572872 | tf_op jit(solution)/shard_map/ppermute | solution.py:460
  94.7 0.7 broadcast_divide_fusion
  95.4 5.1 %near_project.2 = (f32[512,192]{1,0:T(8,128)S(1)}, f32[512,192]{1,0:T(8,128)S(1)}, f32[512,128]{1,0:T(8,128)S(1)}) custom-call(s32[1]{0:T(128)} %bitcast.me_ref.refs_0_, bf16[256,1024]{1,0:T(8,128)(2,1)} %get-tuple-element.40.own0, bf16[256,1024]{1,0:T(8,128)(2,1)} %get-tuple-element.41.own1, bf16[256,1024]{1,0:T(8,128)(2,1)} %collective-permute-done.6.left0, ...), custom_call_target="tpu_custom_call" | custom-call | flops 1207959552 | bytes 7340032 | tf_op jit(solution)/shard_map/near_project/pallas_call | solution.py:300
  100.5 0.7 collective-permute-done.7.low
  101.2 2.5 %far_project.2.refs_1_ = bf16[768,128]{1,0:T(8,128)(2,1)S(1)} custom-call(s32[1]{0:T(128)} %bitcast.me_ref.refs_0_, bf16[256,1024]{1,0:T(8,128)(2,1)} %collective-permute-done.7.low, bf16[256,1024]{1,0:T(8,128)(2,1)} %collective-permute-done.9.high, f32[512,192]{1,0:T(8,128)S(1)} %get-tuple-element.42.gate_in, f32[512,192]{1,0:T(8,128)S(1)} %get-tuple-element.43.up_in, ...), custom_call_target="tpu_custom_call" | custom-call | flops 1000000000 | bytes 4194304 | tf_op jit(solution)/shard_map/far_project/pallas_call | solution.py:334
  103.7 0.1 collective-permute-start.12
  103.8 2.7 %collective-permute-start.13 = (bf16[768,128]{1,0:T(8,128)(2,1)S(1)}, bf16[768,128]{1,0:T(8,128)(2,1)S(1)}, u32[]{:S(2)}, u32[]{:S(2)}) collective-permute-start(bf16[768,128]{1,0:T(8,128)(2,1)S(1)} %far_project.2.refs_1_), channel_id=1, source_target_pairs={{0,3},{1,0},{2,1},{3,2},{4,7},{5,4},{6,5},{7,6},{8,11},{9,8},{10,9... | collective-permute-start | bytes 589832 | tf_op jit(solution)/shard_map/ppermute | solution.py:240
  106.5 0.9 collective-permute-start.14
  107.4 5.1 %collective-permute-done.15.left0 = bf16[256,1024]{1,0:T(8,128)(2,1)} collective-permute-done((bf16[256,1024]{1,0:T(8,128)(2,1)}, bf16[256,1024]{1,0:T(8,128)(2,1)}, u32[]{:S(2)}, u32[]{:S(2)}) %collective-permute-start.15) | collective-permute-done | bytes 524320 | tf_op jit(solution)/shard_map/ppermute | solution.py:459
  112.5 0.0 collective-permute-start.19
  112.5 0.0 collective-permute-done.17.right1
  112.5 2.7 %collective-permute-start.20 = (bf16[256,1024]{1,0:T(8,128)(2,1)}, bf16[256,1024]{1,0:T(8,128)(2,1)}, u32[]{:S(2)}, u32[]{:S(2)}) collective-permute-start(bf16[256,1024]{1,0:T(8,128)(2,1)} %get-tuple-element.48.own0), channel_id=1, source_target_pairs={{0,3},{1,0},{2,1},{3,2},{4,7},{5,4},{6,5},{7,6},{8,11},{9,8},{10,9... | collective-permute-start | bytes 1572872 | tf_op jit(solution)/shard_map/ppermute | solution.py:460
  115.1 2.1 %collective-permute-done.12.refs_2_ = bf16[768,128]{1,0:T(8,128)(2,1)S(1)} collective-permute-done((bf16[768,128]{1,0:T(8,128)(2,1)S(1)}, bf16[768,128]{1,0:T(8,128)(2,1)S(1)}, u32[]{:S(2)}, u32[]{:S(2)}) %collective-permute-start.12) | collective-permute-done | bytes 196640 | tf_op jit(solution)/shard_map/ppermute | solution.py:239
  117.2 0.0 collective-permute-start.16
  117.2 0.0 collective-permute-done.13.refs_3_
  117.2 2.8 %collective-permute-start.18 = (bf16[256,1024]{1,0:T(8,128)(2,1)}, bf16[256,1024]{1,0:T(8,128)(2,1)}, u32[]{:S(2)}, u32[]{:S(2)}) collective-permute-start(bf16[256,1024]{1,0:T(8,128)(2,1)} %collective-permute-done.17.right1), channel_id=1, source_target_pairs={{0,3},{1,0},{2,1},{3,2},{4,7},{5,4},{6,5},{7,6},{8,11},{9,8},{10,9... | collective-permute-start | bytes 1572872 | tf_op jit(solution)/shard_map/ppermute | solution.py:462
  120.1 3.6 %down_project.2 = bf16[512,1024]{1,0:T(8,128)(2,1)} custom-call(s32[1]{0:T(128)} %bitcast.me_ref.refs_0_, bf16[768,128]{1,0:T(8,128)(2,1)S(1)} %far_project.2.refs_1_, bf16[768,128]{1,0:T(8,128)(2,1)S(1)} %collective-permute-done.12.refs_2_, bf16[768,128]{1,0:T(8,128)(2,1)S(1)} %collective-permute-done.13.refs_3_, ...), custom_call_target="tpu_custom_call" | custom-call | flops 805306368 | bytes 3407872 | tf_op jit(solution)/shard_map/down_project/pallas_call | solution.py:383
  123.6 18.2 %all-to-all-start.1 = ((bf16[64,8,1024]{2,1,0:T(8,128)(2,1)}), bf16[64,8,1024]{2,1,0:T(8,128)(2,1)}, u32[]{:S(2)}, u32[]{:S(2)}) async-start(bf16[64,8,1024]{2,1,0:T(8,128)(2,1)} %bitcast.26), calls=%async_computation.1 | async-start | bytes 2097152 | tf_op jit(solution)/shard_map/all_to_all | solution.py:469
  141.8 5.1 %near_project.3 = (f32[512,192]{1,0:T(8,128)S(1)}, f32[512,192]{1,0:T(8,128)S(1)}, f32[512,128]{1,0:T(8,128)S(1)}) custom-call(s32[1]{0:T(128)} %bitcast.me_ref.refs_0_, bf16[256,1024]{1,0:T(8,128)(2,1)} %get-tuple-element.48.own0, bf16[256,1024]{1,0:T(8,128)(2,1)} %get-tuple-element.49.own1, bf16[256,1024]{1,0:T(8,128)(2,1)} %collective-permute-done.15.left0, ...), custom_call_target="tpu_custom_call" | custom-call | flops 1207959552 | bytes 7340032 | tf_op jit(solution)/shard_map/near_project/pallas_call | solution.py:300
  146.9 2.5 %far_project.3.refs_1_ = bf16[768,128]{1,0:T(8,128)(2,1)S(1)} custom-call(s32[1]{0:T(128)} %bitcast.me_ref.refs_0_, bf16[256,1024]{1,0:T(8,128)(2,1)} %collective-permute-done.16.low, bf16[256,1024]{1,0:T(8,128)(2,1)} %collective-permute-done.18.high, f32[512,192]{1,0:T(8,128)S(1)} %get-tuple-element.50.gate_in, f32[512,192]{1,0:T(8,128)S(1)} %get-tuple-element.51.up_in, ...), custom_call_target="tpu_custom_call" | custom-call | flops 14000000000 | bytes 4194304 | tf_op jit(solution)/shard_map/far_project/pallas_call | solution.py:334
  149.4 0.1 collective-permute-start.21
  149.5 2.7 %collective-permute-start.22 = (bf16[768,128]{1,0:T(8,128)(2,1)S(1)}, bf16[768,128]{1,0:T(8,128)(2,1)S(1)}, u32[]{:S(2)}, u32[]{:S(2)}) collective-permute-start(bf16[768,128]{1,0:T(8,128)(2,1)S(1)} %far_project.3.refs_1_), channel_id=1, source_target_pairs={{0,3},{1,0},{2,1},{3,2},{4,7},{5,4},{6,5},{7,6},{8,11},{9,8},{10,9... | collective-permute-start | bytes 589832 | tf_op jit(solution)/shard_map/ppermute | solution.py:240
  152.2 8.7 %collective-permute-done.21.refs_2_ = bf16[768,128]{1,0:T(8,128)(2,1)S(1)} collective-permute-done((bf16[768,128]{1,0:T(8,128)(2,1)S(1)}, bf16[768,128]{1,0:T(8,128)(2,1)S(1)}, u32[]{:S(2)}, u32[]{:S(2)}) %collective-permute-start.21) | collective-permute-done | bytes 196640 | tf_op jit(solution)/shard_map/ppermute | solution.py:239
  160.8 3.5 %down_project.3 = bf16[512,1024]{1,0:T(8,128)(2,1)} custom-call(s32[1]{0:T(128)} %bitcast.me_ref.refs_0_, bf16[768,128]{1,0:T(8,128)(2,1)S(1)} %far_project.3.refs_1_, bf16[768,128]{1,0:T(8,128)(2,1)S(1)} %collective-permute-done.21.refs_2_, bf16[768,128]{1,0:T(8,128)(2,1)S(1)} %collective-permute-done.22.refs_3_, ...), custom_call_target="tpu_custom_call" | custom-call | flops 805306368 | bytes 3407872 | tf_op jit(solution)/shard_map/down_project/pallas_call | solution.py:383
  164.3 5.5 %all-to-all-done.1 = bf16[64,8,1024]{2,1,0:T(8,128)(2,1)} async-done(((bf16[64,8,1024]{2,1,0:T(8,128)(2,1)}), bf16[64,8,1024]{2,1,0:T(8,128)(2,1)}, u32[]{:S(2)}, u32[]{:S(2)}) %all-to-all-start.1) | async-done | bytes 1048608 | tf_op jit(solution)/shard_map/all_to_all | solution.py:469
  169.9 6.2 %all-to-all-start.3 = ((bf16[64,8,1024]{2,1,0:T(8,128)(2,1)}), bf16[64,8,1024]{2,1,0:T(8,128)(2,1)S(1)}, u32[]{:S(2)}, u32[]{:S(2)}) async-start(bf16[64,8,1024]{2,1,0:T(8,128)(2,1)} %bitcast.27), calls=%async_computation.3 | async-start | bytes 2097152 | tf_op jit(solution)/shard_map/all_to_all | solution.py:469
  176.0 1.0 copy.14
  177.0 1.0 copy.15
  178.0 1.0 copy.16
  179.0 1.0 copy.17
  180.0 0.9 copy-done.1
  180.9 1.7 mix_in.2.total_ref
  182.7 21.5 %all-to-all-done.3 = bf16[64,8,1024]{2,1,0:T(8,128)(2,1)S(1)} async-done(((bf16[64,8,1024]{2,1,0:T(8,128)(2,1)}), bf16[64,8,1024]{2,1,0:T(8,128)(2,1)S(1)}, u32[]{:S(2)}, u32[]{:S(2)}) %all-to-all-start.3) | async-done | bytes 1048608 | tf_op jit(solution)/shard_map/all_to_all | solution.py:469
  204.2 1.4 mix_in.3
  (18 shorter events, 0.0 us)
Async XLA Ops:
  2.2 21.1 %copy-start = (bf16[2,192,4096]{2,1,0:T(8,128)(2,1)S(1)}, bf16[2,192,4096]{2,1,0:T(8,128)(2,1)}, u32[]{:S(2)}) copy-start(bf16[2,192,4096]{2,1,0:T(8,128)(2,1)} %refs_5_.5) | copy-start | bytes 9437188
  9.8 41.5 %all-to-all-start = ((bf16[64,8,1024]{2,1,0:T(8,128)(2,1)}), bf16[64,8,1024]{2,1,0:T(8,128)(2,1)}, u32[]{:S(2)}, u32[]{:S(2)}) async-start(bf16[64,8,1024]{2,1,0:T(8,128)(2,1)} %bitcast.29), calls=%async_computation | async-start | bytes 2097152 | tf_op jit(solution)/shard_map/all_to_all | solution.py:457
  24.9 11.6 %collective-permute-start = (bf16[1,192,1024]{2,1,0:T(8,128)(2,1)S(1)}, bf16[1,192,1024]{2,1,0:T(8,128)(2,1)S(1)}, u32[]{:S(2)}, u32[]{:S(2)}) collective-permute-start(bf16[1,192,1024]{2,1,0:T(8,128)(2,1)S(1)} %get-tuple-element.34), channel_id=1, source_target_pairs={{0,1},{1,2},{2,3},{3,0},{4,5},{5,6},{6,7},{7,4},{8,9},{9,10},{10,1... | collective-permute-start | bytes 1179656 | tf_op jit(solution)/shard_map/ppermute | solution.py:239
  26.1 35.6 %collective-permute-start.1 = (bf16[1,192,1024]{2,1,0:T(8,128)(2,1)}, bf16[1,192,1024]{2,1,0:T(8,128)(2,1)}, u32[]{:S(2)}, u32[]{:S(2)}) collective-permute-start(bf16[1,192,1024]{2,1,0:T(8,128)(2,1)} %get-tuple-element.35), channel_id=1, source_target_pairs={{0,3},{1,0},{2,1},{3,2},{4,7},{5,4},{6,5},{7,6},{8,11},{9,8},{10,9... | collective-permute-start | bytes 1179656 | tf_op jit(solution)/shard_map/ppermute | solution.py:240
  27.6 34.1 %collective-permute-start.2 = (bf16[1,192,1024]{2,1,0:T(8,128)(2,1)}, bf16[1,192,1024]{2,1,0:T(8,128)(2,1)}, u32[]{:S(2)}, u32[]{:S(2)}) collective-permute-start(bf16[1,192,1024]{2,1,0:T(8,128)(2,1)} %get-tuple-element.36), channel_id=1, source_target_pairs={{0,2},{1,3},{2,0},{3,1},{4,6},{5,7},{6,4},{7,5},{8,10},{9,11},{10,... | collective-permute-start | bytes 1179656 | tf_op jit(solution)/shard_map/ppermute | solution.py:241
  29.1 32.6 %collective-permute-start.3 = (bf16[1,192,1024]{2,1,0:T(8,128)(2,1)}, bf16[1,192,1024]{2,1,0:T(8,128)(2,1)S(1)}, u32[]{:S(2)}, u32[]{:S(2)}) collective-permute-start(bf16[1,192,1024]{2,1,0:T(8,128)(2,1)} %get-tuple-element.37), channel_id=1, source_target_pairs={{0,1},{1,2},{2,3},{3,0},{4,5},{5,6},{6,7},{7,4},{8,9},{9,10},{10,1... | collective-permute-start | bytes 1179656 | tf_op jit(solution)/shard_map/ppermute | solution.py:239
  29.4 32.3 %collective-permute-start.4 = (bf16[1,192,1024]{2,1,0:T(8,128)(2,1)}, bf16[1,192,1024]{2,1,0:T(8,128)(2,1)}, u32[]{:S(2)}, u32[]{:S(2)}) collective-permute-start(bf16[1,192,1024]{2,1,0:T(8,128)(2,1)} %get-tuple-element.38), channel_id=1, source_target_pairs={{0,3},{1,0},{2,1},{3,2},{4,7},{5,4},{6,5},{7,6},{8,11},{9,8},{10,9... | collective-permute-start | bytes 1179656 | tf_op jit(solution)/shard_map/ppermute | solution.py:240
  36.5 0.7 copy-start.2
  37.2 25.6 %collective-permute-start.5 = (bf16[1,192,1024]{2,1,0:T(8,128)(2,1)}, bf16[1,192,1024]{2,1,0:T(8,128)(2,1)}, u32[]{:S(2)}, u32[]{:S(2)}) collective-permute-start(bf16[1,192,1024]{2,1,0:T(8,128)(2,1)} %get-tuple-element.39), channel_id=1, source_target_pairs={{0,2},{1,3},{2,0},{3,1},{4,6},{5,7},{6,4},{7,5},{8,10},{9,11},{10,... | collective-permute-start | bytes 1179656 | tf_op jit(solution)/shard_map/ppermute | solution.py:241
  51.4 38.4 %all-to-all-start.2 = ((bf16[64,8,1024]{2,1,0:T(8,128)(2,1)}), bf16[64,8,1024]{2,1,0:T(8,128)(2,1)}, u32[]{:S(2)}, u32[]{:S(2)}) async-start(bf16[64,8,1024]{2,1,0:T(8,128)(2,1)} %bitcast.28), calls=%async_computation.2 | async-start | bytes 2097152 | tf_op jit(solution)/shard_map/all_to_all | solution.py:457
  65.1 13.7 %collective-permute-start.6 = (bf16[256,1024]{1,0:T(8,128)(2,1)}, bf16[256,1024]{1,0:T(8,128)(2,1)}, u32[]{:S(2)}, u32[]{:S(2)}) collective-permute-start(bf16[256,1024]{1,0:T(8,128)(2,1)} %get-tuple-element.40.own0), channel_id=1, source_target_pairs={{0,1},{1,2},{2,3},{3,0},{4,5},{5,6},{6,7},{7,4},{8,9},{9,10},{10,1... | collective-permute-start | bytes 1572872 | tf_op jit(solution)/shard_map/ppermute | solution.py:459
  65.8 12.9 %collective-permute-start.8 = (bf16[256,1024]{1,0:T(8,128)(2,1)}, bf16[256,1024]{1,0:T(8,128)(2,1)}, u32[]{:S(2)}, u32[]{:S(2)}) collective-permute-start(bf16[256,1024]{1,0:T(8,128)(2,1)} %get-tuple-element.41.own1), channel_id=1, source_target_pairs={{0,3},{1,0},{2,1},{3,2},{4,7},{5,4},{6,5},{7,6},{8,11},{9,8},{10,9... | collective-permute-start | bytes 1572872 | tf_op jit(solution)/shard_map/ppermute | solution.py:460
  67.8 24.3 %collective-permute-start.10 = (bf16[256,1024]{1,0:T(8,128)(2,1)}, bf16[256,1024]{1,0:T(8,128)(2,1)}, u32[]{:S(2)}, u32[]{:S(2)}) collective-permute-start(bf16[256,1024]{1,0:T(8,128)(2,1)} %get-tuple-element.41.own1), channel_id=1, source_target_pairs={{0,1},{1,2},{2,3},{3,0},{4,5},{5,6},{6,7},{7,4},{8,9},{9,10},{10,1... | collective-permute-start | bytes 1572872 | tf_op jit(solution)/shard_map/ppermute | solution.py:459
  67.8 27.7 %collective-permute-start.11 = (bf16[256,1024]{1,0:T(8,128)(2,1)}, bf16[256,1024]{1,0:T(8,128)(2,1)}, u32[]{:S(2)}, u32[]{:S(2)}) collective-permute-start(bf16[256,1024]{1,0:T(8,128)(2,1)} %get-tuple-element.40.own0), channel_id=1, source_target_pairs={{0,3},{1,0},{2,1},{3,2},{4,7},{5,4},{6,5},{7,6},{8,11},{9,8},{10,9... | collective-permute-start | bytes 1572872 | tf_op jit(solution)/shard_map/ppermute | solution.py:460
  78.8 22.5 %collective-permute-start.7 = (bf16[256,1024]{1,0:T(8,128)(2,1)}, bf16[256,1024]{1,0:T(8,128)(2,1)}, u32[]{:S(2)}, u32[]{:S(2)}) collective-permute-start(bf16[256,1024]{1,0:T(8,128)(2,1)} %collective-permute-done.6.left0), channel_id=1, source_target_pairs={{0,1},{1,2},{2,3},{3,0},{4,5},{5,6},{6,7},{7,4},{8,9},{9,10},{10,1... | collective-permute-start | bytes 1572872 | tf_op jit(solution)/shard_map/ppermute | solution.py:461
  78.8 22.5 %collective-permute-start.9 = (bf16[256,1024]{1,0:T(8,128)(2,1)}, bf16[256,1024]{1,0:T(8,128)(2,1)}, u32[]{:S(2)}, u32[]{:S(2)}) collective-permute-start(bf16[256,1024]{1,0:T(8,128)(2,1)} %collective-permute-done.8.right1), channel_id=1, source_target_pairs={{0,3},{1,0},{2,1},{3,2},{4,7},{5,4},{6,5},{7,6},{8,11},{9,8},{10,9... | collective-permute-start | bytes 1572872 | tf_op jit(solution)/shard_map/ppermute | solution.py:462
  92.0 20.4 %collective-permute-start.15 = (bf16[256,1024]{1,0:T(8,128)(2,1)}, bf16[256,1024]{1,0:T(8,128)(2,1)}, u32[]{:S(2)}, u32[]{:S(2)}) collective-permute-start(bf16[256,1024]{1,0:T(8,128)(2,1)} %get-tuple-element.48.own0), channel_id=1, source_target_pairs={{0,1},{1,2},{2,3},{3,0},{4,5},{5,6},{6,7},{7,4},{8,9},{9,10},{10,1... | collective-permute-start | bytes 1572872 | tf_op jit(solution)/shard_map/ppermute | solution.py:459
  92.0 20.4 %collective-permute-start.17 = (bf16[256,1024]{1,0:T(8,128)(2,1)}, bf16[256,1024]{1,0:T(8,128)(2,1)}, u32[]{:S(2)}, u32[]{:S(2)}) collective-permute-start(bf16[256,1024]{1,0:T(8,128)(2,1)} %get-tuple-element.49.own1), channel_id=1, source_target_pairs={{0,3},{1,0},{2,1},{3,2},{4,7},{5,4},{6,5},{7,6},{8,11},{9,8},{10,9... | collective-permute-start | bytes 1572872 | tf_op jit(solution)/shard_map/ppermute | solution.py:460
  103.7 13.5 %collective-permute-start.12 = (bf16[768,128]{1,0:T(8,128)(2,1)S(1)}, bf16[768,128]{1,0:T(8,128)(2,1)S(1)}, u32[]{:S(2)}, u32[]{:S(2)}) collective-permute-start(bf16[768,128]{1,0:T(8,128)(2,1)S(1)} %far_project.2.refs_1_), channel_id=1, source_target_pairs={{0,1},{1,2},{2,3},{3,0},{4,5},{5,6},{6,7},{7,4},{8,9},{9,10},{10,1... | collective-permute-start | bytes 589832 | tf_op jit(solution)/shard_map/ppermute | solution.py:239
  103.8 13.4 %collective-permute-start.13 = (bf16[768,128]{1,0:T(8,128)(2,1)S(1)}, bf16[768,128]{1,0:T(8,128)(2,1)S(1)}, u32[]{:S(2)}, u32[]{:S(2)}) collective-permute-start(bf16[768,128]{1,0:T(8,128)(2,1)S(1)} %far_project.2.refs_1_), channel_id=1, source_target_pairs={{0,3},{1,0},{2,1},{3,2},{4,7},{5,4},{6,5},{7,6},{8,11},{9,8},{10,9... | collective-permute-start | bytes 589832 | tf_op jit(solution)/shard_map/ppermute | solution.py:240
  106.5 13.6 %collective-permute-start.14 = (bf16[768,128]{1,0:T(8,128)(2,1)S(1)}, bf16[768,128]{1,0:T(8,128)(2,1)S(1)}, u32[]{:S(2)}, u32[]{:S(2)}) collective-permute-start(bf16[768,128]{1,0:T(8,128)(2,1)S(1)} %far_project.2.refs_1_), channel_id=1, source_target_pairs={{0,2},{1,3},{2,0},{3,1},{4,6},{5,7},{6,4},{7,5},{8,10},{9,11},{10,... | collective-permute-start | bytes 589832 | tf_op jit(solution)/shard_map/ppermute | solution.py:241
  112.5 29.3 %collective-permute-start.19 = (bf16[256,1024]{1,0:T(8,128)(2,1)}, bf16[256,1024]{1,0:T(8,128)(2,1)}, u32[]{:S(2)}, u32[]{:S(2)}) collective-permute-start(bf16[256,1024]{1,0:T(8,128)(2,1)} %get-tuple-element.49.own1), channel_id=1, source_target_pairs={{0,1},{1,2},{2,3},{3,0},{4,5},{5,6},{6,7},{7,4},{8,9},{9,10},{10,1... | collective-permute-start | bytes 1572872 | tf_op jit(solution)/shard_map/ppermute | solution.py:459
  112.5 29.4 %collective-permute-start.20 = (bf16[256,1024]{1,0:T(8,128)(2,1)}, bf16[256,1024]{1,0:T(8,128)(2,1)}, u32[]{:S(2)}, u32[]{:S(2)}) collective-permute-start(bf16[256,1024]{1,0:T(8,128)(2,1)} %get-tuple-element.48.own0), channel_id=1, source_target_pairs={{0,3},{1,0},{2,1},{3,2},{4,7},{5,4},{6,5},{7,6},{8,11},{9,8},{10,9... | collective-permute-start | bytes 1572872 | tf_op jit(solution)/shard_map/ppermute | solution.py:460
  117.2 29.7 %collective-permute-start.16 = (bf16[256,1024]{1,0:T(8,128)(2,1)}, bf16[256,1024]{1,0:T(8,128)(2,1)}, u32[]{:S(2)}, u32[]{:S(2)}) collective-permute-start(bf16[256,1024]{1,0:T(8,128)(2,1)} %collective-permute-done.15.left0), channel_id=1, source_target_pairs={{0,1},{1,2},{2,3},{3,0},{4,5},{5,6},{6,7},{7,4},{8,9},{9,10},{10,1... | collective-permute-start | bytes 1572872 | tf_op jit(solution)/shard_map/ppermute | solution.py:461
  117.2 29.7 %collective-permute-start.18 = (bf16[256,1024]{1,0:T(8,128)(2,1)}, bf16[256,1024]{1,0:T(8,128)(2,1)}, u32[]{:S(2)}, u32[]{:S(2)}) collective-permute-start(bf16[256,1024]{1,0:T(8,128)(2,1)} %collective-permute-done.17.right1), channel_id=1, source_target_pairs={{0,3},{1,0},{2,1},{3,2},{4,7},{5,4},{6,5},{7,6},{8,11},{9,8},{10,9... | collective-permute-start | bytes 1572872 | tf_op jit(solution)/shard_map/ppermute | solution.py:462
  123.6 46.2 %all-to-all-start.1 = ((bf16[64,8,1024]{2,1,0:T(8,128)(2,1)}), bf16[64,8,1024]{2,1,0:T(8,128)(2,1)}, u32[]{:S(2)}, u32[]{:S(2)}) async-start(bf16[64,8,1024]{2,1,0:T(8,128)(2,1)} %bitcast.26), calls=%async_computation.1 | async-start | bytes 2097152 | tf_op jit(solution)/shard_map/all_to_all | solution.py:469
  149.4 11.4 %collective-permute-start.21 = (bf16[768,128]{1,0:T(8,128)(2,1)S(1)}, bf16[768,128]{1,0:T(8,128)(2,1)S(1)}, u32[]{:S(2)}, u32[]{:S(2)}) collective-permute-start(bf16[768,128]{1,0:T(8,128)(2,1)S(1)} %far_project.3.refs_1_), channel_id=1, source_target_pairs={{0,1},{1,2},{2,3},{3,0},{4,5},{5,6},{6,7},{7,4},{8,9},{9,10},{10,1... | collective-permute-start | bytes 589832 | tf_op jit(solution)/shard_map/ppermute | solution.py:239
  149.5 11.3 %collective-permute-start.22 = (bf16[768,128]{1,0:T(8,128)(2,1)S(1)}, bf16[768,128]{1,0:T(8,128)(2,1)S(1)}, u32[]{:S(2)}, u32[]{:S(2)}) collective-permute-start(bf16[768,128]{1,0:T(8,128)(2,1)S(1)} %far_project.3.refs_1_), channel_id=1, source_target_pairs={{0,3},{1,0},{2,1},{3,2},{4,7},{5,4},{6,5},{7,6},{8,11},{9,8},{10,9... | collective-permute-start | bytes 589832 | tf_op jit(solution)/shard_map/ppermute | solution.py:240
  152.2 8.7 %collective-permute-start.23 = (bf16[768,128]{1,0:T(8,128)(2,1)S(1)}, bf16[768,128]{1,0:T(8,128)(2,1)S(1)}, u32[]{:S(2)}, u32[]{:S(2)}) collective-permute-start(bf16[768,128]{1,0:T(8,128)(2,1)S(1)} %far_project.3.refs_1_), channel_id=1, source_target_pairs={{0,2},{1,3},{2,0},{3,1},{4,6},{5,7},{6,4},{7,5},{8,10},{9,11},{10,... | collective-permute-start | bytes 589832 | tf_op jit(solution)/shard_map/ppermute | solution.py:241
  169.9 34.3 %all-to-all-start.3 = ((bf16[64,8,1024]{2,1,0:T(8,128)(2,1)}), bf16[64,8,1024]{2,1,0:T(8,128)(2,1)S(1)}, u32[]{:S(2)}, u32[]{:S(2)}) async-start(bf16[64,8,1024]{2,1,0:T(8,128)(2,1)} %bitcast.27), calls=%async_computation.3 | async-start | bytes 2097152 | tf_op jit(solution)/shard_map/all_to_all | solution.py:469
  180.0 1.0 copy-start.1

commit v4 on v3

--- a/solution.py
+++ b/solution.py
@@ -30,66 +30,85 @@
 dot = functools.partial(jnp.dot, preferred_element_type=F32)
 
 
-def route_kernel(ids_ref, probs_ref, *tables):
-    slots, rows = tables[0].shape
-    experts = EXP_DEV * slots // SLOTS
-    ids, probs = ids_ref[...], probs_ref[...]
-    mix = probs / jnp.sum(probs, axis=0, keepdims=True)
+def spread_of(slots, experts, j):
+    owner = lax.broadcasted_iota(jnp.int32, (slots, experts), 0) // SLOTS
+    expert = lax.broadcasted_iota(jnp.int32, (slots, experts), 1)
+    return jnp.where(expert == owner * EXP_DEV + j, 1.0, 0.0).astype(BF16)
+
+
+def chosen_of(spread, hits, earlier):
+    shape = (spread.shape[0], hits.shape[1])
+    slot = (lax.broadcasted_iota(jnp.int32, shape, 0) % SLOTS).astype(F32)
+    return (dot(spread, hits) > 0.5) & (dot(spread, earlier) == slot)
+
+
+def route_kernel(ids_ref, place_ref, hits_ref, earlier_ref):
+    slots, rows = place_ref.shape
+    experts = hits_ref.shape[0]
+    ids = ids_ref[...]
     line = lax.broadcasted_iota(jnp.int32, (experts, rows), 0)
     hits = jnp.zeros((experts, rows), F32)
-    mixed = jnp.zeros((experts, rows), F32)
     for k in range(TOPK):
-        same = ids[k : k + 1, :] == line
-        hits = hits + jnp.where(same, 1.0, 0.0)
-        mixed = mixed + jnp.where(same, mix[k : k + 1, :], 0.0)
+        hits = hits + jnp.where(ids[k : k + 1, :] == line, 1.0, 0.0)
     before = lax.broadcasted_iota(jnp.int32, (rows, rows), 0) < lax.broadcasted_iota(
         jnp.int32, (rows, rows), 1
     )
     hits = hits.astype(BF16)
     earlier = dot(hits, jnp.where(before, 1.0, 0.0).astype(BF16)).astype(BF16)
+    hits_ref[...], earlier_ref[...] = hits, earlier
+    chosen = chosen_of(spread_of(slots, experts, 0), hits, earlier)
+    place_ref[...] = jnp.where(chosen, 1.0, 0.0).astype(BF16)
+
+
+def weigh_kernel(ids_ref, probs_ref, hits_ref, earlier_ref, place_ref, *tables):
+    slots, rows = place_ref.shape
+    ids, probs = ids_ref[...], probs_ref[...]
+    hits, earlier = hits_ref[...], earlier_ref[...]
+    mix = probs / jnp.sum(probs, axis=0, keepdims=True)
+    line = lax.broadcasted_iota(jnp.int32, hits.shape, 0)
+    mixed = jnp.zeros(hits.shape, F32)
+    for k in range(TOPK):
+        mixed = mixed + jnp.where(ids[k : k + 1, :] == line, mix[k : k + 1, :], 0.0)
     mix_hi = mixed.astype(BF16)
     mix_lo = (mixed - mix_hi.astype(F32)).astype(BF16)
-    slot = (lax.broadcasted_iota(jnp.int32, (slots, rows), 0) % SLOTS).astype(F32)
-    owner = lax.broadcasted_iota(jnp.int32, (slots, experts), 0) // SLOTS
-    expert = lax.broadcasted_iota(jnp.int32, (slots, experts), 1)
-
-    def table(spread, tall):
-        return (dot(spread, hits) > 0.5) & (dot(spread, earlier) == tall)
-
     for j in range(EXP_DEV):
-        spread = jnp.where(expert == owner * EXP_DEV + j, 1.0, 0.0).astype(BF16)
-        chosen = table(spread, slot)
+        spread = spread_of(slots, hits.shape[0], j)
+        chosen = chosen_of(spread, hits, earlier)
         tables[j][...] = jnp.where(chosen, dot(spread, mix_hi), 0.0).astype(BF16)
         tables[2 + j][...] = jnp.where(chosen, dot(spread, mix_lo), 0.0).astype(BF16)
-        tables[4 + j][...] = jnp.where(chosen, 1.0, 0.0).astype(BF16)
+        if j == 1:
+            place_ref[...] = jnp.where(chosen, 1.0, 0.0).astype(BF16)
 
 
 def route(ids, probs, devices):
     rows = ids.shape[1]
     table = jax.ShapeDtypeStruct((devices * SLOTS, rows), BF16)
-
-    return pl.pallas_call(
+    count = jax.ShapeDtypeStruct((devices * EXP_DEV, rows), BF16)
+    place0, hits, earlier = pl.pallas_call(
         route_kernel,
-        in_specs=[VMEM, VMEM],
-        out_specs=[VMEM] * 6,
-        out_shape=[table] * 6,
-        cost_estimate=pl.CostEstimate(
-            flops=16 * devices * SLOTS * rows, bytes_accessed=0, transcendentals=0
-        ),
+        in_specs=[VMEM],
+        out_specs=[VMEM] * 3,
+        out_shape=[table, count, count],
         name="route",
-    )(ids, probs)
+    )(ids)
+    place1, hi0, hi1, lo0, lo1 = pl.pallas_call(
+        weigh_kernel,
+        in_specs=[VMEM] * 4,
+        out_specs=[VMEM] * 5,
+        out_shape=[table] * 5,
+        name="weigh",
+    )(ids, probs, hits, earlier)
+    return hi0, hi1, lo0, lo1, place0, place1
 
 
 def split_columns(me, w):
     count, hidden, width = w.shape
     part = width // N_TP
-    block = pl.BlockSpec((1, hidden // 2, part), lambda h, m: (0, h, 0))
-    shape = jax.ShapeDtypeStruct((1, hidden, part), w.dtype)
+    block = pl.BlockSpec((count, hidden // 2, part), lambda h, m: (0, h, 0))
 
     def kernel(me_ref, w_ref, *out_refs):
-        for e in range(count):
-            for turn in range(1, N_TP):
-                out_refs[e * (N_TP - 1) + turn - 1][0] = w_ref[e, :, columns(me_ref, turn, part)]
+        for turn, out_ref in enumerate(out_refs):
+            out_ref[...] = w_ref[:, :, columns(me_ref, turn + 1, part)]
 
     return pl.pallas_call(
         kernel,
@@ -97,9 +116,9 @@
             num_scalar_prefetch=1,
             grid=(2,),
             in_specs=[pl.BlockSpec((count, hidden // 2, width), lambda h, m: (0, h, 0))],
-            out_specs=[block] * (count * (N_TP - 1)),
-        ),
-        out_shape=[shape] * (count * (N_TP - 1)),
+            out_specs=[block] * (N_TP - 1),
+        ),
+        out_shape=[jax.ShapeDtypeStruct((count, hidden, part), w.dtype)] * (N_TP - 1),
         compiler_params=BIG,
         cost_estimate=pl.CostEstimate(flops=0, bytes_accessed=4 * w.size, transcendentals=0),
         name="split_columns",
@@ -374,7 +393,7 @@
     steps = 2
     piece = part // steps
     own = pl.BlockSpec((1, hidden, piece), lambda i, m: (expert, 0, m[0] * steps + i))
-    other = pl.BlockSpec((1, hidden, piece), lambda i, m: (0, 0, i))
+    other = pl.BlockSpec((1, hidden, piece), lambda i, m: (expert, 0, i))
 
     def kernel(*refs):
         head = 1 + 2 * N_TP
@@ -447,15 +466,14 @@
     swap = functools.partial(
         lax.all_to_all, axis_name=group, split_axis=0, concat_axis=0, tiled=True
     )
-    moved = [exchange(*blocks[: N_TP - 1]), exchange(*blocks[N_TP - 1 :])]
-    moved[0] = in_hbm(*moved[0])
+    moved = in_hbm(*exchange(*blocks))
     w_gate, w_up = in_hbm(w_gate, w_up)
     total = summed
     own = ()
     for expert, table, hi, lo in ((0, table0, hi0, lo0), (1, table1, hi1, lo1)):
         placed = place_rows(table, scaled)
         arrived = swap(placed.reshape(devices, SLOTS, part)).reshape(devices, 1, SLOTS, part)
-        own = pick(arrived, 0, PICK_WEIGHT[expert], *moved[0], *moved[1])
+        own = pick(arrived, 0, PICK_WEIGHT[expert], *moved[: 3 * expert])
         left = [lax.ppermute(half, "tp", RIGHT) for half in own]
         right = [lax.ppermute(half, "tp", LEFT) for half in own]
         low = lax.ppermute(left[0], "tp", RIGHT)
@@ -465,7 +483,7 @@
             me, low, high, sums, w_gate, w_up, inv_gain, expert, FAR_WEIGHT[expert]
         )
         packed = packed, *exchange(packed, packed, packed)
-        produced = down_project(me, packed, w_down, moved[expert], slots, expert)
+        produced = down_project(me, packed, w_down, moved, slots, expert)
         back = swap(produced.reshape(devices, SLOTS, part)).reshape(slots, part)
         total = mix_in(total, hi.T, lo.T, back, F32 if expert == 0 else BF16)
     return total

time: 206 us -> 200 us (0.971)
  starting transfers between devices: 79.1 us -> 63.3 us
  waiting for transfers between devices: 76.3 us -> 87 us
  local copies, waits for them, and re-layouts: 5.65 us -> 3.08 us
    ppermute x4 -> x3, waiting for transfers between devices: 15.4 us -> 2.53 us  [exchange(): lax.ppermute(for_right, 'tp', RIGHT)]
    ppermute x4 -> x3, waiting for transfers between devices: 1.08 us -> 8.91 us  [exchange(): lax.ppermute(for_across, 'tp', ACROSS)]
    all_to_all x2, waiting for transfers between devices: 18.6 us -> 26.2 us  [body(): swap(placed.reshape(devices, SLOTS, part)).reshape(devices, 1, SLOTS, part)]
    ppermute x4 -> x3, starting transfers between devices: 9.16 us -> 3.73 us  [exchange(): lax.ppermute(for_left, 'tp', LEFT)]
    all_to_all x2, starting transfers between devices: 24.3 us -> 19.2 us  [body(): back = swap(produced.reshape(devices, SLOTS, part)).reshape(slots, part)]
    ppermute x4 -> x3, waiting for transfers between devices: 0.01 us -> 4.56 us  [exchange(): lax.ppermute(for_left, 'tp', LEFT)]
    ppermute x4, starting transfers between devices: 9.95 us -> 5.51 us  [body(): right = [lax.ppermute(half, 'tp', LEFT) for half in own]]
    all_to_all x2, starting transfers between devices: 23.8 us -> 19.8 us  [body(): swap(placed.reshape(devices, SLOTS, part)).reshape(devices, 1, SLOTS, part)]
  transfers between devices with their start and end apart: 28 -> 25, of which waited for: 11 -> 12; matrix products, arithmetic and copies ran while one was open for 2% -> 2% of each run, Pallas kernels for 16% -> 17%
where the time goes in v4:
time: 200 us; the launch traced here: 199 us
  waiting for transfers between devices  87 us (44%)
  starting transfers between devices  63.3 us (32%)
  Pallas kernels  45.3 us (23%)
  local copies, waits for them, and re-layouts  3.08 us (2%)
    all_to_all x2, waiting for transfers between devices, body(): back = swap(produced.reshape(devices, SLOTS, part)).reshape(slots, part)  27.9 us
    all_to_all x2, waiting for transfers between devices, body(): swap(placed.reshape(devices, SLOTS, part)).reshape(devices, 1, SLOTS, part)  26.2 us
    all_to_all x2, starting transfers between devices, body(): swap(placed.reshape(devices, SLOTS, part)).reshape(devices, 1, SLOTS, part)  19.8 us
    all_to_all x2, starting transfers between devices, body(): back = swap(produced.reshape(devices, SLOTS, part)).reshape(slots, part)  19.2 us
    ppermute x4, waiting for transfers between devices, body(): left = [lax.ppermute(half, 'tp', RIGHT) for half in own]  15.5 us
    pallas_call x2, Pallas kernels, near_project(): pl.pallas_call(near_kernel, grid_spec=pltpu.PrefetchScalarGridSpec(num_sc...  10.1 us
    ppermute x3, waiting for transfers between devices, exchange(): lax.ppermute(for_across, 'tp', ACROSS)  8.91 us
    pallas_call x2, Pallas kernels, down_project(): pl.pallas_call(kernel, grid_spec=pltpu.PrefetchScalarGridSpec(num_scalar_...  7.15 us
  transfers between devices with their start and end apart: 25, of which 12 were waited for; matrix products, arithmetic and copies ran while one was open for 2% of the time, Pallas kernels for 17%

profile of v4, /device:TPU:1, one launch (start us, length us, event | category | flops | bytes accessed | tf_op | source)
XLA Modules:
  0.0 198.9 jit_solution(1741032471592185163)
XLA Ops:
  0.0 1.7 route.1
  1.7 5.3 %attention.1 = (f32[64,1024]{1,0:T(8,128)}, bf16[64,1024]{1,0:T(8,128)(2,1)}) custom-call(s32[64]{0:T(128)} %lens_ref.1, s32[1]{0:T(128)} %bitcast.me_ref.refs_0_, bf16[64,1024]{1,0:T(8,128)(2,1)} %refs_0_.1, bf16[64,128]{1,0:T(8,128)(2,1)} %refs_1_.1, bf16[64,128]{1,0:T(8,128)(2,1)} %refs_2_.1, bf16[64,128,128]{2,1,0:T(8,128)(2,1)} %refs_3_.1, ...), custom_call_target="tpu_custom_call" | custom-call | flops 33554432 | bytes 4194304 | tf_op jit(solution)/shard_map/attention/pallas_call | solution.py:183
  7.0 2.3 %place_rows.2 = bf16[512,1024]{1,0:T(8,128)(2,1)} custom-call(bf16[512,64]{1,0:T(8,128)(2,1)} %get-tuple-element.33.table_ref, bf16[64,1024]{1,0:T(8,128)(2,1)} %get-tuple-element.34.rows_ref), custom_call_target="tpu_custom_call" | custom-call | flops 67108864 | bytes 2097152 | tf_op jit(solution)/shard_map/place_rows/pallas_call | solution.py:211
  9.3 13.5 %all-to-all-start = ((bf16[64,8,1024]{2,1,0:T(8,128)(2,1)}), bf16[64,8,1024]{2,1,0:T(8,128)(2,1)}, u32[]{:S(2)}, u32[]{:S(2)}) async-start(bf16[64,8,1024]{2,1,0:T(8,128)(2,1)} %bitcast.27), calls=%async_computation | async-start | bytes 2097152 | tf_op jit(solution)/shard_map/all_to_all | solution.py:475
  22.8 1.8 split_columns.1
  24.6 1.2 collective-permute-start.9
  25.8 1.5 collective-permute-start.10
  27.2 1.5 collective-permute-start.11
  28.8 2.0 %weigh.1 = (bf16[512,64]{1,0:T(8,128)(2,1)}, bf16[512,64]{1,0:T(8,128)(2,1)}, bf16[512,64]{1,0:T(8,128)(2,1)}, bf16[512,64]{1,0:T(8,128)(2,1)}, bf16[512,64]{1,0:T(8,128)(2,1)}) custom-call(s32[8,64]{1,0:T(8,128)} %bitcast.32, f32[8,64]{1,0:T(8,128)} %bitcast.33, bf16[128,64]{1,0:T(8,128)(2,1)} %get-tuple-element.29.hits_ref, ...), custom_call_target="tpu_custom_call" | custom-call | tf_op jit(solution)/shard_map/weigh/pallas_call | solution.py:94
  30.8 2.3 %place_rows.3 = bf16[512,1024]{1,0:T(8,128)(2,1)} custom-call(bf16[512,64]{1,0:T(8,128)(2,1)} %get-tuple-element.45.table_ref, bf16[64,1024]{1,0:T(8,128)(2,1)} %get-tuple-element.34.rows_ref), custom_call_target="tpu_custom_call" | custom-call | flops 67108864 | bytes 2097152 | tf_op jit(solution)/shard_map/place_rows/pallas_call | solution.py:211
  33.1 17.8 %all-to-all-done = bf16[64,8,1024]{2,1,0:T(8,128)(2,1)} async-done(((bf16[64,8,1024]{2,1,0:T(8,128)(2,1)}), bf16[64,8,1024]{2,1,0:T(8,128)(2,1)}, u32[]{:S(2)}, u32[]{:S(2)}) %all-to-all-start) | async-done | bytes 1048608 | tf_op jit(solution)/shard_map/all_to_all | solution.py:475
  50.8 6.3 %all-to-all-start.2 = ((bf16[64,8,1024]{2,1,0:T(8,128)(2,1)}), bf16[64,8,1024]{2,1,0:T(8,128)(2,1)}, u32[]{:S(2)}, u32[]{:S(2)}) async-start(bf16[64,8,1024]{2,1,0:T(8,128)(2,1)} %bitcast.26), calls=%async_computation.2 | async-start | bytes 2097152 | tf_op jit(solution)/shard_map/all_to_all | solution.py:475
  57.2 2.3 %pick.2 = (bf16[256,1024]{1,0:T(8,128)(2,1)}, bf16[256,1024]{1,0:T(8,128)(2,1)}) custom-call(bf16[64,1,8,1024]{3,2,1,0:T(8,128)(2,1)} %bitcast.7.all_ref), custom_call_target="tpu_custom_call" | custom-call | flops 20000000000 | bytes 2097152 | tf_op jit(solution)/shard_map/pick/pallas_call | solution.py:237
  59.5 1.2 collective-permute-start
  60.7 1.5 collective-permute-start.2
  62.2 0.0 collective-permute-done.9.refs_6_.refs_0_
  62.2 1.3 collective-permute-start.5
  63.5 0.0 collective-permute-done.10.refs_7_.refs_1_
  63.5 0.2 collective-permute-start.4
  63.7 10.4 %collective-permute-done.left0 = bf16[256,1024]{1,0:T(8,128)(2,1)} collective-permute-done((bf16[256,1024]{1,0:T(8,128)(2,1)}, bf16[256,1024]{1,0:T(8,128)(2,1)}, u32[]{:S(2)}, u32[]{:S(2)}) %collective-permute-start) | collective-permute-done | bytes 524320 | tf_op jit(solution)/shard_map/ppermute | solution.py:477
  74.1 0.0 collective-permute-start.1
  74.1 0.0 collective-permute-done.2.right1
  74.1 2.7 %collective-permute-start.3 = (bf16[256,1024]{1,0:T(8,128)(2,1)}, bf16[256,1024]{1,0:T(8,128)(2,1)}, u32[]{:S(2)}, u32[]{:S(2)}) collective-permute-start(bf16[256,1024]{1,0:T(8,128)(2,1)} %collective-permute-done.2.right1), channel_id=1, source_target_pairs={{0,3},{1,0},{2,1},{3,2},{4,7},{5,4},{6,5},{7,6},{8,11},{9,8},{10,9... | collective-permute-start | bytes 1572872 | tf_op jit(solution)/shard_map/ppermute | solution.py:480
  76.8 0.0 collective-permute-done.11.refs_8_.refs_2_
  76.8 8.5 %all-to-all-done.2 = bf16[64,8,1024]{2,1,0:T(8,128)(2,1)} async-done(((bf16[64,8,1024]{2,1,0:T(8,128)(2,1)}), bf16[64,8,1024]{2,1,0:T(8,128)(2,1)}, u32[]{:S(2)}, u32[]{:S(2)}) %all-to-all-start.2) | async-done | bytes 1048608 | tf_op jit(solution)/shard_map/all_to_all | solution.py:475
  85.2 2.2 %pick.3 = (bf16[256,1024]{1,0:T(8,128)(2,1)}, bf16[256,1024]{1,0:T(8,128)(2,1)}) custom-call(bf16[64,1,8,1024]{3,2,1,0:T(8,128)(2,1)} %bitcast.14.all_ref, bf16[2,192,1024]{2,1,0:T(8,128)(2,1)} %collective-permute-done.9.refs_6_.refs_0_, bf16[2,192,1024]{2,1,0:T(8,128)(2,1)} %collective-permute-done.10.refs_7_.refs_1_, ...), custom_call_target="tpu_custom_call" | custom-call | bytes 2097152 | tf_op jit(solution)/shard_map/pick/pallas_call | solution.py:237
  87.5 1.2 collective-permute-start.12
  88.7 0.0 collective-permute-done.5.right0
  88.7 1.5 collective-permute-start.14
  90.2 0.0 collective-permute-done.4.left1
  90.2 5.1 %near_project.2 = (f32[512,192]{1,0:T(8,128)S(1)}, f32[512,192]{1,0:T(8,128)S(1)}, f32[512,128]{1,0:T(8,128)S(1)}) custom-call(s32[1]{0:T(128)} %bitcast.me_ref.refs_0_, bf16[256,1024]{1,0:T(8,128)(2,1)} %get-tuple-element.35.own0, bf16[256,1024]{1,0:T(8,128)(2,1)} %get-tuple-element.36.own1, bf16[256,1024]{1,0:T(8,128)(2,1)} %collective-permute-done.left0, ...), custom_call_target="tpu_custom_call" | custom-call | flops 1207959552 | bytes 7340032 | tf_op jit(solution)/shard_map/near_project/pallas_call | solution.py:319
  95.3 1.3 collective-permute-done.1.low
  96.6 2.5 %far_project.2.refs_1_ = bf16[768,128]{1,0:T(8,128)(2,1)S(1)} custom-call(s32[1]{0:T(128)} %bitcast.me_ref.refs_0_, bf16[256,1024]{1,0:T(8,128)(2,1)} %collective-permute-done.1.low, bf16[256,1024]{1,0:T(8,128)(2,1)} %collective-permute-done.3.high, f32[512,192]{1,0:T(8,128)S(1)} %get-tuple-element.37.gate_in, f32[512,192]{1,0:T(8,128)S(1)} %get-tuple-element.38.up_in, ...), custom_call_target="tpu_custom_call" | custom-call | flops 1000000000 | bytes 4194304 | tf_op jit(solution)/shard_map/far_project/pallas_call | solution.py:353
  99.1 2.2 %collective-permute-start.8 = (bf16[768,128]{1,0:T(8,128)(2,1)S(1)}, bf16[768,128]{1,0:T(8,128)(2,1)S(1)}, u32[]{:S(2)}, u32[]{:S(2)}) collective-permute-start(bf16[768,128]{1,0:T(8,128)(2,1)S(1)} %far_project.2.refs_1_), channel_id=1, source_target_pairs={{0,2},{1,3},{2,0},{3,1},{4,6},{5,7},{6,4},{7,5},{8,10},{9,11},{10,... | collective-permute-start | bytes 589832 | tf_op jit(solution)/shard_map/ppermute | solution.py:260
  101.3 1.2 collective-permute-start.7
  102.4 0.3 collective-permute-start.6
  102.7 5.1 %collective-permute-done.12.left0 = bf16[256,1024]{1,0:T(8,128)(2,1)} collective-permute-done((bf16[256,1024]{1,0:T(8,128)(2,1)}, bf16[256,1024]{1,0:T(8,128)(2,1)}, u32[]{:S(2)}, u32[]{:S(2)}) %collective-permute-start.12) | collective-permute-done | bytes 524320 | tf_op jit(solution)/shard_map/ppermute | solution.py:477
  107.8 1.3 collective-permute-start.17
  109.1 0.0 collective-permute-done.14.right1
  109.1 0.2 collective-permute-start.16
  109.3 3.7 %collective-permute-done.8.refs_4_ = bf16[768,128]{1,0:T(8,128)(2,1)S(1)} collective-permute-done((bf16[768,128]{1,0:T(8,128)(2,1)S(1)}, bf16[768,128]{1,0:T(8,128)(2,1)S(1)}, u32[]{:S(2)}, u32[]{:S(2)}) %collective-permute-start.8) | collective-permute-done | bytes 196640 | tf_op jit(solution)/shard_map/ppermute | solution.py:260
  112.9 0.5 collective-permute-start.13
  113.5 2.4 %collective-permute-done.7.refs_3_ = bf16[768,128]{1,0:T(8,128)(2,1)S(1)} collective-permute-done((bf16[768,128]{1,0:T(8,128)(2,1)S(1)}, bf16[768,128]{1,0:T(8,128)(2,1)S(1)}, u32[]{:S(2)}, u32[]{:S(2)}) %collective-permute-start.7) | collective-permute-done | bytes 196640 | tf_op jit(solution)/shard_map/ppermute | solution.py:259
  115.8 2.6 %collective-permute-start.15 = (bf16[256,1024]{1,0:T(8,128)(2,1)}, bf16[256,1024]{1,0:T(8,128)(2,1)}, u32[]{:S(2)}, u32[]{:S(2)}) collective-permute-start(bf16[256,1024]{1,0:T(8,128)(2,1)} %collective-permute-done.14.right1), channel_id=1, source_target_pairs={{0,3},{1,0},{2,1},{3,2},{4,7},{5,4},{6,5},{7,6},{8,11},{9,8},{10,9... | collective-permute-start | bytes 1572872 | tf_op jit(solution)/shard_map/ppermute | solution.py:480
  118.5 3.6 %down_project.2 = bf16[512,1024]{1,0:T(8,128)(2,1)} custom-call(s32[1]{0:T(128)} %bitcast.me_ref.refs_0_, bf16[768,128]{1,0:T(8,128)(2,1)S(1)} %far_project.2.refs_1_, bf16[768,128]{1,0:T(8,128)(2,1)S(1)} %collective-permute-done.6.refs_2_, bf16[768,128]{1,0:T(8,128)(2,1)S(1)} %collective-permute-done.7.refs_3_, ...), custom_call_target="tpu_custom_call" | custom-call | flops 805306368 | bytes 3407872 | tf_op jit(solution)/shard_map/down_project/pallas_call | solution.py:402
  122.1 13.0 %all-to-all-start.1 = ((bf16[64,8,1024]{2,1,0:T(8,128)(2,1)}), bf16[64,8,1024]{2,1,0:T(8,128)(2,1)}, u32[]{:S(2)}, u32[]{:S(2)}) async-start(bf16[64,8,1024]{2,1,0:T(8,128)(2,1)} %bitcast.28), calls=%async_computation.1 | async-start | bytes 2097152 | tf_op jit(solution)/shard_map/all_to_all | solution.py:487
  135.1 5.1 %near_project.3 = (f32[512,192]{1,0:T(8,128)S(1)}, f32[512,192]{1,0:T(8,128)S(1)}, f32[512,128]{1,0:T(8,128)S(1)}) custom-call(s32[1]{0:T(128)} %bitcast.me_ref.refs_0_, bf16[256,1024]{1,0:T(8,128)(2,1)} %get-tuple-element.46.own0, bf16[256,1024]{1,0:T(8,128)(2,1)} %get-tuple-element.47.own1, bf16[256,1024]{1,0:T(8,128)(2,1)} %collective-permute-done.12.left0, ...), custom_call_target="tpu_custom_call" | custom-call | flops 1207959552 | bytes 7340032 | tf_op jit(solution)/shard_map/near_project/pallas_call | solution.py:319
  140.2 2.5 %far_project.3.refs_1_ = bf16[768,128]{1,0:T(8,128)(2,1)S(1)} custom-call(s32[1]{0:T(128)} %bitcast.me_ref.refs_0_, bf16[256,1024]{1,0:T(8,128)(2,1)} %collective-permute-done.13.low, bf16[256,1024]{1,0:T(8,128)(2,1)} %collective-permute-done.15.high, f32[512,192]{1,0:T(8,128)S(1)} %get-tuple-element.48.gate_in, f32[512,192]{1,0:T(8,128)S(1)} %get-tuple-element.49.up_in, ...), custom_call_target="tpu_custom_call" | custom-call | flops 14000000000 | bytes 4194304 | tf_op jit(solution)/shard_map/far_project/pallas_call | solution.py:353
  142.7 0.8 collective-permute-start.20
  143.5 1.1 collective-permute-start.19
  144.6 0.4 collective-permute-start.18
  144.9 5.2 %collective-permute-done.20.refs_4_ = bf16[768,128]{1,0:T(8,128)(2,1)S(1)} collective-permute-done((bf16[768,128]{1,0:T(8,128)(2,1)S(1)}, bf16[768,128]{1,0:T(8,128)(2,1)S(1)}, u32[]{:S(2)}, u32[]{:S(2)}) %collective-permute-start.20) | collective-permute-done | bytes 196640 | tf_op jit(solution)/shard_map/ppermute | solution.py:260
  150.2 2.2 %collective-permute-done.19.refs_3_ = bf16[768,128]{1,0:T(8,128)(2,1)S(1)} collective-permute-done((bf16[768,128]{1,0:T(8,128)(2,1)S(1)}, bf16[768,128]{1,0:T(8,128)(2,1)S(1)}, u32[]{:S(2)}, u32[]{:S(2)}) %collective-permute-start.19) | collective-permute-done | bytes 196640 | tf_op jit(solution)/shard_map/ppermute | solution.py:259
  152.4 2.5 %collective-permute-done.18.refs_2_ = bf16[768,128]{1,0:T(8,128)(2,1)S(1)} collective-permute-done((bf16[768,128]{1,0:T(8,128)(2,1)S(1)}, bf16[768,128]{1,0:T(8,128)(2,1)S(1)}, u32[]{:S(2)}, u32[]{:S(2)}) %collective-permute-start.18) | collective-permute-done | bytes 196640 | tf_op jit(solution)/shard_map/ppermute | solution.py:258
  154.9 3.6 %down_project.3 = bf16[512,1024]{1,0:T(8,128)(2,1)} custom-call(s32[1]{0:T(128)} %bitcast.me_ref.refs_0_, bf16[768,128]{1,0:T(8,128)(2,1)S(1)} %far_project.3.refs_1_, bf16[768,128]{1,0:T(8,128)(2,1)S(1)} %collective-permute-done.18.refs_2_, bf16[768,128]{1,0:T(8,128)(2,1)S(1)} %collective-permute-done.19.refs_3_, ...), custom_call_target="tpu_custom_call" | custom-call | flops 805306368 | bytes 3407872 | tf_op jit(solution)/shard_map/down_project/pallas_call | solution.py:402
  158.5 4.6 %all-to-all-done.1 = bf16[64,8,1024]{2,1,0:T(8,128)(2,1)} async-done(((bf16[64,8,1024]{2,1,0:T(8,128)(2,1)}), bf16[64,8,1024]{2,1,0:T(8,128)(2,1)}, u32[]{:S(2)}, u32[]{:S(2)}) %all-to-all-start.1) | async-done | bytes 1048608 | tf_op jit(solution)/shard_map/all_to_all | solution.py:487
  163.1 6.3 %all-to-all-start.3 = ((bf16[64,8,1024]{2,1,0:T(8,128)(2,1)}), bf16[64,8,1024]{2,1,0:T(8,128)(2,1)S(1)}, u32[]{:S(2)}, u32[]{:S(2)}) async-start(bf16[64,8,1024]{2,1,0:T(8,128)(2,1)} %bitcast.29), calls=%async_computation.3 | async-start | bytes 2097152 | tf_op jit(solution)/shard_map/all_to_all | solution.py:487
  169.4 1.0 copy.14
  170.4 1.0 copy.15
  171.4 1.0 copy.16
  172.4 0.1 copy.17
  172.5 1.7 mix_in.2.total_ref
  174.2 23.3 %all-to-all-done.3 = bf16[64,8,1024]{2,1,0:T(8,128)(2,1)S(1)} async-done(((bf16[64,8,1024]{2,1,0:T(8,128)(2,1)}), bf16[64,8,1024]{2,1,0:T(8,128)(2,1)S(1)}, u32[]{:S(2)}, u32[]{:S(2)}) %all-to-all-start.3) | async-done | bytes 1048608 | tf_op jit(solution)/shard_map/all_to_all | solution.py:487
  197.5 1.3 mix_in.3
  (15 shorter events, 0.0 us)
Async XLA Ops:
  1.7 21.1 %copy-start = (bf16[2,192,4096]{2,1,0:T(8,128)(2,1)S(1)}, bf16[2,192,4096]{2,1,0:T(8,128)(2,1)}, u32[]{:S(2)}) copy-start(bf16[2,192,4096]{2,1,0:T(8,128)(2,1)} %refs_5_.5) | copy-start | bytes 9437188
  9.3 41.5 %all-to-all-start = ((bf16[64,8,1024]{2,1,0:T(8,128)(2,1)}), bf16[64,8,1024]{2,1,0:T(8,128)(2,1)}, u32[]{:S(2)}, u32[]{:S(2)}) async-start(bf16[64,8,1024]{2,1,0:T(8,128)(2,1)} %bitcast.27), calls=%async_computation | async-start | bytes 2097152 | tf_op jit(solution)/shard_map/all_to_all | solution.py:475
  24.6 37.6 %collective-permute-start.9 = (bf16[2,192,1024]{2,1,0:T(8,128)(2,1)}, bf16[2,192,1024]{2,1,0:T(8,128)(2,1)}, u32[]{:S(2)}, u32[]{:S(2)}) collective-permute-start(bf16[2,192,1024]{2,1,0:T(8,128)(2,1)} %get-tuple-element.40), channel_id=1, source_target_pairs={{0,1},{1,2},{2,3},{3,0},{4,5},{5,6},{6,7},{7,4},{8,9},{9,10},{10,1... | collective-permute-start | bytes 2359304 | tf_op jit(solution)/shard_map/ppermute | solution.py:258
  25.8 37.7 %collective-permute-start.10 = (bf16[2,192,1024]{2,1,0:T(8,128)(2,1)}, bf16[2,192,1024]{2,1,0:T(8,128)(2,1)}, u32[]{:S(2)}, u32[]{:S(2)}) collective-permute-start(bf16[2,192,1024]{2,1,0:T(8,128)(2,1)} %get-tuple-element.41), channel_id=1, source_target_pairs={{0,3},{1,0},{2,1},{3,2},{4,7},{5,4},{6,5},{7,6},{8,11},{9,8},{10,9... | collective-permute-start | bytes 2359304 | tf_op jit(solution)/shard_map/ppermute | solution.py:259
  27.2 49.5 %collective-permute-start.11 = (bf16[2,192,1024]{2,1,0:T(8,128)(2,1)}, bf16[2,192,1024]{2,1,0:T(8,128)(2,1)}, u32[]{:S(2)}, u32[]{:S(2)}) collective-permute-start(bf16[2,192,1024]{2,1,0:T(8,128)(2,1)} %get-tuple-element.42), channel_id=1, source_target_pairs={{0,2},{1,3},{2,0},{3,1},{4,6},{5,7},{6,4},{7,5},{8,10},{9,11},{10,... | collective-permute-start | bytes 2359304 | tf_op jit(solution)/shard_map/ppermute | solution.py:260
  50.8 34.4 %all-to-all-start.2 = ((bf16[64,8,1024]{2,1,0:T(8,128)(2,1)}), bf16[64,8,1024]{2,1,0:T(8,128)(2,1)}, u32[]{:S(2)}, u32[]{:S(2)}) async-start(bf16[64,8,1024]{2,1,0:T(8,128)(2,1)} %bitcast.26), calls=%async_computation.2 | async-start | bytes 2097152 | tf_op jit(solution)/shard_map/all_to_all | solution.py:475
  59.5 30.7 %copy-start.3 = (f32[4096]{0:T(1024)S(1)}, f32[4096]{0:T(1024)}, u32[]{:S(2)}) copy-start(f32[4096]{0:T(1024)} %param.20) | copy-start | bytes 49156
  59.5 14.6 %collective-permute-start = (bf16[256,1024]{1,0:T(8,128)(2,1)}, bf16[256,1024]{1,0:T(8,128)(2,1)}, u32[]{:S(2)}, u32[]{:S(2)}) collective-permute-start(bf16[256,1024]{1,0:T(8,128)(2,1)} %get-tuple-element.35.own0), channel_id=1, source_target_pairs={{0,1},{1,2},{2,3},{3,0},{4,5},{5,6},{6,7},{7,4},{8,9},{9,10},{10,1... | collective-permute-start | bytes 1572872 | tf_op jit(solution)/shard_map/ppermute | solution.py:477
  60.7 13.4 %collective-permute-start.2 = (bf16[256,1024]{1,0:T(8,128)(2,1)}, bf16[256,1024]{1,0:T(8,128)(2,1)}, u32[]{:S(2)}, u32[]{:S(2)}) collective-permute-start(bf16[256,1024]{1,0:T(8,128)(2,1)} %get-tuple-element.36.own1), channel_id=1, source_target_pairs={{0,3},{1,0},{2,1},{3,2},{4,7},{5,4},{6,5},{7,6},{8,11},{9,8},{10,9... | collective-permute-start | bytes 1572872 | tf_op jit(solution)/shard_map/ppermute | solution.py:478
  62.2 26.5 %collective-permute-start.5 = (bf16[256,1024]{1,0:T(8,128)(2,1)}, bf16[256,1024]{1,0:T(8,128)(2,1)}, u32[]{:S(2)}, u32[]{:S(2)}) collective-permute-start(bf16[256,1024]{1,0:T(8,128)(2,1)} %get-tuple-element.35.own0), channel_id=1, source_target_pairs={{0,3},{1,0},{2,1},{3,2},{4,7},{5,4},{6,5},{7,6},{8,11},{9,8},{10,9... | collective-permute-start | bytes 1572872 | tf_op jit(solution)/shard_map/ppermute | solution.py:478
  63.5 26.7 %collective-permute-start.4 = (bf16[256,1024]{1,0:T(8,128)(2,1)}, bf16[256,1024]{1,0:T(8,128)(2,1)}, u32[]{:S(2)}, u32[]{:S(2)}) collective-permute-start(bf16[256,1024]{1,0:T(8,128)(2,1)} %get-tuple-element.36.own1), channel_id=1, source_target_pairs={{0,1},{1,2},{2,3},{3,0},{4,5},{5,6},{6,7},{7,4},{8,9},{9,10},{10,1... | collective-permute-start | bytes 1572872 | tf_op jit(solution)/shard_map/ppermute | solution.py:477
  74.1 22.5 %collective-permute-start.1 = (bf16[256,1024]{1,0:T(8,128)(2,1)}, bf16[256,1024]{1,0:T(8,128)(2,1)}, u32[]{:S(2)}, u32[]{:S(2)}) collective-permute-start(bf16[256,1024]{1,0:T(8,128)(2,1)} %collective-permute-done.left0), channel_id=1, source_target_pairs={{0,1},{1,2},{2,3},{3,0},{4,5},{5,6},{6,7},{7,4},{8,9},{9,10},{10,1... | collective-permute-start | bytes 1572872 | tf_op jit(solution)/shard_map/ppermute | solution.py:479
  74.1 22.5 %collective-permute-start.3 = (bf16[256,1024]{1,0:T(8,128)(2,1)}, bf16[256,1024]{1,0:T(8,128)(2,1)}, u32[]{:S(2)}, u32[]{:S(2)}) collective-permute-start(bf16[256,1024]{1,0:T(8,128)(2,1)} %collective-permute-done.2.right1), channel_id=1, source_target_pairs={{0,3},{1,0},{2,1},{3,2},{4,7},{5,4},{6,5},{7,6},{8,11},{9,8},{10,9... | collective-permute-start | bytes 1572872 | tf_op jit(solution)/shard_map/ppermute | solution.py:480
  87.5 20.3 %collective-permute-start.12 = (bf16[256,1024]{1,0:T(8,128)(2,1)}, bf16[256,1024]{1,0:T(8,128)(2,1)}, u32[]{:S(2)}, u32[]{:S(2)}) collective-permute-start(bf16[256,1024]{1,0:T(8,128)(2,1)} %get-tuple-element.46.own0), channel_id=1, source_target_pairs={{0,1},{1,2},{2,3},{3,0},{4,5},{5,6},{6,7},{7,4},{8,9},{9,10},{10,1... | collective-permute-start | bytes 1572872 | tf_op jit(solution)/shard_map/ppermute | solution.py:477
  88.7 20.4 %collective-permute-start.14 = (bf16[256,1024]{1,0:T(8,128)(2,1)}, bf16[256,1024]{1,0:T(8,128)(2,1)}, u32[]{:S(2)}, u32[]{:S(2)}) collective-permute-start(bf16[256,1024]{1,0:T(8,128)(2,1)} %get-tuple-element.47.own1), channel_id=1, source_target_pairs={{0,3},{1,0},{2,1},{3,2},{4,7},{5,4},{6,5},{7,6},{8,11},{9,8},{10,9... | collective-permute-start | bytes 1572872 | tf_op jit(solution)/shard_map/ppermute | solution.py:478
  99.1 13.9 %collective-permute-start.8 = (bf16[768,128]{1,0:T(8,128)(2,1)S(1)}, bf16[768,128]{1,0:T(8,128)(2,1)S(1)}, u32[]{:S(2)}, u32[]{:S(2)}) collective-permute-start(bf16[768,128]{1,0:T(8,128)(2,1)S(1)} %far_project.2.refs_1_), channel_id=1, source_target_pairs={{0,2},{1,3},{2,0},{3,1},{4,6},{5,7},{6,4},{7,5},{8,10},{9,11},{10,... | collective-permute-start | bytes 589832 | tf_op jit(solution)/shard_map/ppermute | solution.py:260
  101.3 14.6 %collective-permute-start.7 = (bf16[768,128]{1,0:T(8,128)(2,1)S(1)}, bf16[768,128]{1,0:T(8,128)(2,1)S(1)}, u32[]{:S(2)}, u32[]{:S(2)}) collective-permute-start(bf16[768,128]{1,0:T(8,128)(2,1)S(1)} %far_project.2.refs_1_), channel_id=1, source_target_pairs={{0,3},{1,0},{2,1},{3,2},{4,7},{5,4},{6,5},{7,6},{8,11},{9,8},{10,9... | collective-permute-start | bytes 589832 | tf_op jit(solution)/shard_map/ppermute | solution.py:259
  102.4 16.1 %collective-permute-start.6 = (bf16[768,128]{1,0:T(8,128)(2,1)S(1)}, bf16[768,128]{1,0:T(8,128)(2,1)S(1)}, u32[]{:S(2)}, u32[]{:S(2)}) collective-permute-start(bf16[768,128]{1,0:T(8,128)(2,1)S(1)} %far_project.2.refs_1_), channel_id=1, source_target_pairs={{0,1},{1,2},{2,3},{3,0},{4,5},{5,6},{6,7},{7,4},{8,9},{9,10},{10,1... | collective-permute-start | bytes 589832 | tf_op jit(solution)/shard_map/ppermute | solution.py:258
  107.8 27.3 %collective-permute-start.17 = (bf16[256,1024]{1,0:T(8,128)(2,1)}, bf16[256,1024]{1,0:T(8,128)(2,1)}, u32[]{:S(2)}, u32[]{:S(2)}) collective-permute-start(bf16[256,1024]{1,0:T(8,128)(2,1)} %get-tuple-element.46.own0), channel_id=1, source_target_pairs={{0,3},{1,0},{2,1},{3,2},{4,7},{5,4},{6,5},{7,6},{8,11},{9,8},{10,9... | collective-permute-start | bytes 1572872 | tf_op jit(solution)/shard_map/ppermute | solution.py:478
  109.1 26.0 %collective-permute-start.16 = (bf16[256,1024]{1,0:T(8,128)(2,1)}, bf16[256,1024]{1,0:T(8,128)(2,1)}, u32[]{:S(2)}, u32[]{:S(2)}) collective-permute-start(bf16[256,1024]{1,0:T(8,128)(2,1)} %get-tuple-element.47.own1), channel_id=1, source_target_pairs={{0,1},{1,2},{2,3},{3,0},{4,5},{5,6},{6,7},{7,4},{8,9},{9,10},{10,1... | collective-permute-start | bytes 1572872 | tf_op jit(solution)/shard_map/ppermute | solution.py:477
  112.9 27.2 %collective-permute-start.13 = (bf16[256,1024]{1,0:T(8,128)(2,1)}, bf16[256,1024]{1,0:T(8,128)(2,1)}, u32[]{:S(2)}, u32[]{:S(2)}) collective-permute-start(bf16[256,1024]{1,0:T(8,128)(2,1)} %collective-permute-done.12.left0), channel_id=1, source_target_pairs={{0,1},{1,2},{2,3},{3,0},{4,5},{5,6},{6,7},{7,4},{8,9},{9,10},{10,1... | collective-permute-start | bytes 1572872 | tf_op jit(solution)/shard_map/ppermute | solution.py:479
  115.8 24.3 %collective-permute-start.15 = (bf16[256,1024]{1,0:T(8,128)(2,1)}, bf16[256,1024]{1,0:T(8,128)(2,1)}, u32[]{:S(2)}, u32[]{:S(2)}) collective-permute-start(bf16[256,1024]{1,0:T(8,128)(2,1)} %collective-permute-done.14.right1), channel_id=1, source_target_pairs={{0,3},{1,0},{2,1},{3,2},{4,7},{5,4},{6,5},{7,6},{8,11},{9,8},{10,9... | collective-permute-start | bytes 1572872 | tf_op jit(solution)/shard_map/ppermute | solution.py:480
  122.1 41.0 %all-to-all-start.1 = ((bf16[64,8,1024]{2,1,0:T(8,128)(2,1)}), bf16[64,8,1024]{2,1,0:T(8,128)(2,1)}, u32[]{:S(2)}, u32[]{:S(2)}) async-start(bf16[64,8,1024]{2,1,0:T(8,128)(2,1)} %bitcast.28), calls=%async_computation.1 | async-start | bytes 2097152 | tf_op jit(solution)/shard_map/all_to_all | solution.py:487
  142.7 29.7 %copy-start.2 = (bf16[512,64]{1,0:T(8,128)(2,1)S(1)}, bf16[512,64]{1,0:T(8,128)(2,1)}, u32[]{:S(2)}) copy-start(bf16[512,64]{1,0:T(8,128)(2,1)} %get-tuple-element.44) | copy-start | bytes 196612
  142.7 29.8 %copy-start.1 = (f32[64,1024]{1,0:T(8,128)S(1)}, f32[64,1024]{1,0:T(8,128)}, u32[]{:S(2)}) copy-start(f32[64,1024]{1,0:T(8,128)} %get-tuple-element.28.total_ref) | copy-start | bytes 786436
  142.7 7.5 %collective-permute-start.20 = (bf16[768,128]{1,0:T(8,128)(2,1)S(1)}, bf16[768,128]{1,0:T(8,128)(2,1)S(1)}, u32[]{:S(2)}, u32[]{:S(2)}) collective-permute-start(bf16[768,128]{1,0:T(8,128)(2,1)S(1)} %far_project.3.refs_1_), channel_id=1, source_target_pairs={{0,2},{1,3},{2,0},{3,1},{4,6},{5,7},{6,4},{7,5},{8,10},{9,11},{10,... | collective-permute-start | bytes 589832 | tf_op jit(solution)/shard_map/ppermute | solution.py:260
  143.5 8.9 %collective-permute-start.19 = (bf16[768,128]{1,0:T(8,128)(2,1)S(1)}, bf16[768,128]{1,0:T(8,128)(2,1)S(1)}, u32[]{:S(2)}, u32[]{:S(2)}) collective-permute-start(bf16[768,128]{1,0:T(8,128)(2,1)S(1)} %far_project.3.refs_1_), channel_id=1, source_target_pairs={{0,3},{1,0},{2,1},{3,2},{4,7},{5,4},{6,5},{7,6},{8,11},{9,8},{10,9... | collective-permute-start | bytes 589832 | tf_op jit(solution)/shard_map/ppermute | solution.py:259
  144.6 10.3 %collective-permute-start.18 = (bf16[768,128]{1,0:T(8,128)(2,1)S(1)}, bf16[768,128]{1,0:T(8,128)(2,1)S(1)}, u32[]{:S(2)}, u32[]{:S(2)}) collective-permute-start(bf16[768,128]{1,0:T(8,128)(2,1)S(1)} %far_project.3.refs_1_), channel_id=1, source_target_pairs={{0,1},{1,2},{2,3},{3,0},{4,5},{5,6},{6,7},{7,4},{8,9},{9,10},{10,1... | collective-permute-start | bytes 589832 | tf_op jit(solution)/shard_map/ppermute | solution.py:258
  163.1 34.4 %all-to-all-start.3 = ((bf16[64,8,1024]{2,1,0:T(8,128)(2,1)}), bf16[64,8,1024]{2,1,0:T(8,128)(2,1)S(1)}, u32[]{:S(2)}, u32[]{:S(2)}) async-start(bf16[64,8,1024]{2,1,0:T(8,128)(2,1)} %bitcast.29), calls=%async_computation.3 | async-start | bytes 2097152 | tf_op jit(solution)/shard_map/all_to_all | solution.py:487

commit v5 on v4

--- a/solution.py
+++ b/solution.py
@@ -42,10 +42,8 @@
     return (dot(spread, hits) > 0.5) & (dot(spread, earlier) == slot)
 
 
-def route_kernel(ids_ref, place_ref, hits_ref, earlier_ref):
-    slots, rows = place_ref.shape
-    experts = hits_ref.shape[0]
-    ids = ids_ref[...]
+def counts_of(ids, experts):
+    rows = ids.shape[1]
     line = lax.broadcasted_iota(jnp.int32, (experts, rows), 0)
     hits = jnp.zeros((experts, rows), F32)
     for k in range(TOPK):
@@ -54,16 +52,14 @@
         jnp.int32, (rows, rows), 1
     )
     hits = hits.astype(BF16)
-    earlier = dot(hits, jnp.where(before, 1.0, 0.0).astype(BF16)).astype(BF16)
-    hits_ref[...], earlier_ref[...] = hits, earlier
-    chosen = chosen_of(spread_of(slots, experts, 0), hits, earlier)
-    place_ref[...] = jnp.where(chosen, 1.0, 0.0).astype(BF16)
-
-
-def weigh_kernel(ids_ref, probs_ref, hits_ref, earlier_ref, place_ref, *tables):
+    return hits, dot(hits, jnp.where(before, 1.0, 0.0).astype(BF16)).astype(BF16)
+
+
+def weigh_kernel(ids_ref, probs_ref, place_ref, *tables):
     slots, rows = place_ref.shape
+    experts = EXP_DEV * slots // SLOTS
     ids, probs = ids_ref[...], probs_ref[...]
-    hits, earlier = hits_ref[...], earlier_ref[...]
+    hits, earlier = counts_of(ids, experts)
     mix = probs / jnp.sum(probs, axis=0, keepdims=True)
     line = lax.broadcasted_iota(jnp.int32, hits.shape, 0)
     mixed = jnp.zeros(hits.shape, F32)
@@ -72,7 +68,7 @@
     mix_hi = mixed.astype(BF16)
     mix_lo = (mixed - mix_hi.astype(F32)).astype(BF16)
     for j in range(EXP_DEV):
-        spread = spread_of(slots, hits.shape[0], j)
+        spread = spread_of(slots, experts, j)
         chosen = chosen_of(spread, hits, earlier)
         tables[j][...] = jnp.where(chosen, dot(spread, mix_hi), 0.0).astype(BF16)
         tables[2 + j][...] = jnp.where(chosen, dot(spread, mix_lo), 0.0).astype(BF16)
@@ -80,25 +76,19 @@
             place_ref[...] = jnp.where(chosen, 1.0, 0.0).astype(BF16)
 
 
-def route(ids, probs, devices):
-    rows = ids.shape[1]
-    table = jax.ShapeDtypeStruct((devices * SLOTS, rows), BF16)
-    count = jax.ShapeDtypeStruct((devices * EXP_DEV, rows), BF16)
-    place0, hits, earlier = pl.pallas_call(
-        route_kernel,
-        in_specs=[VMEM],
-        out_specs=[VMEM] * 3,
-        out_shape=[table, count, count],
-        name="route",
-    )(ids)
-    place1, hi0, hi1, lo0, lo1 = pl.pallas_call(
-        weigh_kernel,
-        in_specs=[VMEM] * 4,
+def weigh(ids, probs, devices, after):
+    table = jax.ShapeDtypeStruct((devices * SLOTS, ids.shape[1]), BF16)
+
+    def kernel(ids_ref, probs_ref, _, *tables):
+        weigh_kernel(ids_ref, probs_ref, *tables)
+
+    return pl.pallas_call(
+        kernel,
+        in_specs=[VMEM, VMEM, ANY],
         out_specs=[VMEM] * 5,
         out_shape=[table] * 5,
         name="weigh",
-    )(ids, probs, hits, earlier)
-    return hi0, hi1, lo0, lo1, place0, place1
+    )(ids, probs, after)
 
 
 def split_columns(me, w):
@@ -126,7 +116,8 @@
 
 
 def attention_kernel(
-    lens_ref, q_ref, nk_ref, nv_ref, k_ref, v_ref, res_ref, gain_ref, summed_ref, scaled_ref
+    lens_ref, q_ref, nk_ref, nv_ref, k_ref, v_ref, res_ref, gain_ref, ids_ref,
+    summed_ref, scaled_ref, placed_ref, table, held
 ):
     rows, span, depth = k_ref.shape
     heads = q_ref.shape[1] // depth
@@ -166,10 +157,24 @@
         rows, heads * depth
     )
     summed_ref[...] = summed
-    scaled_ref[...] = (summed * gain_ref[...]).astype(BF16)
-
-
-def attention(lens, me, queries, new_key, new_value, keys, values, residual, gain):
+    scaled = (summed * gain_ref[...]).astype(BF16)
+    scaled_ref[...] = scaled
+    held[pl.ds(pl.multiple_of(base, rows), rows), :] = scaled
+
+    @pl.when(pl.program_id(0) == 0)
+    def _():
+        slots = table.shape[0]
+        experts = EXP_DEV * slots // SLOTS
+        hits, earlier = counts_of(ids_ref[...], experts)
+        chosen = chosen_of(spread_of(slots, experts, 0), hits, earlier)
+        table[...] = jnp.where(chosen, 1.0, 0.0).astype(BF16)
+
+    @pl.when(pl.program_id(0) == pl.num_programs(0) - 1)
+    def _():
+        placed_ref[...] = dot(table[...], held[...]).astype(BF16)
+
+
+def attention(lens, me, queries, new_key, new_value, keys, values, residual, gain, ids, devices):
     rows, part = queries.shape
     span, depth = keys.shape[1:]
     step = 32
@@ -186,11 +191,18 @@
             num_scalar_prefetch=2,
             grid=(rows // step,),
             in_specs=[wide, slim, slim, cache, cache, wide,
-                      pl.BlockSpec((1, part), lambda i, n, m: (0, m[0]))],
-            out_specs=[wide, wide],
+                      pl.BlockSpec((1, part), lambda i, n, m: (0, m[0])),
+                      pl.BlockSpec(ids.shape, lambda i, n, m: (0, 0))],
+            out_specs=[wide, wide,
+                       pl.BlockSpec((devices * SLOTS, part), lambda i, n, m: (0, 0))],
+            scratch_shapes=[
+                pltpu.VMEM((devices * SLOTS, rows), BF16), pltpu.VMEM((rows, part), BF16)
+            ],
         ),
         out_shape=[
-            jax.ShapeDtypeStruct((rows, part), F32), jax.ShapeDtypeStruct((rows, part), BF16)
+            jax.ShapeDtypeStruct((rows, part), F32),
+            jax.ShapeDtypeStruct((rows, part), BF16),
+            jax.ShapeDtypeStruct((devices * SLOTS, part), BF16),
         ],
         compiler_params=pltpu.CompilerParams(vmem_limit_bytes=58 << 20),
         cost_estimate=pl.CostEstimate(
@@ -199,7 +211,7 @@
             transcendentals=rows * part,
         ),
         name="attention",
-    )(lens, me, queries, new_key, new_value, keys, values, residual, gain)
+    )(lens, me, queries, new_key, new_value, keys, values, residual, gain, ids)
 
 
 def place_kernel(table_ref, rows_ref, *refs):
@@ -456,13 +468,15 @@
     devices = lax.axis_size("side") * lax.axis_size("grp")
     slots = devices * SLOTS
     me = lax.axis_index("tp").astype(jnp.int32).reshape(1)
-    hi0, hi1, lo0, lo1, table0, table1 = route(expert_ids.T, gate_probs.T, devices)
     blocks = split_columns(me, w_down)
     gain = norm_gain.reshape(1, -1)
     inv_gain = 1.0 / gain
-    summed, scaled = attention(
-        cache_len, me, queries, new_key, new_value, key_cache, value_cache, residual, gain
-    )
+    ids = expert_ids.T
+    summed, scaled, placed0 = attention(
+        cache_len, me, queries, new_key, new_value, key_cache, value_cache, residual, gain,
+        ids, devices,
+    )
+    table1, hi0, hi1, lo0, lo1 = weigh(ids, gate_probs.T, devices, blocks[0])
     swap = functools.partial(
         lax.all_to_all, axis_name=group, split_axis=0, concat_axis=0, tiled=True
     )
@@ -470,8 +484,8 @@
     w_gate, w_up = in_hbm(w_gate, w_up)
     total = summed
     own = ()
-    for expert, table, hi, lo in ((0, table0, hi0, lo0), (1, table1, hi1, lo1)):
-        placed = place_rows(table, scaled)
+    for expert, hi, lo in ((0, hi0, lo0), (1, hi1, lo1)):
+        placed = place_rows(table1, scaled) if expert else placed0
         arrived = swap(placed.reshape(devices, SLOTS, part)).reshape(devices, 1, SLOTS, part)
         own = pick(arrived, 0, PICK_WEIGHT[expert], *moved[: 3 * expert])
         left = [lax.ppermute(half, "tp", RIGHT) for half in own]

time: 200 us -> 198 us (0.990)
  waiting for transfers between devices: 87 us -> 90 us
  Pallas kernels: 45.3 us -> 42.4 us
  starting transfers between devices: 63.3 us -> 61.2 us
    ppermute x4, waiting for transfers between devices: 15.5 us -> 19.7 us  [body(): left = [lax.ppermute(half, 'tp', RIGHT) for half in own]]
    ppermute x3, starting transfers between devices: 4.54 us -> 1.25 us  [exchange(): lax.ppermute(for_across, 'tp', ACROSS)]
    ppermute x2, waiting for transfers between devices: 1.31 us -> 4.21 us  [body(): low = lax.ppermute(left[0], 'tp', RIGHT)]
    pallas_call x2 -> x1, Pallas kernels: 4.62 us -> 2.29 us  [place_rows(): pl.pallas_call(place_kernel, grid=(2,), in_specs=[pl.BlockSpec((slots //...]
  transfers between devices with their start and end apart: 25 -> 25, of which waited for: 12 -> 13; matrix products, arithmetic and copies ran while one was open for 2% -> 2% of each run, Pallas kernels for 17% -> 18%
where the time goes in v5:
time: 198 us; the launch traced here: 197 us
  waiting for transfers between devices  90 us (45%)
  starting transfers between devices  61.2 us (31%)
  Pallas kernels  42.4 us (21%)
  local copies, waits for them, and re-layouts  3.08 us (2%)
    all_to_all x2, waiting for transfers between devices, body(): back = swap(produced.reshape(devices, SLOTS, part)).reshape(slots, part)  27 us
    all_to_all x2, waiting for transfers between devices, body(): swap(placed.reshape(devices, SLOTS, part)).reshape(devices, 1, SLOTS, part)  24.5 us
    all_to_all x2, starting transfers between devices, body(): back = swap(produced.reshape(devices, SLOTS, part)).reshape(slots, part)  20.1 us
    all_to_all x2, starting transfers between devices, body(): swap(placed.reshape(devices, SLOTS, part)).reshape(devices, 1, SLOTS, part)  19.8 us
    ppermute x4, waiting for transfers between devices, body(): left = [lax.ppermute(half, 'tp', RIGHT) for half in own]  19.7 us
    pallas_call x2, Pallas kernels, near_project(): pl.pallas_call(near_kernel, grid_spec=pltpu.PrefetchScalarGridSpec(num_sc...  10.1 us
    ppermute x3, waiting for transfers between devices, exchange(): lax.ppermute(for_across, 'tp', ACROSS)  7.44 us
    pallas_call x2, Pallas kernels, down_project(): pl.pallas_call(kernel, grid_spec=pltpu.PrefetchScalarGridSpec(num_scalar_...  7.18 us
  transfers between devices with their start and end apart: 25, of which 13 were waited for; matrix products, arithmetic and copies ran while one was open for 2% of the time, Pallas kernels for 18%

profile of v5, /device:TPU:1, one launch (start us, length us, event | category | flops | bytes accessed | tf_op | source)
XLA Modules:
  0.0 196.9 jit_solution(6516763737869310707)
XLA Ops:
  0.0 6.5 %attention.1 = (f32[64,1024]{1,0:T(8,128)}, bf16[64,1024]{1,0:T(8,128)(2,1)}, bf16[512,1024]{1,0:T(8,128)(2,1)}) custom-call(s32[64]{0:T(128)} %lens_ref.1, s32[1]{0:T(128)} %bitcast.me_ref.refs_0_, bf16[64,1024]{1,0:T(8,128)(2,1)} %refs_0_.1, bf16[64,128]{1,0:T(8,128)(2,1)} %refs_1_.1, bf16[64,128]{1,0:T(8,128)(2,1)} %refs_2_.1, ...), custom_call_target="tpu_custom_call" | custom-call | flops 33554432 | bytes 4194304 | tf_op jit(solution)/shard_map/attention/pallas_call | solution.py:188
  6.5 13.5 %all-to-all-start = ((bf16[64,8,1024]{2,1,0:T(8,128)(2,1)}), bf16[64,8,1024]{2,1,0:T(8,128)(2,1)}, u32[]{:S(2)}, u32[]{:S(2)}) async-start(bf16[64,8,1024]{2,1,0:T(8,128)(2,1)} %bitcast.29), calls=%async_computation | async-start | bytes 2097152 | tf_op jit(solution)/shard_map/all_to_all | solution.py:489
  20.0 1.8 split_columns.1
  21.7 2.5 %collective-permute-start.10 = (bf16[2,192,1024]{2,1,0:T(8,128)(2,1)}, bf16[2,192,1024]{2,1,0:T(8,128)(2,1)}, u32[]{:S(2)}, u32[]{:S(2)}) collective-permute-start(bf16[2,192,1024]{2,1,0:T(8,128)(2,1)} %get-tuple-element.36), channel_id=1, source_target_pairs={{0,3},{1,0},{2,1},{3,2},{4,7},{5,4},{6,5},{7,6},{8,11},{9,8},{10,9... | collective-permute-start | bytes 2359304 | tf_op jit(solution)/shard_map/ppermute | solution.py:271
  24.2 0.5 collective-permute-start.11
  24.7 0.6 collective-permute-start.9
  25.3 2.0 %weigh.1 = (bf16[512,64]{1,0:T(8,128)(2,1)}, bf16[512,64]{1,0:T(8,128)(2,1)}, bf16[512,64]{1,0:T(8,128)(2,1)}, bf16[512,64]{1,0:T(8,128)(2,1)}, bf16[512,64]{1,0:T(8,128)(2,1)}) custom-call(s32[8,64]{1,0:T(8,128)} %bitcast.32, f32[8,64]{1,0:T(8,128)} %bitcast.33, bf16[2,192,1024]{2,1,0:T(8,128)(2,1)} %get-tuple-element.27._), custom_call_target="tpu_custom_call" | custom-call | tf_op jit(solution)/shard_map/weigh/pallas_call | solution.py:85
  27.4 2.3 %place_rows.1 = bf16[512,1024]{1,0:T(8,128)(2,1)} custom-call(bf16[512,64]{1,0:T(8,128)(2,1)} %get-tuple-element.40.table_ref, bf16[64,1024]{1,0:T(8,128)(2,1)} %get-tuple-element.41.rows_ref), custom_call_target="tpu_custom_call" | custom-call | flops 67108864 | bytes 2097152 | tf_op jit(solution)/shard_map/place_rows/pallas_call | solution.py:223
  29.6 18.4 %all-to-all-done = bf16[64,8,1024]{2,1,0:T(8,128)(2,1)} async-done(((bf16[64,8,1024]{2,1,0:T(8,128)(2,1)}), bf16[64,8,1024]{2,1,0:T(8,128)(2,1)}, u32[]{:S(2)}, u32[]{:S(2)}) %all-to-all-start) | async-done | bytes 1048608 | tf_op jit(solution)/shard_map/all_to_all | solution.py:489
  48.0 6.3 %all-to-all-start.2 = ((bf16[64,8,1024]{2,1,0:T(8,128)(2,1)}), bf16[64,8,1024]{2,1,0:T(8,128)(2,1)}, u32[]{:S(2)}, u32[]{:S(2)}) async-start(bf16[64,8,1024]{2,1,0:T(8,128)(2,1)} %bitcast.26), calls=%async_computation.2 | async-start | bytes 2097152 | tf_op jit(solution)/shard_map/all_to_all | solution.py:489
  54.4 2.3 %pick.2 = (bf16[256,1024]{1,0:T(8,128)(2,1)}, bf16[256,1024]{1,0:T(8,128)(2,1)}) custom-call(bf16[64,1,8,1024]{3,2,1,0:T(8,128)(2,1)} %bitcast.7.all_ref), custom_call_target="tpu_custom_call" | custom-call | flops 20000000000 | bytes 2097152 | tf_op jit(solution)/shard_map/pick/pallas_call | solution.py:249
  56.7 1.2 collective-permute-start
  57.9 1.5 collective-permute-start.2
  59.3 0.0 collective-permute-done.10.refs_7_.refs_1_
  59.3 1.9 collective-permute-start.5
  61.2 0.0 collective-permute-done.11.refs_8_.refs_2_
  61.3 0.0 collective-permute-start.4
  61.3 12.3 %collective-permute-done.left0 = bf16[256,1024]{1,0:T(8,128)(2,1)} collective-permute-done((bf16[256,1024]{1,0:T(8,128)(2,1)}, bf16[256,1024]{1,0:T(8,128)(2,1)}, u32[]{:S(2)}, u32[]{:S(2)}) %collective-permute-start) | collective-permute-done | bytes 524320 | tf_op jit(solution)/shard_map/ppermute | solution.py:491
  73.6 0.0 collective-permute-start.1
  73.6 0.0 collective-permute-done.2.right1
  73.6 2.7 %collective-permute-start.3 = (bf16[256,1024]{1,0:T(8,128)(2,1)}, bf16[256,1024]{1,0:T(8,128)(2,1)}, u32[]{:S(2)}, u32[]{:S(2)}) collective-permute-start(bf16[256,1024]{1,0:T(8,128)(2,1)} %collective-permute-done.2.right1), channel_id=1, source_target_pairs={{0,3},{1,0},{2,1},{3,2},{4,7},{5,4},{6,5},{7,6},{8,11},{9,8},{10,9... | collective-permute-start | bytes 1572872 | tf_op jit(solution)/shard_map/ppermute | solution.py:494
  76.2 0.0 collective-permute-done.9.refs_6_.refs_0_
  76.2 6.2 %all-to-all-done.2 = bf16[64,8,1024]{2,1,0:T(8,128)(2,1)} async-done(((bf16[64,8,1024]{2,1,0:T(8,128)(2,1)}), bf16[64,8,1024]{2,1,0:T(8,128)(2,1)}, u32[]{:S(2)}, u32[]{:S(2)}) %all-to-all-start.2) | async-done | bytes 1048608 | tf_op jit(solution)/shard_map/all_to_all | solution.py:489
  82.4 2.2 %pick.3 = (bf16[256,1024]{1,0:T(8,128)(2,1)}, bf16[256,1024]{1,0:T(8,128)(2,1)}) custom-call(bf16[64,1,8,1024]{3,2,1,0:T(8,128)(2,1)} %bitcast.14.all_ref, bf16[2,192,1024]{2,1,0:T(8,128)(2,1)} %collective-permute-done.9.refs_6_.refs_0_, bf16[2,192,1024]{2,1,0:T(8,128)(2,1)} %collective-permute-done.10.refs_7_.refs_1_, ...), custom_call_target="tpu_custom_call" | custom-call | bytes 2097152 | tf_op jit(solution)/shard_map/pick/pallas_call | solution.py:249
  84.7 1.2 collective-permute-start.12
  85.9 0.0 collective-permute-done.5.right0
  85.9 1.5 collective-permute-start.14
  87.4 0.0 collective-permute-done.4.left1
  87.4 5.1 %near_project.2 = (f32[512,192]{1,0:T(8,128)S(1)}, f32[512,192]{1,0:T(8,128)S(1)}, f32[512,128]{1,0:T(8,128)S(1)}) custom-call(s32[1]{0:T(128)} %bitcast.me_ref.refs_0_, bf16[256,1024]{1,0:T(8,128)(2,1)} %get-tuple-element.31.own0, bf16[256,1024]{1,0:T(8,128)(2,1)} %get-tuple-element.32.own1, bf16[256,1024]{1,0:T(8,128)(2,1)} %collective-permute-done.left0, ...), custom_call_target="tpu_custom_call" | custom-call | flops 1207959552 | bytes 7340032 | tf_op jit(solution)/shard_map/near_project/pallas_call | solution.py:331
  92.4 3.6 %collective-permute-done.1.low = bf16[256,1024]{1,0:T(8,128)(2,1)} collective-permute-done((bf16[256,1024]{1,0:T(8,128)(2,1)}, bf16[256,1024]{1,0:T(8,128)(2,1)}, u32[]{:S(2)}, u32[]{:S(2)}) %collective-permute-start.1) | collective-permute-done | bytes 524320 | tf_op jit(solution)/shard_map/ppermute | solution.py:493
  96.0 0.0 collective-permute-done.3.high
  96.0 2.5 %far_project.2.refs_1_ = bf16[768,128]{1,0:T(8,128)(2,1)S(1)} custom-call(s32[1]{0:T(128)} %bitcast.me_ref.refs_0_, bf16[256,1024]{1,0:T(8,128)(2,1)} %collective-permute-done.1.low, bf16[256,1024]{1,0:T(8,128)(2,1)} %collective-permute-done.3.high, f32[512,192]{1,0:T(8,128)S(1)} %get-tuple-element.33.gate_in, f32[512,192]{1,0:T(8,128)S(1)} %get-tuple-element.34.up_in, ...), custom_call_target="tpu_custom_call" | custom-call | flops 1000000000 | bytes 4194304 | tf_op jit(solution)/shard_map/far_project/pallas_call | solution.py:365
  98.5 0.2 collective-permute-start.8
  98.8 0.9 collective-permute-start.7
  99.6 0.6 collective-permute-start.6
  100.2 7.4 %collective-permute-done.12.left0 = bf16[256,1024]{1,0:T(8,128)(2,1)} collective-permute-done((bf16[256,1024]{1,0:T(8,128)(2,1)}, bf16[256,1024]{1,0:T(8,128)(2,1)}, u32[]{:S(2)}, u32[]{:S(2)}) %collective-permute-start.12) | collective-permute-done | bytes 524320 | tf_op jit(solution)/shard_map/ppermute | solution.py:491
  107.6 0.0 collective-permute-start.17
  107.6 0.0 collective-permute-done.14.right1
  107.6 1.5 collective-permute-start.16
  109.1 1.9 collective-permute-done.8.refs_4_
  111.0 2.0 %collective-permute-done.7.refs_3_ = bf16[768,128]{1,0:T(8,128)(2,1)S(1)} collective-permute-done((bf16[768,128]{1,0:T(8,128)(2,1)S(1)}, bf16[768,128]{1,0:T(8,128)(2,1)S(1)}, u32[]{:S(2)}, u32[]{:S(2)}) %collective-permute-start.7) | collective-permute-done | bytes 196640 | tf_op jit(solution)/shard_map/ppermute | solution.py:271
  113.0 2.6 %collective-permute-start.15 = (bf16[256,1024]{1,0:T(8,128)(2,1)}, bf16[256,1024]{1,0:T(8,128)(2,1)}, u32[]{:S(2)}, u32[]{:S(2)}) collective-permute-start(bf16[256,1024]{1,0:T(8,128)(2,1)} %collective-permute-done.14.right1), channel_id=1, source_target_pairs={{0,3},{1,0},{2,1},{3,2},{4,7},{5,4},{6,5},{7,6},{8,11},{9,8},{10,9... | collective-permute-start | bytes 1572872 | tf_op jit(solution)/shard_map/ppermute | solution.py:494
  115.6 3.6 %down_project.2 = bf16[512,1024]{1,0:T(8,128)(2,1)} custom-call(s32[1]{0:T(128)} %bitcast.me_ref.refs_0_, bf16[768,128]{1,0:T(8,128)(2,1)S(1)} %far_project.2.refs_1_, bf16[768,128]{1,0:T(8,128)(2,1)S(1)} %collective-permute-done.6.refs_2_, bf16[768,128]{1,0:T(8,128)(2,1)S(1)} %collective-permute-done.7.refs_3_, ...), custom_call_target="tpu_custom_call" | custom-call | flops 805306368 | bytes 3407872 | tf_op jit(solution)/shard_map/down_project/pallas_call | solution.py:414
  119.2 13.0 %all-to-all-start.1 = ((bf16[64,8,1024]{2,1,0:T(8,128)(2,1)}), bf16[64,8,1024]{2,1,0:T(8,128)(2,1)}, u32[]{:S(2)}, u32[]{:S(2)}) async-start(bf16[64,8,1024]{2,1,0:T(8,128)(2,1)} %bitcast.27), calls=%async_computation.1 | async-start | bytes 2097152 | tf_op jit(solution)/shard_map/all_to_all | solution.py:501
  132.2 5.1 %near_project.3 = (f32[512,192]{1,0:T(8,128)S(1)}, f32[512,192]{1,0:T(8,128)S(1)}, f32[512,128]{1,0:T(8,128)S(1)}) custom-call(s32[1]{0:T(128)} %bitcast.me_ref.refs_0_, bf16[256,1024]{1,0:T(8,128)(2,1)} %get-tuple-element.42.own0, bf16[256,1024]{1,0:T(8,128)(2,1)} %get-tuple-element.43.own1, bf16[256,1024]{1,0:T(8,128)(2,1)} %collective-permute-done.12.left0, ...), custom_call_target="tpu_custom_call" | custom-call | flops 1207959552 | bytes 7340032 | tf_op jit(solution)/shard_map/near_project/pallas_call | solution.py:331
  137.3 0.6 collective-permute-done.13.low
  137.9 0.0 collective-permute-done.15.high
  137.9 2.5 %far_project.3.refs_1_ = bf16[768,128]{1,0:T(8,128)(2,1)S(1)} custom-call(s32[1]{0:T(128)} %bitcast.me_ref.refs_0_, bf16[256,1024]{1,0:T(8,128)(2,1)} %collective-permute-done.13.low, bf16[256,1024]{1,0:T(8,128)(2,1)} %collective-permute-done.15.high, f32[512,192]{1,0:T(8,128)S(1)} %get-tuple-element.44.gate_in, f32[512,192]{1,0:T(8,128)S(1)} %get-tuple-element.45.up_in, ...), custom_call_target="tpu_custom_call" | custom-call | flops 14000000000 | bytes 4194304 | tf_op jit(solution)/shard_map/far_project/pallas_call | solution.py:365
  140.4 0.5 collective-permute-start.20
  140.9 0.8 collective-permute-start.19
  141.7 0.6 collective-permute-start.18
  142.4 5.5 %collective-permute-done.20.refs_4_ = bf16[768,128]{1,0:T(8,128)(2,1)S(1)} collective-permute-done((bf16[768,128]{1,0:T(8,128)(2,1)S(1)}, bf16[768,128]{1,0:T(8,128)(2,1)S(1)}, u32[]{:S(2)}, u32[]{:S(2)}) %collective-permute-start.20) | collective-permute-done | bytes 196640 | tf_op jit(solution)/shard_map/ppermute | solution.py:272
  147.9 1.6 collective-permute-done.19.refs_3_
  149.5 3.5 %collective-permute-done.18.refs_2_ = bf16[768,128]{1,0:T(8,128)(2,1)S(1)} collective-permute-done((bf16[768,128]{1,0:T(8,128)(2,1)S(1)}, bf16[768,128]{1,0:T(8,128)(2,1)S(1)}, u32[]{:S(2)}, u32[]{:S(2)}) %collective-permute-start.18) | collective-permute-done | bytes 196640 | tf_op jit(solution)/shard_map/ppermute | solution.py:270
  153.0 3.6 %down_project.3 = bf16[512,1024]{1,0:T(8,128)(2,1)} custom-call(s32[1]{0:T(128)} %bitcast.me_ref.refs_0_, bf16[768,128]{1,0:T(8,128)(2,1)S(1)} %far_project.3.refs_1_, bf16[768,128]{1,0:T(8,128)(2,1)S(1)} %collective-permute-done.18.refs_2_, bf16[768,128]{1,0:T(8,128)(2,1)S(1)} %collective-permute-done.19.refs_3_, ...), custom_call_target="tpu_custom_call" | custom-call | flops 805306368 | bytes 3407872 | tf_op jit(solution)/shard_map/down_project/pallas_call | solution.py:414
  156.6 3.7 %all-to-all-done.1 = bf16[64,8,1024]{2,1,0:T(8,128)(2,1)} async-done(((bf16[64,8,1024]{2,1,0:T(8,128)(2,1)}), bf16[64,8,1024]{2,1,0:T(8,128)(2,1)}, u32[]{:S(2)}, u32[]{:S(2)}) %all-to-all-start.1) | async-done | bytes 1048608 | tf_op jit(solution)/shard_map/all_to_all | solution.py:501
  160.3 7.1 %all-to-all-start.3 = ((bf16[64,8,1024]{2,1,0:T(8,128)(2,1)}), bf16[64,8,1024]{2,1,0:T(8,128)(2,1)S(1)}, u32[]{:S(2)}, u32[]{:S(2)}) async-start(bf16[64,8,1024]{2,1,0:T(8,128)(2,1)} %bitcast.28), calls=%async_computation.3 | async-start | bytes 2097152 | tf_op jit(solution)/shard_map/all_to_all | solution.py:501
  167.4 1.0 copy.14
  168.4 1.0 copy.15
  169.4 1.0 copy.16
  170.4 0.1 copy.17
  170.5 1.7 mix_in.2.total_ref
  172.2 23.3 %all-to-all-done.3 = bf16[64,8,1024]{2,1,0:T(8,128)(2,1)S(1)} async-done(((bf16[64,8,1024]{2,1,0:T(8,128)(2,1)}), bf16[64,8,1024]{2,1,0:T(8,128)(2,1)S(1)}, u32[]{:S(2)}, u32[]{:S(2)}) %all-to-all-start.3) | async-done | bytes 1048608 | tf_op jit(solution)/shard_map/all_to_all | solution.py:501
  195.5 1.3 mix_in.3
  (13 shorter events, 0.0 us)
Async XLA Ops:
  0.0 19.9 %copy-start = (bf16[2,192,4096]{2,1,0:T(8,128)(2,1)S(1)}, bf16[2,192,4096]{2,1,0:T(8,128)(2,1)}, u32[]{:S(2)}) copy-start(bf16[2,192,4096]{2,1,0:T(8,128)(2,1)} %refs_5_.5) | copy-start | bytes 9437188
  6.5 41.5 %all-to-all-start = ((bf16[64,8,1024]{2,1,0:T(8,128)(2,1)}), bf16[64,8,1024]{2,1,0:T(8,128)(2,1)}, u32[]{:S(2)}, u32[]{:S(2)}) async-start(bf16[64,8,1024]{2,1,0:T(8,128)(2,1)} %bitcast.29), calls=%async_computation | async-start | bytes 2097152 | tf_op jit(solution)/shard_map/all_to_all | solution.py:489
  21.7 37.6 %collective-permute-start.10 = (bf16[2,192,1024]{2,1,0:T(8,128)(2,1)}, bf16[2,192,1024]{2,1,0:T(8,128)(2,1)}, u32[]{:S(2)}, u32[]{:S(2)}) collective-permute-start(bf16[2,192,1024]{2,1,0:T(8,128)(2,1)} %get-tuple-element.36), channel_id=1, source_target_pairs={{0,3},{1,0},{2,1},{3,2},{4,7},{5,4},{6,5},{7,6},{8,11},{9,8},{10,9... | collective-permute-start | bytes 2359304 | tf_op jit(solution)/shard_map/ppermute | solution.py:271
  24.2 37.1 %collective-permute-start.11 = (bf16[2,192,1024]{2,1,0:T(8,128)(2,1)}, bf16[2,192,1024]{2,1,0:T(8,128)(2,1)}, u32[]{:S(2)}, u32[]{:S(2)}) collective-permute-start(bf16[2,192,1024]{2,1,0:T(8,128)(2,1)} %get-tuple-element.37), channel_id=1, source_target_pairs={{0,2},{1,3},{2,0},{3,1},{4,6},{5,7},{6,4},{7,5},{8,10},{9,11},{10,... | collective-permute-start | bytes 2359304 | tf_op jit(solution)/shard_map/ppermute | solution.py:272
  24.7 51.5 %collective-permute-start.9 = (bf16[2,192,1024]{2,1,0:T(8,128)(2,1)}, bf16[2,192,1024]{2,1,0:T(8,128)(2,1)}, u32[]{:S(2)}, u32[]{:S(2)}) collective-permute-start(bf16[2,192,1024]{2,1,0:T(8,128)(2,1)} %get-tuple-element.27._), channel_id=1, source_target_pairs={{0,1},{1,2},{2,3},{3,0},{4,5},{5,6},{6,7},{7,4},{8,9},{9,10},{10,1... | collective-permute-start | bytes 2359304 | tf_op jit(solution)/shard_map/ppermute | solution.py:270
  48.0 34.4 %all-to-all-start.2 = ((bf16[64,8,1024]{2,1,0:T(8,128)(2,1)}), bf16[64,8,1024]{2,1,0:T(8,128)(2,1)}, u32[]{:S(2)}, u32[]{:S(2)}) async-start(bf16[64,8,1024]{2,1,0:T(8,128)(2,1)} %bitcast.26), calls=%async_computation.2 | async-start | bytes 2097152 | tf_op jit(solution)/shard_map/all_to_all | solution.py:489
  56.7 30.7 %copy-start.3 = (f32[4096]{0:T(1024)S(1)}, f32[4096]{0:T(1024)}, u32[]{:S(2)}) copy-start(f32[4096]{0:T(1024)} %param.20) | copy-start | bytes 49156
  56.7 16.9 %collective-permute-start = (bf16[256,1024]{1,0:T(8,128)(2,1)}, bf16[256,1024]{1,0:T(8,128)(2,1)}, u32[]{:S(2)}, u32[]{:S(2)}) collective-permute-start(bf16[256,1024]{1,0:T(8,128)(2,1)} %get-tuple-element.31.own0), channel_id=1, source_target_pairs={{0,1},{1,2},{2,3},{3,0},{4,5},{5,6},{6,7},{7,4},{8,9},{9,10},{10,1... | collective-permute-start | bytes 1572872 | tf_op jit(solution)/shard_map/ppermute | solution.py:491
  57.9 15.7 %collective-permute-start.2 = (bf16[256,1024]{1,0:T(8,128)(2,1)}, bf16[256,1024]{1,0:T(8,128)(2,1)}, u32[]{:S(2)}, u32[]{:S(2)}) collective-permute-start(bf16[256,1024]{1,0:T(8,128)(2,1)} %get-tuple-element.32.own1), channel_id=1, source_target_pairs={{0,3},{1,0},{2,1},{3,2},{4,7},{5,4},{6,5},{7,6},{8,11},{9,8},{10,9... | collective-permute-start | bytes 1572872 | tf_op jit(solution)/shard_map/ppermute | solution.py:492
  59.3 26.5 %collective-permute-start.5 = (bf16[256,1024]{1,0:T(8,128)(2,1)}, bf16[256,1024]{1,0:T(8,128)(2,1)}, u32[]{:S(2)}, u32[]{:S(2)}) collective-permute-start(bf16[256,1024]{1,0:T(8,128)(2,1)} %get-tuple-element.31.own0), channel_id=1, source_target_pairs={{0,3},{1,0},{2,1},{3,2},{4,7},{5,4},{6,5},{7,6},{8,11},{9,8},{10,9... | collective-permute-start | bytes 1572872 | tf_op jit(solution)/shard_map/ppermute | solution.py:492
  61.3 26.1 %collective-permute-start.4 = (bf16[256,1024]{1,0:T(8,128)(2,1)}, bf16[256,1024]{1,0:T(8,128)(2,1)}, u32[]{:S(2)}, u32[]{:S(2)}) collective-permute-start(bf16[256,1024]{1,0:T(8,128)(2,1)} %get-tuple-element.32.own1), channel_id=1, source_target_pairs={{0,1},{1,2},{2,3},{3,0},{4,5},{5,6},{6,7},{7,4},{8,9},{9,10},{10,1... | collective-permute-start | bytes 1572872 | tf_op jit(solution)/shard_map/ppermute | solution.py:491
  73.6 22.5 %collective-permute-start.1 = (bf16[256,1024]{1,0:T(8,128)(2,1)}, bf16[256,1024]{1,0:T(8,128)(2,1)}, u32[]{:S(2)}, u32[]{:S(2)}) collective-permute-start(bf16[256,1024]{1,0:T(8,128)(2,1)} %collective-permute-done.left0), channel_id=1, source_target_pairs={{0,1},{1,2},{2,3},{3,0},{4,5},{5,6},{6,7},{7,4},{8,9},{9,10},{10,1... | collective-permute-start | bytes 1572872 | tf_op jit(solution)/shard_map/ppermute | solution.py:493
  73.6 22.5 %collective-permute-start.3 = (bf16[256,1024]{1,0:T(8,128)(2,1)}, bf16[256,1024]{1,0:T(8,128)(2,1)}, u32[]{:S(2)}, u32[]{:S(2)}) collective-permute-start(bf16[256,1024]{1,0:T(8,128)(2,1)} %collective-permute-done.2.right1), channel_id=1, source_target_pairs={{0,3},{1,0},{2,1},{3,2},{4,7},{5,4},{6,5},{7,6},{8,11},{9,8},{10,9... | collective-permute-start | bytes 1572872 | tf_op jit(solution)/shard_map/ppermute | solution.py:494
  84.7 23.0 %collective-permute-start.12 = (bf16[256,1024]{1,0:T(8,128)(2,1)}, bf16[256,1024]{1,0:T(8,128)(2,1)}, u32[]{:S(2)}, u32[]{:S(2)}) collective-permute-start(bf16[256,1024]{1,0:T(8,128)(2,1)} %get-tuple-element.42.own0), channel_id=1, source_target_pairs={{0,1},{1,2},{2,3},{3,0},{4,5},{5,6},{6,7},{7,4},{8,9},{9,10},{10,1... | collective-permute-start | bytes 1572872 | tf_op jit(solution)/shard_map/ppermute | solution.py:491
  85.9 21.8 %collective-permute-start.14 = (bf16[256,1024]{1,0:T(8,128)(2,1)}, bf16[256,1024]{1,0:T(8,128)(2,1)}, u32[]{:S(2)}, u32[]{:S(2)}) collective-permute-start(bf16[256,1024]{1,0:T(8,128)(2,1)} %get-tuple-element.43.own1), channel_id=1, source_target_pairs={{0,3},{1,0},{2,1},{3,2},{4,7},{5,4},{6,5},{7,6},{8,11},{9,8},{10,9... | collective-permute-start | bytes 1572872 | tf_op jit(solution)/shard_map/ppermute | solution.py:492
  98.5 12.5 %collective-permute-start.8 = (bf16[768,128]{1,0:T(8,128)(2,1)S(1)}, bf16[768,128]{1,0:T(8,128)(2,1)S(1)}, u32[]{:S(2)}, u32[]{:S(2)}) collective-permute-start(bf16[768,128]{1,0:T(8,128)(2,1)S(1)} %far_project.2.refs_1_), channel_id=1, source_target_pairs={{0,2},{1,3},{2,0},{3,1},{4,6},{5,7},{6,4},{7,5},{8,10},{9,11},{10,... | collective-permute-start | bytes 589832 | tf_op jit(solution)/shard_map/ppermute | solution.py:272
  98.8 14.2 %collective-permute-start.7 = (bf16[768,128]{1,0:T(8,128)(2,1)S(1)}, bf16[768,128]{1,0:T(8,128)(2,1)S(1)}, u32[]{:S(2)}, u32[]{:S(2)}) collective-permute-start(bf16[768,128]{1,0:T(8,128)(2,1)S(1)} %far_project.2.refs_1_), channel_id=1, source_target_pairs={{0,3},{1,0},{2,1},{3,2},{4,7},{5,4},{6,5},{7,6},{8,11},{9,8},{10,9... | collective-permute-start | bytes 589832 | tf_op jit(solution)/shard_map/ppermute | solution.py:271
  99.6 16.0 %collective-permute-start.6 = (bf16[768,128]{1,0:T(8,128)(2,1)S(1)}, bf16[768,128]{1,0:T(8,128)(2,1)S(1)}, u32[]{:S(2)}, u32[]{:S(2)}) collective-permute-start(bf16[768,128]{1,0:T(8,128)(2,1)S(1)} %far_project.2.refs_1_), channel_id=1, source_target_pairs={{0,1},{1,2},{2,3},{3,0},{4,5},{5,6},{6,7},{7,4},{8,9},{9,10},{10,1... | collective-permute-start | bytes 589832 | tf_op jit(solution)/shard_map/ppermute | solution.py:270
  107.6 24.6 %collective-permute-start.17 = (bf16[256,1024]{1,0:T(8,128)(2,1)}, bf16[256,1024]{1,0:T(8,128)(2,1)}, u32[]{:S(2)}, u32[]{:S(2)}) collective-permute-start(bf16[256,1024]{1,0:T(8,128)(2,1)} %get-tuple-element.42.own0), channel_id=1, source_target_pairs={{0,3},{1,0},{2,1},{3,2},{4,7},{5,4},{6,5},{7,6},{8,11},{9,8},{10,9... | collective-permute-start | bytes 1572872 | tf_op jit(solution)/shard_map/ppermute | solution.py:492
  107.6 24.6 %collective-permute-start.16 = (bf16[256,1024]{1,0:T(8,128)(2,1)}, bf16[256,1024]{1,0:T(8,128)(2,1)}, u32[]{:S(2)}, u32[]{:S(2)}) collective-permute-start(bf16[256,1024]{1,0:T(8,128)(2,1)} %get-tuple-element.43.own1), channel_id=1, source_target_pairs={{0,1},{1,2},{2,3},{3,0},{4,5},{5,6},{6,7},{7,4},{8,9},{9,10},{10,1... | collective-permute-start | bytes 1572872 | tf_op jit(solution)/shard_map/ppermute | solution.py:491
  111.0 26.9 %collective-permute-start.13 = (bf16[256,1024]{1,0:T(8,128)(2,1)}, bf16[256,1024]{1,0:T(8,128)(2,1)}, u32[]{:S(2)}, u32[]{:S(2)}) collective-permute-start(bf16[256,1024]{1,0:T(8,128)(2,1)} %collective-permute-done.12.left0), channel_id=1, source_target_pairs={{0,1},{1,2},{2,3},{3,0},{4,5},{5,6},{6,7},{7,4},{8,9},{9,10},{10,1... | collective-permute-start | bytes 1572872 | tf_op jit(solution)/shard_map/ppermute | solution.py:493
  113.0 24.9 %collective-permute-start.15 = (bf16[256,1024]{1,0:T(8,128)(2,1)}, bf16[256,1024]{1,0:T(8,128)(2,1)}, u32[]{:S(2)}, u32[]{:S(2)}) collective-permute-start(bf16[256,1024]{1,0:T(8,128)(2,1)} %collective-permute-done.14.right1), channel_id=1, source_target_pairs={{0,3},{1,0},{2,1},{3,2},{4,7},{5,4},{6,5},{7,6},{8,11},{9,8},{10,9... | collective-permute-start | bytes 1572872 | tf_op jit(solution)/shard_map/ppermute | solution.py:494
  119.2 41.0 %all-to-all-start.1 = ((bf16[64,8,1024]{2,1,0:T(8,128)(2,1)}), bf16[64,8,1024]{2,1,0:T(8,128)(2,1)}, u32[]{:S(2)}, u32[]{:S(2)}) async-start(bf16[64,8,1024]{2,1,0:T(8,128)(2,1)} %bitcast.27), calls=%async_computation.1 | async-start | bytes 2097152 | tf_op jit(solution)/shard_map/all_to_all | solution.py:501
  140.4 30.0 %copy-start.2 = (bf16[512,64]{1,0:T(8,128)(2,1)S(1)}, bf16[512,64]{1,0:T(8,128)(2,1)}, u32[]{:S(2)}) copy-start(bf16[512,64]{1,0:T(8,128)(2,1)} %get-tuple-element.39) | copy-start | bytes 196612
  140.4 30.1 %copy-start.1 = (f32[64,1024]{1,0:T(8,128)S(1)}, f32[64,1024]{1,0:T(8,128)}, u32[]{:S(2)}) copy-start(f32[64,1024]{1,0:T(8,128)} %get-tuple-element.26.total_ref) | copy-start | bytes 786436
  140.4 7.5 %collective-permute-start.20 = (bf16[768,128]{1,0:T(8,128)(2,1)S(1)}, bf16[768,128]{1,0:T(8,128)(2,1)S(1)}, u32[]{:S(2)}, u32[]{:S(2)}) collective-permute-start(bf16[768,128]{1,0:T(8,128)(2,1)S(1)} %far_project.3.refs_1_), channel_id=1, source_target_pairs={{0,2},{1,3},{2,0},{3,1},{4,6},{5,7},{6,4},{7,5},{8,10},{9,11},{10,... | collective-permute-start | bytes 589832 | tf_op jit(solution)/shard_map/ppermute | solution.py:272
  140.9 8.6 %collective-permute-start.19 = (bf16[768,128]{1,0:T(8,128)(2,1)S(1)}, bf16[768,128]{1,0:T(8,128)(2,1)S(1)}, u32[]{:S(2)}, u32[]{:S(2)}) collective-permute-start(bf16[768,128]{1,0:T(8,128)(2,1)S(1)} %far_project.3.refs_1_), channel_id=1, source_target_pairs={{0,3},{1,0},{2,1},{3,2},{4,7},{5,4},{6,5},{7,6},{8,11},{9,8},{10,9... | collective-permute-start | bytes 589832 | tf_op jit(solution)/shard_map/ppermute | solution.py:271
  141.7 11.2 %collective-permute-start.18 = (bf16[768,128]{1,0:T(8,128)(2,1)S(1)}, bf16[768,128]{1,0:T(8,128)(2,1)S(1)}, u32[]{:S(2)}, u32[]{:S(2)}) collective-permute-start(bf16[768,128]{1,0:T(8,128)(2,1)S(1)} %far_project.3.refs_1_), channel_id=1, source_target_pairs={{0,1},{1,2},{2,3},{3,0},{4,5},{5,6},{6,7},{7,4},{8,9},{9,10},{10,1... | collective-permute-start | bytes 589832 | tf_op jit(solution)/shard_map/ppermute | solution.py:270
  160.3 35.3 %all-to-all-start.3 = ((bf16[64,8,1024]{2,1,0:T(8,128)(2,1)}), bf16[64,8,1024]{2,1,0:T(8,128)(2,1)S(1)}, u32[]{:S(2)}, u32[]{:S(2)}) async-start(bf16[64,8,1024]{2,1,0:T(8,128)(2,1)} %bitcast.28), calls=%async_computation.3 | async-start | bytes 2097152 | tf_op jit(solution)/shard_map/all_to_all | solution.py:501

commit v6 on v5

--- a/solution.py
+++ b/solution.py
@@ -402,7 +402,7 @@
 def down_project(me, packed, w_down, moved, rows, expert, *after):
     _, hidden, part = moved[0].shape
     whole = pl.BlockSpec(packed[0].shape, lambda i, m: (0, 0))
-    steps = 2
+    steps = 1
     piece = part // steps
     own = pl.BlockSpec((1, hidden, piece), lambda i, m: (expert, 0, m[0] * steps + i))
     other = pl.BlockSpec((1, hidden, piece), lambda i, m: (expert, 0, i))

time: 198 us -> 198 us (level)
  transfers between devices with their start and end apart: 25 -> 25, of which waited for: 13 -> 13; matrix products, arithmetic and copies ran while one was open for 2% -> 2% of each run, Pallas kernels for 18% -> 17%
where the time goes in v6:
time: 198 us; the launch traced here: 197 us
  waiting for transfers between devices  90.1 us (46%)
  starting transfers between devices  61.2 us (31%)
  Pallas kernels  42.2 us (21%)
  local copies, waits for them, and re-layouts  3.08 us (2%)
    all_to_all x2, waiting for transfers between devices, body(): back = swap(produced.reshape(devices, SLOTS, part)).reshape(slots, part)  27 us
    all_to_all x2, waiting for transfers between devices, body(): swap(placed.reshape(devices, SLOTS, part)).reshape(devices, 1, SLOTS, part)  24.5 us
    all_to_all x2, starting transfers between devices, body(): back = swap(produced.reshape(devices, SLOTS, part)).reshape(slots, part)  20.1 us
    all_to_all x2, starting transfers between devices, body(): swap(placed.reshape(devices, SLOTS, part)).reshape(devices, 1, SLOTS, part)  19.8 us
    ppermute x4, waiting for transfers between devices, body(): left = [lax.ppermute(half, 'tp', RIGHT) for half in own]  19.7 us
    pallas_call x2, Pallas kernels, near_project(): pl.pallas_call(near_kernel, grid_spec=pltpu.PrefetchScalarGridSpec(num_sc...  10.1 us
    ppermute x3, waiting for transfers between devices, exchange(): lax.ppermute(for_across, 'tp', ACROSS)  7.44 us
    pallas_call x2, Pallas kernels, down_project(): pl.pallas_call(kernel, grid_spec=pltpu.PrefetchScalarGridSpec(num_scalar_...  6.95 us
  transfers between devices with their start and end apart: 25, of which 13 were waited for; matrix products, arithmetic and copies ran while one was open for 2% of the time, Pallas kernels for 17%

profile of v6, /device:TPU:1, one launch (start us, length us, event | category | flops | bytes accessed | tf_op | source)
XLA Modules:
  0.0 196.8 jit_solution(13029572343937440320)
XLA Ops:
  0.0 6.5 %attention.1 = (f32[64,1024]{1,0:T(8,128)}, bf16[64,1024]{1,0:T(8,128)(2,1)}, bf16[512,1024]{1,0:T(8,128)(2,1)}) custom-call(s32[64]{0:T(128)} %lens_ref.1, s32[1]{0:T(128)} %bitcast.me_ref.refs_0_, bf16[64,1024]{1,0:T(8,128)(2,1)} %refs_0_.1, bf16[64,128]{1,0:T(8,128)(2,1)} %refs_1_.1, bf16[64,128]{1,0:T(8,128)(2,1)} %refs_2_.1, ...), custom_call_target="tpu_custom_call" | custom-call | flops 33554432 | bytes 4194304 | tf_op jit(solution)/shard_map/attention/pallas_call | solution.py:188
  6.5 13.5 %all-to-all-start = ((bf16[64,8,1024]{2,1,0:T(8,128)(2,1)}), bf16[64,8,1024]{2,1,0:T(8,128)(2,1)}, u32[]{:S(2)}, u32[]{:S(2)}) async-start(bf16[64,8,1024]{2,1,0:T(8,128)(2,1)} %bitcast.29), calls=%async_computation | async-start | bytes 2097152 | tf_op jit(solution)/shard_map/all_to_all | solution.py:489
  20.0 1.8 split_columns.1
  21.7 2.5 %collective-permute-start.10 = (bf16[2,192,1024]{2,1,0:T(8,128)(2,1)}, bf16[2,192,1024]{2,1,0:T(8,128)(2,1)}, u32[]{:S(2)}, u32[]{:S(2)}) collective-permute-start(bf16[2,192,1024]{2,1,0:T(8,128)(2,1)} %get-tuple-element.36), channel_id=1, source_target_pairs={{0,3},{1,0},{2,1},{3,2},{4,7},{5,4},{6,5},{7,6},{8,11},{9,8},{10,9... | collective-permute-start | bytes 2359304 | tf_op jit(solution)/shard_map/ppermute | solution.py:271
  24.2 0.5 collective-permute-start.11
  24.7 0.6 collective-permute-start.9
  25.3 2.0 %weigh.1 = (bf16[512,64]{1,0:T(8,128)(2,1)}, bf16[512,64]{1,0:T(8,128)(2,1)}, bf16[512,64]{1,0:T(8,128)(2,1)}, bf16[512,64]{1,0:T(8,128)(2,1)}, bf16[512,64]{1,0:T(8,128)(2,1)}) custom-call(s32[8,64]{1,0:T(8,128)} %bitcast.32, f32[8,64]{1,0:T(8,128)} %bitcast.33, bf16[2,192,1024]{2,1,0:T(8,128)(2,1)} %get-tuple-element.27._), custom_call_target="tpu_custom_call" | custom-call | tf_op jit(solution)/shard_map/weigh/pallas_call | solution.py:85
  27.4 2.3 %place_rows.1 = bf16[512,1024]{1,0:T(8,128)(2,1)} custom-call(bf16[512,64]{1,0:T(8,128)(2,1)} %get-tuple-element.40.table_ref, bf16[64,1024]{1,0:T(8,128)(2,1)} %get-tuple-element.41.rows_ref), custom_call_target="tpu_custom_call" | custom-call | flops 67108864 | bytes 2097152 | tf_op jit(solution)/shard_map/place_rows/pallas_call | solution.py:223
  29.6 18.4 %all-to-all-done = bf16[64,8,1024]{2,1,0:T(8,128)(2,1)} async-done(((bf16[64,8,1024]{2,1,0:T(8,128)(2,1)}), bf16[64,8,1024]{2,1,0:T(8,128)(2,1)}, u32[]{:S(2)}, u32[]{:S(2)}) %all-to-all-start) | async-done | bytes 1048608 | tf_op jit(solution)/shard_map/all_to_all | solution.py:489
  48.0 6.3 %all-to-all-start.2 = ((bf16[64,8,1024]{2,1,0:T(8,128)(2,1)}), bf16[64,8,1024]{2,1,0:T(8,128)(2,1)}, u32[]{:S(2)}, u32[]{:S(2)}) async-start(bf16[64,8,1024]{2,1,0:T(8,128)(2,1)} %bitcast.26), calls=%async_computation.2 | async-start | bytes 2097152 | tf_op jit(solution)/shard_map/all_to_all | solution.py:489
  54.4 2.3 %pick.2 = (bf16[256,1024]{1,0:T(8,128)(2,1)}, bf16[256,1024]{1,0:T(8,128)(2,1)}) custom-call(bf16[64,1,8,1024]{3,2,1,0:T(8,128)(2,1)} %bitcast.7.all_ref), custom_call_target="tpu_custom_call" | custom-call | flops 20000000000 | bytes 2097152 | tf_op jit(solution)/shard_map/pick/pallas_call | solution.py:249
  56.7 1.2 collective-permute-start
  57.9 1.5 collective-permute-start.2
  59.3 0.0 collective-permute-done.10.refs_7_.refs_1_
  59.3 1.9 collective-permute-start.5
  61.2 0.0 collective-permute-done.11.refs_8_.refs_2_
  61.3 0.0 collective-permute-start.4
  61.3 12.3 %collective-permute-done.left0 = bf16[256,1024]{1,0:T(8,128)(2,1)} collective-permute-done((bf16[256,1024]{1,0:T(8,128)(2,1)}, bf16[256,1024]{1,0:T(8,128)(2,1)}, u32[]{:S(2)}, u32[]{:S(2)}) %collective-permute-start) | collective-permute-done | bytes 524320 | tf_op jit(solution)/shard_map/ppermute | solution.py:491
  73.6 0.0 collective-permute-start.1
  73.6 0.0 collective-permute-done.2.right1
  73.6 2.7 %collective-permute-start.3 = (bf16[256,1024]{1,0:T(8,128)(2,1)}, bf16[256,1024]{1,0:T(8,128)(2,1)}, u32[]{:S(2)}, u32[]{:S(2)}) collective-permute-start(bf16[256,1024]{1,0:T(8,128)(2,1)} %collective-permute-done.2.right1), channel_id=1, source_target_pairs={{0,3},{1,0},{2,1},{3,2},{4,7},{5,4},{6,5},{7,6},{8,11},{9,8},{10,9... | collective-permute-start | bytes 1572872 | tf_op jit(solution)/shard_map/ppermute | solution.py:494
  76.2 0.0 collective-permute-done.9.refs_6_.refs_0_
  76.2 6.2 %all-to-all-done.2 = bf16[64,8,1024]{2,1,0:T(8,128)(2,1)} async-done(((bf16[64,8,1024]{2,1,0:T(8,128)(2,1)}), bf16[64,8,1024]{2,1,0:T(8,128)(2,1)}, u32[]{:S(2)}, u32[]{:S(2)}) %all-to-all-start.2) | async-done | bytes 1048608 | tf_op jit(solution)/shard_map/all_to_all | solution.py:489
  82.4 2.2 %pick.3 = (bf16[256,1024]{1,0:T(8,128)(2,1)}, bf16[256,1024]{1,0:T(8,128)(2,1)}) custom-call(bf16[64,1,8,1024]{3,2,1,0:T(8,128)(2,1)} %bitcast.14.all_ref, bf16[2,192,1024]{2,1,0:T(8,128)(2,1)} %collective-permute-done.9.refs_6_.refs_0_, bf16[2,192,1024]{2,1,0:T(8,128)(2,1)} %collective-permute-done.10.refs_7_.refs_1_, ...), custom_call_target="tpu_custom_call" | custom-call | bytes 2097152 | tf_op jit(solution)/shard_map/pick/pallas_call | solution.py:249
  84.7 1.2 collective-permute-start.12
  85.9 0.0 collective-permute-done.5.right0
  85.9 1.5 collective-permute-start.14
  87.4 0.0 collective-permute-done.4.left1
  87.4 5.1 %near_project.2 = (f32[512,192]{1,0:T(8,128)S(1)}, f32[512,192]{1,0:T(8,128)S(1)}, f32[512,128]{1,0:T(8,128)S(1)}) custom-call(s32[1]{0:T(128)} %bitcast.me_ref.refs_0_, bf16[256,1024]{1,0:T(8,128)(2,1)} %get-tuple-element.31.own0, bf16[256,1024]{1,0:T(8,128)(2,1)} %get-tuple-element.32.own1, bf16[256,1024]{1,0:T(8,128)(2,1)} %collective-permute-done.left0, ...), custom_call_target="tpu_custom_call" | custom-call | flops 1207959552 | bytes 7340032 | tf_op jit(solution)/shard_map/near_project/pallas_call | solution.py:331
  92.4 3.6 %collective-permute-done.1.low = bf16[256,1024]{1,0:T(8,128)(2,1)} collective-permute-done((bf16[256,1024]{1,0:T(8,128)(2,1)}, bf16[256,1024]{1,0:T(8,128)(2,1)}, u32[]{:S(2)}, u32[]{:S(2)}) %collective-permute-start.1) | collective-permute-done | bytes 524320 | tf_op jit(solution)/shard_map/ppermute | solution.py:493
  96.0 2.5 %far_project.2.refs_1_ = bf16[768,128]{1,0:T(8,128)(2,1)S(1)} custom-call(s32[1]{0:T(128)} %bitcast.me_ref.refs_0_, bf16[256,1024]{1,0:T(8,128)(2,1)} %collective-permute-done.1.low, bf16[256,1024]{1,0:T(8,128)(2,1)} %collective-permute-done.3.high, f32[512,192]{1,0:T(8,128)S(1)} %get-tuple-element.33.gate_in, f32[512,192]{1,0:T(8,128)S(1)} %get-tuple-element.34.up_in, ...), custom_call_target="tpu_custom_call" | custom-call | flops 1000000000 | bytes 4194304 | tf_op jit(solution)/shard_map/far_project/pallas_call | solution.py:365
  98.5 0.2 collective-permute-start.8
  98.8 0.9 collective-permute-start.7
  99.6 0.6 collective-permute-start.6
  100.2 7.4 %collective-permute-done.12.left0 = bf16[256,1024]{1,0:T(8,128)(2,1)} collective-permute-done((bf16[256,1024]{1,0:T(8,128)(2,1)}, bf16[256,1024]{1,0:T(8,128)(2,1)}, u32[]{:S(2)}, u32[]{:S(2)}) %collective-permute-start.12) | collective-permute-done | bytes 524320 | tf_op jit(solution)/shard_map/ppermute | solution.py:491
  107.6 0.0 collective-permute-done.14.right1
  107.6 1.5 collective-permute-start.16
  109.1 1.9 collective-permute-done.8.refs_4_
  111.0 0.0 collective-permute-start.13
  111.0 2.0 %collective-permute-done.7.refs_3_ = bf16[768,128]{1,0:T(8,128)(2,1)S(1)} collective-permute-done((bf16[768,128]{1,0:T(8,128)(2,1)S(1)}, bf16[768,128]{1,0:T(8,128)(2,1)S(1)}, u32[]{:S(2)}, u32[]{:S(2)}) %collective-permute-start.7) | collective-permute-done | bytes 196640 | tf_op jit(solution)/shard_map/ppermute | solution.py:271
  113.0 2.6 %collective-permute-start.15 = (bf16[256,1024]{1,0:T(8,128)(2,1)}, bf16[256,1024]{1,0:T(8,128)(2,1)}, u32[]{:S(2)}, u32[]{:S(2)}) collective-permute-start(bf16[256,1024]{1,0:T(8,128)(2,1)} %collective-permute-done.14.right1), channel_id=1, source_target_pairs={{0,3},{1,0},{2,1},{3,2},{4,7},{5,4},{6,5},{7,6},{8,11},{9,8},{10,9... | collective-permute-start | bytes 1572872 | tf_op jit(solution)/shard_map/ppermute | solution.py:494
  115.6 0.0 collective-permute-done.6.refs_2_
  115.6 3.5 %down_project.2 = bf16[512,1024]{1,0:T(8,128)(2,1)} custom-call(s32[1]{0:T(128)} %bitcast.me_ref.refs_0_, bf16[768,128]{1,0:T(8,128)(2,1)S(1)} %far_project.2.refs_1_, bf16[768,128]{1,0:T(8,128)(2,1)S(1)} %collective-permute-done.6.refs_2_, bf16[768,128]{1,0:T(8,128)(2,1)S(1)} %collective-permute-done.7.refs_3_, ...), custom_call_target="tpu_custom_call" | custom-call | flops 805306368 | bytes 3407872 | tf_op jit(solution)/shard_map/down_project/pallas_call | solution.py:414
  119.1 13.0 %all-to-all-start.1 = ((bf16[64,8,1024]{2,1,0:T(8,128)(2,1)}), bf16[64,8,1024]{2,1,0:T(8,128)(2,1)}, u32[]{:S(2)}, u32[]{:S(2)}) async-start(bf16[64,8,1024]{2,1,0:T(8,128)(2,1)} %bitcast.27), calls=%async_computation.1 | async-start | bytes 2097152 | tf_op jit(solution)/shard_map/all_to_all | solution.py:501
  132.1 0.0 collective-permute-done.17.right0
  132.1 5.1 %near_project.3 = (f32[512,192]{1,0:T(8,128)S(1)}, f32[512,192]{1,0:T(8,128)S(1)}, f32[512,128]{1,0:T(8,128)S(1)}) custom-call(s32[1]{0:T(128)} %bitcast.me_ref.refs_0_, bf16[256,1024]{1,0:T(8,128)(2,1)} %get-tuple-element.42.own0, bf16[256,1024]{1,0:T(8,128)(2,1)} %get-tuple-element.43.own1, bf16[256,1024]{1,0:T(8,128)(2,1)} %collective-permute-done.12.left0, ...), custom_call_target="tpu_custom_call" | custom-call | flops 1207959552 | bytes 7340032 | tf_op jit(solution)/shard_map/near_project/pallas_call | solution.py:331
  137.2 0.7 collective-permute-done.13.low
  137.9 2.5 %far_project.3.refs_1_ = bf16[768,128]{1,0:T(8,128)(2,1)S(1)} custom-call(s32[1]{0:T(128)} %bitcast.me_ref.refs_0_, bf16[256,1024]{1,0:T(8,128)(2,1)} %collective-permute-done.13.low, bf16[256,1024]{1,0:T(8,128)(2,1)} %collective-permute-done.15.high, f32[512,192]{1,0:T(8,128)S(1)} %get-tuple-element.44.gate_in, f32[512,192]{1,0:T(8,128)S(1)} %get-tuple-element.45.up_in, ...), custom_call_target="tpu_custom_call" | custom-call | flops 14000000000 | bytes 4194304 | tf_op jit(solution)/shard_map/far_project/pallas_call | solution.py:365
  140.4 0.5 collective-permute-start.20
  140.9 0.8 collective-permute-start.19
  141.7 0.6 collective-permute-start.18
  142.4 5.5 %collective-permute-done.20.refs_4_ = bf16[768,128]{1,0:T(8,128)(2,1)S(1)} collective-permute-done((bf16[768,128]{1,0:T(8,128)(2,1)S(1)}, bf16[768,128]{1,0:T(8,128)(2,1)S(1)}, u32[]{:S(2)}, u32[]{:S(2)}) %collective-permute-start.20) | collective-permute-done | bytes 196640 | tf_op jit(solution)/shard_map/ppermute | solution.py:272
  147.9 1.6 collective-permute-done.19.refs_3_
  149.5 3.5 %collective-permute-done.18.refs_2_ = bf16[768,128]{1,0:T(8,128)(2,1)S(1)} collective-permute-done((bf16[768,128]{1,0:T(8,128)(2,1)S(1)}, bf16[768,128]{1,0:T(8,128)(2,1)S(1)}, u32[]{:S(2)}, u32[]{:S(2)}) %collective-permute-start.18) | collective-permute-done | bytes 196640 | tf_op jit(solution)/shard_map/ppermute | solution.py:270
  153.0 3.5 %down_project.3 = bf16[512,1024]{1,0:T(8,128)(2,1)} custom-call(s32[1]{0:T(128)} %bitcast.me_ref.refs_0_, bf16[768,128]{1,0:T(8,128)(2,1)S(1)} %far_project.3.refs_1_, bf16[768,128]{1,0:T(8,128)(2,1)S(1)} %collective-permute-done.18.refs_2_, bf16[768,128]{1,0:T(8,128)(2,1)S(1)} %collective-permute-done.19.refs_3_, ...), custom_call_target="tpu_custom_call" | custom-call | flops 805306368 | bytes 3407872 | tf_op jit(solution)/shard_map/down_project/pallas_call | solution.py:414
  156.5 3.7 %all-to-all-done.1 = bf16[64,8,1024]{2,1,0:T(8,128)(2,1)} async-done(((bf16[64,8,1024]{2,1,0:T(8,128)(2,1)}), bf16[64,8,1024]{2,1,0:T(8,128)(2,1)}, u32[]{:S(2)}, u32[]{:S(2)}) %all-to-all-start.1) | async-done | bytes 1048608 | tf_op jit(solution)/shard_map/all_to_all | solution.py:501
  160.1 7.1 %all-to-all-start.3 = ((bf16[64,8,1024]{2,1,0:T(8,128)(2,1)}), bf16[64,8,1024]{2,1,0:T(8,128)(2,1)S(1)}, u32[]{:S(2)}, u32[]{:S(2)}) async-start(bf16[64,8,1024]{2,1,0:T(8,128)(2,1)} %bitcast.28), calls=%async_computation.3 | async-start | bytes 2097152 | tf_op jit(solution)/shard_map/all_to_all | solution.py:501
  167.3 1.0 copy.14
  168.3 1.0 copy.15
  169.3 1.0 copy.16
  170.3 0.1 copy.17
  170.4 1.7 mix_in.2.total_ref
  172.1 23.3 %all-to-all-done.3 = bf16[64,8,1024]{2,1,0:T(8,128)(2,1)S(1)} async-done(((bf16[64,8,1024]{2,1,0:T(8,128)(2,1)}), bf16[64,8,1024]{2,1,0:T(8,128)(2,1)S(1)}, u32[]{:S(2)}, u32[]{:S(2)}) %all-to-all-start.3) | async-done | bytes 1048608 | tf_op jit(solution)/shard_map/all_to_all | solution.py:501
  195.4 1.3 mix_in.3
  (13 shorter events, 0.0 us)
Async XLA Ops:
  0.0 19.9 %copy-start = (bf16[2,192,4096]{2,1,0:T(8,128)(2,1)S(1)}, bf16[2,192,4096]{2,1,0:T(8,128)(2,1)}, u32[]{:S(2)}) copy-start(bf16[2,192,4096]{2,1,0:T(8,128)(2,1)} %refs_5_.5) | copy-start | bytes 9437188
  6.5 41.5 %all-to-all-start = ((bf16[64,8,1024]{2,1,0:T(8,128)(2,1)}), bf16[64,8,1024]{2,1,0:T(8,128)(2,1)}, u32[]{:S(2)}, u32[]{:S(2)}) async-start(bf16[64,8,1024]{2,1,0:T(8,128)(2,1)} %bitcast.29), calls=%async_computation | async-start | bytes 2097152 | tf_op jit(solution)/shard_map/all_to_all | solution.py:489
  21.7 37.6 %collective-permute-start.10 = (bf16[2,192,1024]{2,1,0:T(8,128)(2,1)}, bf16[2,192,1024]{2,1,0:T(8,128)(2,1)}, u32[]{:S(2)}, u32[]{:S(2)}) collective-permute-start(bf16[2,192,1024]{2,1,0:T(8,128)(2,1)} %get-tuple-element.36), channel_id=1, source_target_pairs={{0,3},{1,0},{2,1},{3,2},{4,7},{5,4},{6,5},{7,6},{8,11},{9,8},{10,9... | collective-permute-start | bytes 2359304 | tf_op jit(solution)/shard_map/ppermute | solution.py:271
  24.2 37.1 %collective-permute-start.11 = (bf16[2,192,1024]{2,1,0:T(8,128)(2,1)}, bf16[2,192,1024]{2,1,0:T(8,128)(2,1)}, u32[]{:S(2)}, u32[]{:S(2)}) collective-permute-start(bf16[2,192,1024]{2,1,0:T(8,128)(2,1)} %get-tuple-element.37), channel_id=1, source_target_pairs={{0,2},{1,3},{2,0},{3,1},{4,6},{5,7},{6,4},{7,5},{8,10},{9,11},{10,... | collective-permute-start | bytes 2359304 | tf_op jit(solution)/shard_map/ppermute | solution.py:272
  24.7 51.5 %collective-permute-start.9 = (bf16[2,192,1024]{2,1,0:T(8,128)(2,1)}, bf16[2,192,1024]{2,1,0:T(8,128)(2,1)}, u32[]{:S(2)}, u32[]{:S(2)}) collective-permute-start(bf16[2,192,1024]{2,1,0:T(8,128)(2,1)} %get-tuple-element.27._), channel_id=1, source_target_pairs={{0,1},{1,2},{2,3},{3,0},{4,5},{5,6},{6,7},{7,4},{8,9},{9,10},{10,1... | collective-permute-start | bytes 2359304 | tf_op jit(solution)/shard_map/ppermute | solution.py:270
  48.0 34.4 %all-to-all-start.2 = ((bf16[64,8,1024]{2,1,0:T(8,128)(2,1)}), bf16[64,8,1024]{2,1,0:T(8,128)(2,1)}, u32[]{:S(2)}, u32[]{:S(2)}) async-start(bf16[64,8,1024]{2,1,0:T(8,128)(2,1)} %bitcast.26), calls=%async_computation.2 | async-start | bytes 2097152 | tf_op jit(solution)/shard_map/all_to_all | solution.py:489
  56.7 30.7 %copy-start.3 = (f32[4096]{0:T(1024)S(1)}, f32[4096]{0:T(1024)}, u32[]{:S(2)}) copy-start(f32[4096]{0:T(1024)} %param.20) | copy-start | bytes 49156
  56.7 16.9 %collective-permute-start = (bf16[256,1024]{1,0:T(8,128)(2,1)}, bf16[256,1024]{1,0:T(8,128)(2,1)}, u32[]{:S(2)}, u32[]{:S(2)}) collective-permute-start(bf16[256,1024]{1,0:T(8,128)(2,1)} %get-tuple-element.31.own0), channel_id=1, source_target_pairs={{0,1},{1,2},{2,3},{3,0},{4,5},{5,6},{6,7},{7,4},{8,9},{9,10},{10,1... | collective-permute-start | bytes 1572872 | tf_op jit(solution)/shard_map/ppermute | solution.py:491
  57.9 15.7 %collective-permute-start.2 = (bf16[256,1024]{1,0:T(8,128)(2,1)}, bf16[256,1024]{1,0:T(8,128)(2,1)}, u32[]{:S(2)}, u32[]{:S(2)}) collective-permute-start(bf16[256,1024]{1,0:T(8,128)(2,1)} %get-tuple-element.32.own1), channel_id=1, source_target_pairs={{0,3},{1,0},{2,1},{3,2},{4,7},{5,4},{6,5},{7,6},{8,11},{9,8},{10,9... | collective-permute-start | bytes 1572872 | tf_op jit(solution)/shard_map/ppermute | solution.py:492
  59.3 26.5 %collective-permute-start.5 = (bf16[256,1024]{1,0:T(8,128)(2,1)}, bf16[256,1024]{1,0:T(8,128)(2,1)}, u32[]{:S(2)}, u32[]{:S(2)}) collective-permute-start(bf16[256,1024]{1,0:T(8,128)(2,1)} %get-tuple-element.31.own0), channel_id=1, source_target_pairs={{0,3},{1,0},{2,1},{3,2},{4,7},{5,4},{6,5},{7,6},{8,11},{9,8},{10,9... | collective-permute-start | bytes 1572872 | tf_op jit(solution)/shard_map/ppermute | solution.py:492
  61.3 26.1 %collective-permute-start.4 = (bf16[256,1024]{1,0:T(8,128)(2,1)}, bf16[256,1024]{1,0:T(8,128)(2,1)}, u32[]{:S(2)}, u32[]{:S(2)}) collective-permute-start(bf16[256,1024]{1,0:T(8,128)(2,1)} %get-tuple-element.32.own1), channel_id=1, source_target_pairs={{0,1},{1,2},{2,3},{3,0},{4,5},{5,6},{6,7},{7,4},{8,9},{9,10},{10,1... | collective-permute-start | bytes 1572872 | tf_op jit(solution)/shard_map/ppermute | solution.py:491
  73.6 22.5 %collective-permute-start.1 = (bf16[256,1024]{1,0:T(8,128)(2,1)}, bf16[256,1024]{1,0:T(8,128)(2,1)}, u32[]{:S(2)}, u32[]{:S(2)}) collective-permute-start(bf16[256,1024]{1,0:T(8,128)(2,1)} %collective-permute-done.left0), channel_id=1, source_target_pairs={{0,1},{1,2},{2,3},{3,0},{4,5},{5,6},{6,7},{7,4},{8,9},{9,10},{10,1... | collective-permute-start | bytes 1572872 | tf_op jit(solution)/shard_map/ppermute | solution.py:493
  73.6 22.5 %collective-permute-start.3 = (bf16[256,1024]{1,0:T(8,128)(2,1)}, bf16[256,1024]{1,0:T(8,128)(2,1)}, u32[]{:S(2)}, u32[]{:S(2)}) collective-permute-start(bf16[256,1024]{1,0:T(8,128)(2,1)} %collective-permute-done.2.right1), channel_id=1, source_target_pairs={{0,3},{1,0},{2,1},{3,2},{4,7},{5,4},{6,5},{7,6},{8,11},{9,8},{10,9... | collective-permute-start | bytes 1572872 | tf_op jit(solution)/shard_map/ppermute | solution.py:494
  84.7 23.0 %collective-permute-start.12 = (bf16[256,1024]{1,0:T(8,128)(2,1)}, bf16[256,1024]{1,0:T(8,128)(2,1)}, u32[]{:S(2)}, u32[]{:S(2)}) collective-permute-start(bf16[256,1024]{1,0:T(8,128)(2,1)} %get-tuple-element.42.own0), channel_id=1, source_target_pairs={{0,1},{1,2},{2,3},{3,0},{4,5},{5,6},{6,7},{7,4},{8,9},{9,10},{10,1... | collective-permute-start | bytes 1572872 | tf_op jit(solution)/shard_map/ppermute | solution.py:491
  85.9 21.8 %collective-permute-start.14 = (bf16[256,1024]{1,0:T(8,128)(2,1)}, bf16[256,1024]{1,0:T(8,128)(2,1)}, u32[]{:S(2)}, u32[]{:S(2)}) collective-permute-start(bf16[256,1024]{1,0:T(8,128)(2,1)} %get-tuple-element.43.own1), channel_id=1, source_target_pairs={{0,3},{1,0},{2,1},{3,2},{4,7},{5,4},{6,5},{7,6},{8,11},{9,8},{10,9... | collective-permute-start | bytes 1572872 | tf_op jit(solution)/shard_map/ppermute | solution.py:492
  98.5 12.5 %collective-permute-start.8 = (bf16[768,128]{1,0:T(8,128)(2,1)S(1)}, bf16[768,128]{1,0:T(8,128)(2,1)S(1)}, u32[]{:S(2)}, u32[]{:S(2)}) collective-permute-start(bf16[768,128]{1,0:T(8,128)(2,1)S(1)} %far_project.2.refs_1_), channel_id=1, source_target_pairs={{0,2},{1,3},{2,0},{3,1},{4,6},{5,7},{6,4},{7,5},{8,10},{9,11},{10,... | collective-permute-start | bytes 589832 | tf_op jit(solution)/shard_map/ppermute | solution.py:272
  98.8 14.2 %collective-permute-start.7 = (bf16[768,128]{1,0:T(8,128)(2,1)S(1)}, bf16[768,128]{1,0:T(8,128)(2,1)S(1)}, u32[]{:S(2)}, u32[]{:S(2)}) collective-permute-start(bf16[768,128]{1,0:T(8,128)(2,1)S(1)} %far_project.2.refs_1_), channel_id=1, source_target_pairs={{0,3},{1,0},{2,1},{3,2},{4,7},{5,4},{6,5},{7,6},{8,11},{9,8},{10,9... | collective-permute-start | bytes 589832 | tf_op jit(solution)/shard_map/ppermute | solution.py:271
  99.6 16.0 %collective-permute-start.6 = (bf16[768,128]{1,0:T(8,128)(2,1)S(1)}, bf16[768,128]{1,0:T(8,128)(2,1)S(1)}, u32[]{:S(2)}, u32[]{:S(2)}) collective-permute-start(bf16[768,128]{1,0:T(8,128)(2,1)S(1)} %far_project.2.refs_1_), channel_id=1, source_target_pairs={{0,1},{1,2},{2,3},{3,0},{4,5},{5,6},{6,7},{7,4},{8,9},{9,10},{10,1... | collective-permute-start | bytes 589832 | tf_op jit(solution)/shard_map/ppermute | solution.py:270
  107.6 24.5 %collective-permute-start.17 = (bf16[256,1024]{1,0:T(8,128)(2,1)}, bf16[256,1024]{1,0:T(8,128)(2,1)}, u32[]{:S(2)}, u32[]{:S(2)}) collective-permute-start(bf16[256,1024]{1,0:T(8,128)(2,1)} %get-tuple-element.42.own0), channel_id=1, source_target_pairs={{0,3},{1,0},{2,1},{3,2},{4,7},{5,4},{6,5},{7,6},{8,11},{9,8},{10,9... | collective-permute-start | bytes 1572872 | tf_op jit(solution)/shard_map/ppermute | solution.py:492
  107.6 24.5 %collective-permute-start.16 = (bf16[256,1024]{1,0:T(8,128)(2,1)}, bf16[256,1024]{1,0:T(8,128)(2,1)}, u32[]{:S(2)}, u32[]{:S(2)}) collective-permute-start(bf16[256,1024]{1,0:T(8,128)(2,1)} %get-tuple-element.43.own1), channel_id=1, source_target_pairs={{0,1},{1,2},{2,3},{3,0},{4,5},{5,6},{6,7},{7,4},{8,9},{9,10},{10,1... | collective-permute-start | bytes 1572872 | tf_op jit(solution)/shard_map/ppermute | solution.py:491
  111.0 26.9 %collective-permute-start.13 = (bf16[256,1024]{1,0:T(8,128)(2,1)}, bf16[256,1024]{1,0:T(8,128)(2,1)}, u32[]{:S(2)}, u32[]{:S(2)}) collective-permute-start(bf16[256,1024]{1,0:T(8,128)(2,1)} %collective-permute-done.12.left0), channel_id=1, source_target_pairs={{0,1},{1,2},{2,3},{3,0},{4,5},{5,6},{6,7},{7,4},{8,9},{9,10},{10,1... | collective-permute-start | bytes 1572872 | tf_op jit(solution)/shard_map/ppermute | solution.py:493
  113.0 24.9 %collective-permute-start.15 = (bf16[256,1024]{1,0:T(8,128)(2,1)}, bf16[256,1024]{1,0:T(8,128)(2,1)}, u32[]{:S(2)}, u32[]{:S(2)}) collective-permute-start(bf16[256,1024]{1,0:T(8,128)(2,1)} %collective-permute-done.14.right1), channel_id=1, source_target_pairs={{0,3},{1,0},{2,1},{3,2},{4,7},{5,4},{6,5},{7,6},{8,11},{9,8},{10,9... | collective-permute-start | bytes 1572872 | tf_op jit(solution)/shard_map/ppermute | solution.py:494
  119.1 41.0 %all-to-all-start.1 = ((bf16[64,8,1024]{2,1,0:T(8,128)(2,1)}), bf16[64,8,1024]{2,1,0:T(8,128)(2,1)}, u32[]{:S(2)}, u32[]{:S(2)}) async-start(bf16[64,8,1024]{2,1,0:T(8,128)(2,1)} %bitcast.27), calls=%async_computation.1 | async-start | bytes 2097152 | tf_op jit(solution)/shard_map/all_to_all | solution.py:501
  140.4 29.8 %copy-start.2 = (bf16[512,64]{1,0:T(8,128)(2,1)S(1)}, bf16[512,64]{1,0:T(8,128)(2,1)}, u32[]{:S(2)}) copy-start(bf16[512,64]{1,0:T(8,128)(2,1)} %get-tuple-element.39) | copy-start | bytes 196612
  140.4 30.0 %copy-start.1 = (f32[64,1024]{1,0:T(8,128)S(1)}, f32[64,1024]{1,0:T(8,128)}, u32[]{:S(2)}) copy-start(f32[64,1024]{1,0:T(8,128)} %get-tuple-element.26.total_ref) | copy-start | bytes 786436
  140.4 7.5 %collective-permute-start.20 = (bf16[768,128]{1,0:T(8,128)(2,1)S(1)}, bf16[768,128]{1,0:T(8,128)(2,1)S(1)}, u32[]{:S(2)}, u32[]{:S(2)}) collective-permute-start(bf16[768,128]{1,0:T(8,128)(2,1)S(1)} %far_project.3.refs_1_), channel_id=1, source_target_pairs={{0,2},{1,3},{2,0},{3,1},{4,6},{5,7},{6,4},{7,5},{8,10},{9,11},{10,... | collective-permute-start | bytes 589832 | tf_op jit(solution)/shard_map/ppermute | solution.py:272
  140.9 8.6 %collective-permute-start.19 = (bf16[768,128]{1,0:T(8,128)(2,1)S(1)}, bf16[768,128]{1,0:T(8,128)(2,1)S(1)}, u32[]{:S(2)}, u32[]{:S(2)}) collective-permute-start(bf16[768,128]{1,0:T(8,128)(2,1)S(1)} %far_project.3.refs_1_), channel_id=1, source_target_pairs={{0,3},{1,0},{2,1},{3,2},{4,7},{5,4},{6,5},{7,6},{8,11},{9,8},{10,9... | collective-permute-start | bytes 589832 | tf_op jit(solution)/shard_map/ppermute | solution.py:271
  141.7 11.2 %collective-permute-start.18 = (bf16[768,128]{1,0:T(8,128)(2,1)S(1)}, bf16[768,128]{1,0:T(8,128)(2,1)S(1)}, u32[]{:S(2)}, u32[]{:S(2)}) collective-permute-start(bf16[768,128]{1,0:T(8,128)(2,1)S(1)} %far_project.3.refs_1_), channel_id=1, source_target_pairs={{0,1},{1,2},{2,3},{3,0},{4,5},{5,6},{6,7},{7,4},{8,9},{9,10},{10,1... | collective-permute-start | bytes 589832 | tf_op jit(solution)/shard_map/ppermute | solution.py:270
  160.1 35.3 %all-to-all-start.3 = ((bf16[64,8,1024]{2,1,0:T(8,128)(2,1)}), bf16[64,8,1024]{2,1,0:T(8,128)(2,1)S(1)}, u32[]{:S(2)}, u32[]{:S(2)}) async-start(bf16[64,8,1024]{2,1,0:T(8,128)(2,1)} %bitcast.28), calls=%async_computation.3 | async-start | bytes 2097152 | tf_op jit(solution)/shard_map/all_to_all | solution.py:501
